TPU v7x, 128 devices: a whole 4x4x4 slice. The times are simulated.
128 devices in a mesh: segment: 4 (over x), col: 32 (over z, y, core).
Axes of the slice: x: 4, y: 4, z: 4, core: 2. Of those that a mesh axis runs over, the one named last changes fastest.
Arguments:
- left_env: bfloat16 [384, 8192], P(None, 'col'), may hold values from -6 to 6
- bit_strings: int32 [384, 4], P(None, 'segment'), may hold values from 0 to 1
- site_tensors: bfloat16 [4, 2, 8192, 8192], P('segment', None, None, 'col'), may hold values from -0.0625 to 0.0625
Outputs:
- section_env: bfloat16 [4, 384, 8192], P('segment', None, 'col')
- section_log: float32 [4, 384], P('segment')
All inputs are finite; a program needn't handle non-finite values. Where the computation divides by a largest or mean magnitude, that divisor is 1e-20 or more.
Results may differ from a plain program's by a relative error of at most 0.0065.
Values may be sent and summed in bfloat16 or wider, within the bound.
No kernel may reach another device: no remote copies, remote signals or barrier semaphores. Data moves between devices by JAX's collectives and lax.ppermute only.
A program may use at most 128 MiB of HBM per device.

v0:
```python
import jax
import jax.numpy as jnp
from jax import lax
from jax.sharding import PartitionSpec as P

MICRO = 2


epsilon = 1e-06


def sent_to_all(value, axis):
    length = lax.axis_size(axis)
    return lax.all_to_all(
        jnp.broadcast_to(value[None], (length, *value.shape)), axis, 0, 0, tiled=True
    )


def taken_together(value, axis):
    everything = sent_to_all(value, axis)
    return jnp.max(everything, axis=0)


def passed_along(value, axis, by):
    length = lax.axis_size(axis)
    pairs = [(i, i + by) for i in range(length) if 0 <= i + by < length]
    return lax.ppermute(value, axis, pairs)


def advance(vector, bit_column, tensor):
    batch_rows = vector.shape[0]
    col_width = tensor.shape[2]
    block = min(128, batch_rows)
    buffer_rows = (batch_rows + block - 1 + block - 1) // block * block
    block_count = buffer_rows // block
    ones_before = jnp.cumsum(bit_column) - bit_column
    index_rows = jnp.arange(batch_rows, dtype=jnp.int32)
    zeros_before = index_rows - ones_before
    zero_count = batch_rows - jnp.sum(bit_column)
    start_one = (zero_count + block - 1) // block * block
    slot = jnp.where(bit_column == 1, start_one + ones_before, zeros_before)
    source = jnp.zeros((buffer_rows,), jnp.int32).at[slot].set(index_rows)
    filled = jnp.zeros((buffer_rows,), jnp.bool_).at[slot].set(True)
    block_bit = (jnp.arange(block_count, dtype=jnp.int32) * block >= start_one).astype(jnp.int32)
    arranged_in = jnp.where(
        filled[:, None], jnp.take(vector, source, axis=0), jnp.zeros((), vector.dtype)
    )
    gathered_piece = lax.all_gather(arranged_in, "col", axis=1, tiled=True)
    width = gathered_piece.shape[1]
    pieces = gathered_piece.reshape(block_count, block, width)

    def one_block(inputs):
        rows_block, bit_value = inputs
        weight_block = lax.dynamic_slice(
            tensor, (bit_value, 0, jnp.int32(0)), (1, width, col_width)
        )[0]
        return jnp.dot(rows_block, weight_block, preferred_element_type=jnp.float32)

    result = lax.map(one_block, (pieces, block_bit))
    arranged_out = result.reshape(buffer_rows, col_width)
    chosen = jnp.take(arranged_out, slot, axis=0)
    maximum = taken_together(jnp.max(jnp.abs(chosen), axis=1), "col") + epsilon
    return ((chosen / maximum[:, None]).astype(jnp.bfloat16), jnp.log(maximum))


def local(left_env, bit_strings, site_tensors):
    segment_count = lax.axis_size("segment")
    segment_index = lax.axis_index("segment")
    row_count = left_env.shape[0]
    col_width = left_env.shape[1]
    granules = MICRO
    batch_rows = row_count // granules
    env_out = jnp.zeros((row_count, col_width), jnp.bfloat16)
    log_out = jnp.zeros((row_count,), jnp.float32)
    incoming = jnp.zeros((batch_rows, col_width), jnp.bfloat16)
    tick_total = granules + segment_count - 1
    for tick_step in range(tick_total):
        position = tick_step - segment_index
        active = (position >= 0) & (position < granules)
        offset_rows = jnp.clip(position, 0, granules - 1) * batch_rows
        from_input = lax.dynamic_slice_in_dim(left_env, offset_rows, batch_rows, 0)
        current = jnp.where(segment_index == 0, from_input, incoming)
        bit_block = lax.dynamic_slice_in_dim(bit_strings, offset_rows, batch_rows, 0)
        current, logs_site = advance(current, bit_block[:, 0], site_tensors[0])
        old_env = lax.dynamic_slice_in_dim(env_out, offset_rows, batch_rows, 0)
        old_log = lax.dynamic_slice_in_dim(log_out, offset_rows, batch_rows, 0)
        env_out = lax.dynamic_update_slice_in_dim(
            env_out, jnp.where(active, current, old_env), offset_rows, 0
        )
        log_out = lax.dynamic_update_slice_in_dim(
            log_out, jnp.where(active, logs_site, old_log), offset_rows, 0
        )
        if tick_step + 1 < tick_total:
            incoming = passed_along(current, "segment", 1)
    return (env_out[None], log_out[None])


def solution(mesh):
    placed = (P(None, "col"), P(None, "segment"), P("segment", None, None, "col"))
    return jax.shard_map(
        local,
        mesh=mesh,
        in_specs=placed,
        out_specs=(P("segment", None, "col"), P("segment", None)),
        check_vma=False,
    )
```

profile of v0, /device:TPU:1, one launch (start us, length us, event | category | flops | bytes accessed | tf_op | source)
XLA Modules:
  0.0 496.4 jit_solution(4290405413867485066)
XLA Ops:
  7.2 1.7 fusion.101
  12.4 2.1 gather_fusion
  20.4 54.5 %all-gather.6.cloned.1.call-done = bf16[384,8192]{1,0:T(8,128)(2,1)} async-done(((bf16[384,256]{1,0:T(8,128)(2,1)}), bf16[384,8192]{1,0:T(8,128)(2,1)}) %all-gather.6.cloned.1.call-update) | async-done | bytes 6291472 | tf_op jit(solution)/shard_map/all_gather | solution.py:48
  75.0 18.3 %while.50 = (s32[]{:T(128)}, f32[3,128,256]{2,1,0:T(8,128)S(1)}, bf16[3,128,8192]{2,1,0:T(8,128)(2,1)}, s32[3]{0:T(128)S(1)}, bf16[2,8192,256]{2,1,0:T(8,128)(2,1)}, /*index=5*/s32[]{:T(128)}, s32[]{:T(128)}, s32[]{:T(128)}) while((s32[]{:T(128)}, f32[3,128,256]{2,1,0:T(8,128)S(1)}, bf16[3,128,8192]{2,1,0:T(8,128)(2,1)}, s32[3]{0:T(128)S(1)}, ...), condition=%wide.region_6.8_spmd, body=%wide.region_5.7_spmd.sunk | while | flops 536870912 | bytes 6423687 | solution.py:59
  77.5 3.5 fusion.123
  83.6 3.5 fusion.123
  89.7 3.5 fusion.123
  95.0 5.5 %all-to-all-start = ((f32[32,1,192]{2,1,0:T(1,128)}), f32[32,1,192]{2,1,0:T(1,128)S(1)}, u32[]{:S(2)}, u32[]{:S(2)}) async-start(f32[32,1,192]{2,1,0:T(1,128)} %broadcast_in_dim.147), calls=%async_computation | async-start | bytes 65536 | tf_op jit(solution)/shard_map/all_to_all | solution.py:14
  101.8 5.9 %all-to-all-done = f32[32,1,192]{2,1,0:T(1,128)S(1)} async-done(((f32[32,1,192]{2,1,0:T(1,128)}), f32[32,1,192]{2,1,0:T(1,128)S(1)}, u32[]{:S(2)}, u32[]{:S(2)}) %all-to-all-start) | async-done | bytes 24608 | tf_op jit(solution)/shard_map/all_to_all | solution.py:14
  108.1 3.1 collective-permute-start
  111.2 1.6 collective-permute-done
  112.8 2.1 gather_fusion.2
  117.0 53.0 %all-gather.8.cloned.1.call-done = bf16[384,8192]{1,0:T(8,128)(2,1)} async-done(((bf16[384,256]{1,0:T(8,128)(2,1)}), bf16[384,8192]{1,0:T(8,128)(2,1)}) %all-gather.8.cloned.1.call-update) | async-done | bytes 6291472 | tf_op jit(solution)/shard_map/all_gather | solution.py:48
  170.1 18.3 %while.51 = (s32[]{:T(128)}, f32[3,128,256]{2,1,0:T(8,128)S(1)}, bf16[3,128,8192]{2,1,0:T(8,128)(2,1)}, s32[3]{0:T(128)S(1)}, bf16[2,8192,256]{2,1,0:T(8,128)(2,1)}, /*index=5*/s32[]{:T(128)}, s32[]{:T(128)}, s32[]{:T(128)}) while((s32[]{:T(128)}, f32[3,128,256]{2,1,0:T(8,128)S(1)}, bf16[3,128,8192]{2,1,0:T(8,128)(2,1)}, s32[3]{0:T(128)S(1)}, ...), condition=%wide.region_15.18_spmd, body=%wide.region_14.17_spmd.sunk | while | flops 536870912 | bytes 6423687 | solution.py:59
  172.6 3.5 fusion.126
  178.7 3.5 fusion.126
  184.8 3.5 fusion.126
  190.1 5.5 %all-to-all-start.1 = ((f32[32,1,192]{2,1,0:T(1,128)}), f32[32,1,192]{2,1,0:T(1,128)S(1)}, u32[]{:S(2)}, u32[]{:S(2)}) async-start(f32[32,1,192]{2,1,0:T(1,128)} %broadcast_in_dim.150), calls=%async_computation.1 | async-start | bytes 65536 | tf_op jit(solution)/shard_map/all_to_all | solution.py:14
  196.9 5.9 %all-to-all-done.1 = f32[32,1,192]{2,1,0:T(1,128)S(1)} async-done(((f32[32,1,192]{2,1,0:T(1,128)}), f32[32,1,192]{2,1,0:T(1,128)S(1)}, u32[]{:S(2)}, u32[]{:S(2)}) %all-to-all-start.1) | async-done | bytes 24608 | tf_op jit(solution)/shard_map/all_to_all | solution.py:14
  203.2 3.3 collective-permute-start.1
  208.0 2.1 gather_fusion.4
  214.7 50.5 %all-gather.10.cloned.1.call-done = bf16[384,8192]{1,0:T(8,128)(2,1)} async-done(((bf16[384,256]{1,0:T(8,128)(2,1)}), bf16[384,8192]{1,0:T(8,128)(2,1)}) %all-gather.10.cloned.1.call-update) | async-done | bytes 6291472 | tf_op jit(solution)/shard_map/all_gather | solution.py:48
  265.2 18.3 %while.52 = (s32[]{:T(128)}, f32[3,128,256]{2,1,0:T(8,128)S(1)}, bf16[3,128,8192]{2,1,0:T(8,128)(2,1)}, s32[3]{0:T(128)S(1)}, bf16[2,8192,256]{2,1,0:T(8,128)(2,1)}, /*index=5*/s32[]{:T(128)}, s32[]{:T(128)}, s32[]{:T(128)}) while((s32[]{:T(128)}, f32[3,128,256]{2,1,0:T(8,128)S(1)}, bf16[3,128,8192]{2,1,0:T(8,128)(2,1)}, s32[3]{0:T(128)S(1)}, ...), condition=%wide.region_24.27_spmd, body=%wide.region_23.26_spmd.sunk | while | flops 536870912 | bytes 6423687 | solution.py:59
  267.8 3.5 fusion.129
  273.9 3.5 fusion.129
  280.0 3.5 fusion.129
  285.2 5.5 %all-to-all-start.2 = ((f32[32,1,192]{2,1,0:T(1,128)}), f32[32,1,192]{2,1,0:T(1,128)S(1)}, u32[]{:S(2)}, u32[]{:S(2)}) async-start(f32[32,1,192]{2,1,0:T(1,128)} %broadcast_in_dim.153), calls=%async_computation.2 | async-start | bytes 65536 | tf_op jit(solution)/shard_map/all_to_all | solution.py:14
  292.1 5.9 %all-to-all-done.2 = f32[32,1,192]{2,1,0:T(1,128)S(1)} async-done(((f32[32,1,192]{2,1,0:T(1,128)}), f32[32,1,192]{2,1,0:T(1,128)S(1)}, u32[]{:S(2)}, u32[]{:S(2)}) %all-to-all-start.2) | async-done | bytes 24608 | tf_op jit(solution)/shard_map/all_to_all | solution.py:14
  298.4 3.1 collective-permute-start.2
  301.5 1.6 collective-permute-done.2
  303.1 2.1 gather_fusion.6
  307.3 53.0 %all-gather.12.cloned.1.call-done = bf16[384,8192]{1,0:T(8,128)(2,1)} async-done(((bf16[384,256]{1,0:T(8,128)(2,1)}), bf16[384,8192]{1,0:T(8,128)(2,1)}) %all-gather.12.cloned.1.call-update) | async-done | bytes 6291472 | tf_op jit(solution)/shard_map/all_gather | solution.py:48
  360.4 18.3 %while.53 = (s32[]{:T(128)}, f32[3,128,256]{2,1,0:T(8,128)S(1)}, bf16[3,128,8192]{2,1,0:T(8,128)(2,1)}, s32[3]{0:T(128)S(1)}, bf16[2,8192,256]{2,1,0:T(8,128)(2,1)}, /*index=5*/s32[]{:T(128)}, s32[]{:T(128)}, s32[]{:T(128)}) while((s32[]{:T(128)}, f32[3,128,256]{2,1,0:T(8,128)S(1)}, bf16[3,128,8192]{2,1,0:T(8,128)(2,1)}, s32[3]{0:T(128)S(1)}, ...), condition=%wide.region_33.36_spmd, body=%wide.region_32.35_spmd.sunk | while | flops 536870912 | bytes 6423687 | solution.py:59
  362.9 3.5 fusion.132
  369.0 3.5 fusion.132
  375.1 3.5 fusion.132
  380.4 5.5 %all-to-all-start.3 = ((f32[32,1,192]{2,1,0:T(1,128)}), f32[32,1,192]{2,1,0:T(1,128)S(1)}, u32[]{:S(2)}, u32[]{:S(2)}) async-start(f32[32,1,192]{2,1,0:T(1,128)} %broadcast_in_dim.156), calls=%async_computation.3 | async-start | bytes 65536 | tf_op jit(solution)/shard_map/all_to_all | solution.py:14
  387.2 5.9 %all-to-all-done.3 = f32[32,1,192]{2,1,0:T(1,128)S(1)} async-done(((f32[32,1,192]{2,1,0:T(1,128)}), f32[32,1,192]{2,1,0:T(1,128)S(1)}, u32[]{:S(2)}, u32[]{:S(2)}) %all-to-all-start.3) | async-done | bytes 24608 | tf_op jit(solution)/shard_map/all_to_all | solution.py:14
  393.5 3.1 collective-permute-start.3
  396.6 1.6 collective-permute-done.3
  398.3 2.1 gather_fusion.8
  401.2 54.3 %all-gather.14.cloned.1.call-done = bf16[384,8192]{1,0:T(8,128)(2,1)} async-done(((bf16[384,256]{1,0:T(8,128)(2,1)}), bf16[384,8192]{1,0:T(8,128)(2,1)}) %all-gather.14.cloned.1.call-update) | async-done | bytes 6291472 | tf_op jit(solution)/shard_map/all_gather | solution.py:48
  455.5 18.3 %while.54 = (s32[]{:T(128)}, f32[3,128,256]{2,1,0:T(8,128)S(1)}, bf16[3,128,8192]{2,1,0:T(8,128)(2,1)}, s32[3]{0:T(128)S(1)}, bf16[2,8192,256]{2,1,0:T(8,128)(2,1)}, /*index=5*/s32[]{:T(128)}, s32[]{:T(128)}, s32[]{:T(128)}) while((s32[]{:T(128)}, f32[3,128,256]{2,1,0:T(8,128)S(1)}, bf16[3,128,8192]{2,1,0:T(8,128)(2,1)}, s32[3]{0:T(128)S(1)}, ...), condition=%wide.region_42.45_spmd, body=%wide.region_41.44_spmd.sunk | while | flops 536870912 | bytes 6423687 | solution.py:59
  458.1 3.5 fusion.135
  464.2 3.5 fusion.135
  470.3 3.5 fusion.135
  475.5 5.5 %all-to-all-start.4 = ((f32[32,1,192]{2,1,0:T(1,128)}), f32[32,1,192]{2,1,0:T(1,128)S(1)}, u32[]{:S(2)}, u32[]{:S(2)}) async-start(f32[32,1,192]{2,1,0:T(1,128)} %broadcast_in_dim.160), calls=%async_computation.4 | async-start | bytes 65536 | tf_op jit(solution)/shard_map/all_to_all | solution.py:14
  481.1 7.2 %all-to-all-done.4 = f32[32,1,192]{2,1,0:T(1,128)S(1)} async-done(((f32[32,1,192]{2,1,0:T(1,128)}), f32[32,1,192]{2,1,0:T(1,128)S(1)}, u32[]{:S(2)}, u32[]{:S(2)}) %all-to-all-start.4) | async-done | bytes 24608 | tf_op jit(solution)/shard_map/all_to_all | solution.py:14
  (156 shorter events, 42.9 us)
Async XLA Ops:
  7.2 67.8 %all-gather.6.cloned.1.call-start = ((), (), s32[]{:S(2)}) async-start(), calls=%async_computation.5 | async-start | bytes 6488064 | tf_op jit(solution)/shard_map/all_gather | solution.py:48
  75.0 37.8 %copy-start = (bf16[384,256]{1,0:T(8,128)(2,1)S(1)}, bf16[384,256]{1,0:T(8,128)(2,1)}, u32[]{:S(2)}) copy-start(bf16[384,256]{1,0:T(8,128)(2,1)} %param.17) | copy-start | bytes 589828
  95.0 12.8 %all-to-all-start = ((f32[32,1,192]{2,1,0:T(1,128)}), f32[32,1,192]{2,1,0:T(1,128)S(1)}, u32[]{:S(2)}, u32[]{:S(2)}) async-start(f32[32,1,192]{2,1,0:T(1,128)} %broadcast_in_dim.147), calls=%async_computation | async-start | bytes 65536 | tf_op jit(solution)/shard_map/all_to_all | solution.py:14
  100.5 69.6 %all-gather.8.cloned.1.call-start = ((), (), s32[]{:S(2)}) async-start(), calls=%async_computation.6 | async-start | bytes 6488064 | tf_op jit(solution)/shard_map/all_gather | solution.py:48
  108.1 4.7 collective-permute-start
  190.1 12.8 %all-to-all-start.1 = ((f32[32,1,192]{2,1,0:T(1,128)}), f32[32,1,192]{2,1,0:T(1,128)S(1)}, u32[]{:S(2)}, u32[]{:S(2)}) async-start(f32[32,1,192]{2,1,0:T(1,128)} %broadcast_in_dim.150), calls=%async_computation.1 | async-start | bytes 65536 | tf_op jit(solution)/shard_map/all_to_all | solution.py:14
  195.6 69.6 %all-gather.10.cloned.1.call-start = ((), (), s32[]{:S(2)}) async-start(), calls=%async_computation.7 | async-start | bytes 6488064 | tf_op jit(solution)/shard_map/all_gather | solution.py:48
  203.2 4.7 collective-permute-start.1
  285.2 12.8 %all-to-all-start.2 = ((f32[32,1,192]{2,1,0:T(1,128)}), f32[32,1,192]{2,1,0:T(1,128)S(1)}, u32[]{:S(2)}, u32[]{:S(2)}) async-start(f32[32,1,192]{2,1,0:T(1,128)} %broadcast_in_dim.153), calls=%async_computation.2 | async-start | bytes 65536 | tf_op jit(solution)/shard_map/all_to_all | solution.py:14
  290.8 69.6 %all-gather.12.cloned.1.call-start = ((), (), s32[]{:S(2)}) async-start(), calls=%async_computation.8 | async-start | bytes 6488064 | tf_op jit(solution)/shard_map/all_gather | solution.py:48
  298.4 4.7 collective-permute-start.2
  380.4 12.8 %all-to-all-start.3 = ((f32[32,1,192]{2,1,0:T(1,128)}), f32[32,1,192]{2,1,0:T(1,128)S(1)}, u32[]{:S(2)}, u32[]{:S(2)}) async-start(f32[32,1,192]{2,1,0:T(1,128)} %broadcast_in_dim.156), calls=%async_computation.3 | async-start | bytes 65536 | tf_op jit(solution)/shard_map/all_to_all | solution.py:14
  385.9 69.6 %all-gather.14.cloned.1.call-start = ((), (), s32[]{:S(2)}) async-start(), calls=%async_computation.9 | async-start | bytes 6488064 | tf_op jit(solution)/shard_map/all_gather | solution.py:48
  393.5 4.7 collective-permute-start.3
  475.5 12.8 %all-to-all-start.4 = ((f32[32,1,192]{2,1,0:T(1,128)}), f32[32,1,192]{2,1,0:T(1,128)S(1)}, u32[]{:S(2)}, u32[]{:S(2)}) async-start(f32[32,1,192]{2,1,0:T(1,128)} %broadcast_in_dim.160), calls=%async_computation.4 | async-start | bytes 65536 | tf_op jit(solution)/shard_map/all_to_all | solution.py:14
  488.6 0.6 copy-start.2
  489.2 0.7 copy-start.1
Sparse Core Ops, SparseCore 0:
  16.7 58.1 all-gather.5
  115.9 54.1 all-gather.7
  211.0 54.1 all-gather.9
  306.2 54.1 all-gather.11
  401.3 54.1 all-gather.13
where the time goes:
time: 497 us; the launch traced here: 496 us
  waiting for transfers between devices  303 us (61%)
  matrix products  53.1 us (11%)
  local copies, waits for them, and re-layouts  41.3 us (8%)
  starting transfers between devices  40.3 us (8%)
  loops' own time  29.5 us (6%)
  between operations  17.7 us (4%)
  other arithmetic  11.8 us (2%)
    all_gather x5, waiting for transfers between devices, advance(): gathered_piece = lax.all_gather(arranged_in, 'col', axis=1, tiled=True)  265 us
    dot_general x15, matrix products, one_block(): return jnp.dot(rows_block, weight_block, preferred_element_type=jnp.float32)  53.1 us
    all_to_all x5, waiting for transfers between devices, sent_to_all(): lax.all_to_all(jnp.broadcast_to(value[None], (length, *value.shape)), axi...  30.9 us
    another operation x5, loops' own time, advance(): result = lax.map(one_block, (pieces, block_bit))  29.5 us
    all_to_all x5, starting transfers between devices, sent_to_all(): lax.all_to_all(jnp.broadcast_to(value[None], (length, *value.shape)), axi...  27.5 us
    ppermute x4, starting transfers between devices, passed_along(): return lax.ppermute(value, axis, pairs)  12.6 us
    gather x5, local copies, waits for them, and re-layouts, advance(): jnp.take(vector, source, axis=0)  10.3 us
  transfers between devices with their start and end apart: 14, of which 14 were waited for; matrix products, arithmetic and copies ran while one was open for 3% of the time, Pallas kernels for 0%

commit v1 on v0

v1 whole, which is shorter than its diff:
```python
import functools

import jax
import jax.numpy as jnp
from jax import lax
from jax.experimental import pallas as pl
from jax.experimental.pallas import tpu as pltpu
from jax.sharding import PartitionSpec as P

MICRO = 4
EXTRA = 16

epsilon = 1e-06


def kernel(blocks, core_ref, own_ref, other_ref, bit_ref, tensor_ref, block_ref, product_ref, largest_ref):
    rows = product_ref.shape[0]
    width = product_ref.shape[1]
    core = core_ref[0]

    def add_on(i, carry):
        total_zero, total_one, largest = carry
        for ref, side in ((own_ref, core), (other_ref, 1 - core)):
            start = pl.multiple_of((2 * i + side) * width, width)
            piece = ref[i, :rows, :]
            total_zero += jnp.dot(
                piece, tensor_ref[0, pl.ds(start, width), :], preferred_element_type=jnp.float32
            )
            total_one += jnp.dot(
                piece, tensor_ref[1, pl.ds(start, width), :], preferred_element_type=jnp.float32
            )
            parts = ref[i, rows:, :].astype(jnp.float32)
            largest = jnp.maximum(largest, (parts[0:1] + parts[1:2]) + parts[2:3])
        return total_zero, total_one, largest

    zeros = jnp.zeros((rows, width), jnp.float32)
    carry = (zeros, zeros, jnp.zeros((1, width), jnp.float32))
    for i in range(blocks):
        carry = add_on(i, carry)
    total_zero, total_one, largest = carry
    divisor = jnp.broadcast_to(largest, (8, width)).T[:rows, 0:1]
    product = jnp.where(bit_ref[...] == 1, total_one, total_zero) / divisor
    product_ref[...] = product
    block_ref[:rows, :] = product.astype(jnp.bfloat16)
    local = jnp.max(jnp.abs(product), axis=1, keepdims=True) + epsilon
    local = jnp.concatenate([local, jnp.zeros((width - rows, 1), jnp.float32)], axis=0)
    local = jnp.broadcast_to(local, (width, 128)).T[0:8]
    largest_ref[...] = local
    high = local.astype(jnp.bfloat16).astype(jnp.float32)
    rest = local - high
    middle = rest.astype(jnp.bfloat16).astype(jnp.float32)
    low = rest - middle
    row = lax.broadcasted_iota(jnp.int32, (EXTRA, width), 0)
    extra = jnp.where(
        row == 0, high[0:1], jnp.where(row == 1, middle[0:1], jnp.where(row == 2, low[0:1], 0.0))
    )
    block_ref[rows:, :] = extra.astype(jnp.bfloat16)


def site(core, own, other, bits, tensor):
    blocks, height, width = own.shape
    rows = height - EXTRA
    vmem = pl.BlockSpec(memory_space=pltpu.VMEM)
    return pl.pallas_call(
        functools.partial(kernel, blocks),
        out_shape=(
            jax.ShapeDtypeStruct((height, width), jnp.bfloat16),
            jax.ShapeDtypeStruct((rows, width), jnp.float32),
            jax.ShapeDtypeStruct((8, width), jnp.float32),
        ),
        in_specs=[pl.BlockSpec(memory_space=pltpu.SMEM), vmem, vmem, vmem, vmem],
        out_specs=(vmem, vmem, vmem),
        compiler_params=pltpu.CompilerParams(vmem_limit_bytes=40 * 1024 * 1024),
        name="site",
    )(core, own, other, bits, tensor)


def local(left_env, bit_strings, site_tensors):
    segments = lax.axis_size("segment")
    segment = lax.axis_index("segment")
    cols = lax.axis_size("col")
    chips = cols // 2
    core = (lax.axis_index("col") % 2).reshape(1)
    row_count, width = left_env.shape
    rows = row_count // MICRO
    tensor = site_tensors[0]
    same_core = [[2 * i + c for i in range(chips)] for c in range(2)]
    swap = [(i, i ^ 1) for i in range(cols)]
    forward = [(i, i + 1) for i in range(segments - 1)]
    ones = jnp.where(
        lax.broadcasted_iota(jnp.int32, (EXTRA, width), 0) == 0, 1.0, 0.0
    ).astype(jnp.bfloat16)

    ticks = MICRO + segments - 1
    incoming = None
    products, maxima = [], []
    for tick in range(ticks):
        batch = min(tick, MICRO - 1)
        first = jnp.concatenate([left_env[batch * rows:(batch + 1) * rows], ones], axis=0)
        current = first if incoming is None else jnp.where(segment == 0, first, incoming)
        own = lax.all_to_all(
            jnp.broadcast_to(current[None], (chips, *current.shape)),
            "col", 0, 0, axis_index_groups=same_core, tiled=True,
        )
        other = lax.ppermute(own, "col", swap)
        position = jnp.clip(tick - segment, 0, MICRO - 1)
        bits = lax.dynamic_slice_in_dim(bit_strings, position * rows, rows, 0)
        block, product, largest = site(core, own, other, bits, tensor)
        products.append(product)
        maxima.append(largest[0, :rows])
        if tick + 1 < ticks:
            incoming = lax.ppermute(block, "segment", forward)

    largest = lax.dynamic_slice_in_dim(jnp.stack(maxima), segment, MICRO, 0)
    everything = lax.all_to_all(
        jnp.broadcast_to(largest[None], (cols, *largest.shape)), "col", 0, 0, tiled=True
    )
    maximum = jnp.max(everything, axis=0)
    product = lax.dynamic_slice_in_dim(jnp.stack(products), segment, MICRO, 0)
    env = (product / maximum[:, :, None]).astype(jnp.bfloat16)
    return env.reshape(1, row_count, width), jnp.log(maximum).reshape(1, row_count)


def solution(mesh):
    placed = (P(None, "col"), P(None, "segment"), P("segment", None, None, "col"))
    return jax.shard_map(
        local,
        mesh=mesh,
        in_specs=placed,
        out_specs=(P("segment", None, "col"), P("segment", None)),
        check_vma=False,
    )
```

time: 497 us -> 237 us (0.48)
  waiting for transfers between devices: 303 us -> 20.4 us
  blocking collectives: 0 us -> 137 us
  matrix products: 53.1 us -> 0 us
  loops' own time: 29.5 us -> 0 us
  between operations: 17.7 us -> 0.89 us
  other arithmetic: 11.8 us -> 1.43 us
    all_gather x5 -> x0, waiting for transfers between devices: 265 us -> none  [advance(): gathered_piece = lax.all_gather(arranged_in, 'col', axis=1, tiled=True)]
    all_to_all x0 -> x8, blocking collectives: none -> 137 us  [the longest x7 126 us: local(): lax.all_to_all(jnp.broadcast_to(current[None], (chips, *current.shape)),...]
    dot_general x15 -> x0, matrix products: 53.1 us -> none  [one_block(): return jnp.dot(rows_block, weight_block, preferred_element_type=jnp.float32)]
    pallas_call x0 -> x6, local copies, waits for them, and re-layouts: none -> 30.9 us  [site(): pl.pallas_call(functools.partial(kernel, blocks), out_shape=(jax.ShapeDty...]
    all_to_all x5 -> x0, waiting for transfers between devices: 30.9 us -> none  [sent_to_all(): lax.all_to_all(jnp.broadcast_to(value[None], (length, *value.shape)), axi...]
    another operation x5 -> x0, loops' own time: 29.5 us -> none  [advance(): result = lax.map(one_block, (pieces, block_bit))]
    all_to_all x5 -> x0, starting transfers between devices: 27.5 us -> none  [sent_to_all(): lax.all_to_all(jnp.broadcast_to(value[None], (length, *value.shape)), axi...]
    ppermute x4 -> x13, starting transfers between devices: 12.6 us -> 37.2 us  [the longest x6 22.3 us: local(): incoming = lax.ppermute(block, 'segment', forward)]
  transfers between devices with their start and end apart: 14 -> 13, of which waited for: 14 -> 13; matrix products, arithmetic and copies ran while one was open for 3% -> 1% of each run, Pallas kernels for 0% -> 0%
where the time goes in v1:
time: 237 us; the launch traced here: 236 us
  blocking collectives  137 us (58%)
  local copies, waits for them, and re-layouts  38.1 us (16%)
  starting transfers between devices  37.2 us (16%)
  waiting for transfers between devices  20.4 us (9%)
    all_to_all x7, blocking collectives, local(): lax.all_to_all(jnp.broadcast_to(current[None], (chips, *current.shape)),...  126 us
    pallas_call x6, local copies, waits for them, and re-layouts, site(): pl.pallas_call(functools.partial(kernel, blocks), out_shape=(jax.ShapeDty...  30.9 us
    ppermute x6, starting transfers between devices, local(): incoming = lax.ppermute(block, 'segment', forward)  22.3 us
    ppermute x7, starting transfers between devices, local(): other = lax.ppermute(own, 'col', swap)  14.9 us
    ppermute x7, waiting for transfers between devices, local(): other = lax.ppermute(own, 'col', swap)  13 us
    all_to_all x1, blocking collectives, local(): lax.all_to_all(jnp.broadcast_to(largest[None], (cols, *largest.shape)), '...  10.6 us
    ppermute x6, waiting for transfers between devices, local(): incoming = lax.ppermute(block, 'segment', forward)  7.4 us
  transfers between devices with their start and end apart: 13, of which 13 were waited for; matrix products, arithmetic and copies ran while one was open for 1% of the time, Pallas kernels for 0%

profile of v1, /device:TPU:1, one launch (start us, length us, event | category | flops | bytes accessed | tf_op | source)
XLA Modules:
  0.0 236.5 jit_solution(8498986162032584205)
XLA Ops:
  0.6 0.9 fusion.25
  1.8 23.3 %all_to_all.40.own_ref = bf16[16,112,256]{2,1,0:T(8,128)(2,1)S(1)} all-to-all(bf16[16,112,256]{2,1,0:T(8,128)(2,1)S(1)} %broadcast_in_dim.26), channel_id=1, replica_groups={{0,2,4,6,8,10,12,14,16,18,20,22,24,26,28,30},{1,3,5,7,9,11,13,15,17,19,..., dimensions={0} | all-to-all | bytes 1835008 | tf_op jit(solution)/shard_map/all_to_all | solution.py:101
  25.0 1.8 collective-permute-start
  26.9 0.9 constant_dynamic-slice_fusion.1
  27.8 0.1 copy.28.bit_ref
  27.9 1.1 collective-permute-done.other_ref
  29.0 3.4 %copy-done = bf16[1,2,8192,256]{3,2,1,0:T(8,128)(2,1)S(1)} copy-done((bf16[1,2,8192,256]{3,2,1,0:T(8,128)(2,1)S(1)}, bf16[1,2,8192,256]{3,2,1,0:T(8,128)(2,1)}, u32[]{:S(2)}) %copy-start) | copy-done | bytes 8388632
  32.4 1.7 site.7
  34.0 3.1 %collective-permute-start.1 = (bf16[112,256]{1,0:T(8,128)(2,1)S(1)}, bf16[112,256]{1,0:T(8,128)(2,1)S(1)}, u32[]{:S(2)}, u32[]{:S(2)}) collective-permute-start(bf16[112,256]{1,0:T(8,128)(2,1)S(1)} %get-tuple-element.23), channel_id=1, source_target_pairs={{0,32},{32,64},{64,96},{1,33},{33,65},{65,97},{2,34},{34,66},{66,9... | collective-permute-start | bytes 172040 | tf_op jit(solution)/shard_map/ppermute | solution.py:112
  37.1 1.2 collective-permute-done.1
  38.5 17.0 %all_to_all.41 = bf16[16,112,256]{2,1,0:T(8,128)(2,1)S(1)} all-to-all(bf16[16,112,256]{2,1,0:T(8,128)(2,1)S(1)} %broadcast_in_dim.27), channel_id=1, replica_groups={{0,2,4,6,8,10,12,14,16,18,20,22,24,26,28,30},{1,3,5,7,9,11,13,15,17,19,..., dimensions={0} | all-to-all | bytes 1835008 | tf_op jit(solution)/shard_map/all_to_all | solution.py:101
  55.5 2.4 collective-permute-start.2
  58.0 2.0 collective-permute-done.2
  60.0 5.0 %site.13 = (f32[7,96,256]{2,1,0:T(8,128)S(1)}, bf16[112,256]{1,0:T(8,128)(2,1)S(1)}, f32[8,256]{1,0:T(8,128)S(1)}) fusion(f32[7,96,256]{2,1,0:T(8,128)S(1)} %bitcast_dynamic-update-slice_fusion.6, s32[1]{0:T(128)} %bitcast.core_ref, bf16[16,112,256]{2,1,0:T(8,128)(2,1)S(1)} %all_to_all.41, bf16[16,112,256]{2,1,0:T(8,128)(2,1)S(1)} %collective-permute-done.2, ...), kind=kCustom, calls=%fused_computation.6 | custom fusion | bytes 10436612 | tf_op jit(solution)/shard_map/site/pallas_call | solution.py:64
  65.0 3.9 %collective-permute-start.3 = (bf16[112,256]{1,0:T(8,128)(2,1)S(1)}, bf16[112,256]{1,0:T(8,128)(2,1)S(1)}, u32[]{:S(2)}, u32[]{:S(2)}) collective-permute-start(bf16[112,256]{1,0:T(8,128)(2,1)S(1)} %get-tuple-element.51), channel_id=1, source_target_pairs={{0,32},{32,64},{64,96},{1,33},{33,65},{65,97},{2,34},{34,66},{66,9... | collective-permute-start | bytes 172040 | tf_op jit(solution)/shard_map/ppermute | solution.py:112
  68.9 1.2 collective-permute-done.3
  70.3 17.3 %all_to_all.42 = bf16[16,112,256]{2,1,0:T(8,128)(2,1)S(1)} all-to-all(bf16[16,112,256]{2,1,0:T(8,128)(2,1)S(1)} %broadcast_in_dim.28), channel_id=1, replica_groups={{0,2,4,6,8,10,12,14,16,18,20,22,24,26,28,30},{1,3,5,7,9,11,13,15,17,19,..., dimensions={0} | all-to-all | bytes 1835008 | tf_op jit(solution)/shard_map/all_to_all | solution.py:101
  87.6 2.1 collective-permute-start.4
  89.8 2.0 collective-permute-done.4
  91.8 5.0 %site.12 = (f32[7,96,256]{2,1,0:T(8,128)S(1)}, bf16[112,256]{1,0:T(8,128)(2,1)S(1)}, f32[8,256]{1,0:T(8,128)S(1)}) fusion(f32[7,96,256]{2,1,0:T(8,128)S(1)} %get-tuple-element.50, s32[1]{0:T(128)} %bitcast.core_ref, bf16[16,112,256]{2,1,0:T(8,128)(2,1)S(1)} %all_to_all.42, bf16[16,112,256]{2,1,0:T(8,128)(2,1)S(1)} %collective-permute-done.4, ...), kind=kCustom, calls=%fused_computation.5 | custom fusion | bytes 10436612 | tf_op jit(solution)/shard_map/site/pallas_call | solution.py:64
  96.8 3.7 %collective-permute-start.5 = (bf16[112,256]{1,0:T(8,128)(2,1)S(1)}, bf16[112,256]{1,0:T(8,128)(2,1)S(1)}, u32[]{:S(2)}, u32[]{:S(2)}) collective-permute-start(bf16[112,256]{1,0:T(8,128)(2,1)S(1)} %get-tuple-element.45), channel_id=1, source_target_pairs={{0,32},{32,64},{64,96},{1,33},{33,65},{65,97},{2,34},{34,66},{66,9... | collective-permute-start | bytes 172040 | tf_op jit(solution)/shard_map/ppermute | solution.py:112
  100.6 1.2 collective-permute-done.5
  102.0 17.0 %all_to_all.43 = bf16[16,112,256]{2,1,0:T(8,128)(2,1)S(1)} all-to-all(bf16[16,112,256]{2,1,0:T(8,128)(2,1)S(1)} %broadcast_in_dim.29), channel_id=1, replica_groups={{0,2,4,6,8,10,12,14,16,18,20,22,24,26,28,30},{1,3,5,7,9,11,13,15,17,19,..., dimensions={0} | all-to-all | bytes 1835008 | tf_op jit(solution)/shard_map/all_to_all | solution.py:101
  119.0 2.3 collective-permute-start.6
  121.3 0.1 copy.31
  121.4 2.0 collective-permute-done.6
  123.4 5.0 %site.11 = (f32[7,96,256]{2,1,0:T(8,128)S(1)}, bf16[112,256]{1,0:T(8,128)(2,1)S(1)}, f32[8,256]{1,0:T(8,128)S(1)}) fusion(f32[7,96,256]{2,1,0:T(8,128)S(1)} %get-tuple-element.44, s32[1]{0:T(128)} %bitcast.core_ref, bf16[16,112,256]{2,1,0:T(8,128)(2,1)S(1)} %all_to_all.43, bf16[16,112,256]{2,1,0:T(8,128)(2,1)S(1)} %collective-permute-done.6, ...), kind=kCustom, calls=%fused_computation.4 | custom fusion | bytes 10436612 | tf_op jit(solution)/shard_map/site/pallas_call | solution.py:64
  128.5 3.9 %collective-permute-start.7 = (bf16[112,256]{1,0:T(8,128)(2,1)S(1)}, bf16[112,256]{1,0:T(8,128)(2,1)S(1)}, u32[]{:S(2)}, u32[]{:S(2)}) collective-permute-start(bf16[112,256]{1,0:T(8,128)(2,1)S(1)} %get-tuple-element.57), channel_id=1, source_target_pairs={{0,32},{32,64},{64,96},{1,33},{33,65},{65,97},{2,34},{34,66},{66,9... | collective-permute-start | bytes 172040 | tf_op jit(solution)/shard_map/ppermute | solution.py:112
  132.4 1.2 collective-permute-done.7
  133.8 17.3 %all_to_all.44 = bf16[16,112,256]{2,1,0:T(8,128)(2,1)S(1)} all-to-all(bf16[16,112,256]{2,1,0:T(8,128)(2,1)S(1)} %broadcast_in_dim.30), channel_id=1, replica_groups={{0,2,4,6,8,10,12,14,16,18,20,22,24,26,28,30},{1,3,5,7,9,11,13,15,17,19,..., dimensions={0} | all-to-all | bytes 1835008 | tf_op jit(solution)/shard_map/all_to_all | solution.py:101
  151.1 2.0 collective-permute-start.8
  153.2 2.0 collective-permute-done.8
  155.2 5.0 %site.10 = (f32[7,96,256]{2,1,0:T(8,128)S(1)}, bf16[112,256]{1,0:T(8,128)(2,1)S(1)}, f32[8,256]{1,0:T(8,128)S(1)}) fusion(f32[7,96,256]{2,1,0:T(8,128)S(1)} %get-tuple-element.56, s32[1]{0:T(128)} %bitcast.core_ref, bf16[16,112,256]{2,1,0:T(8,128)(2,1)S(1)} %all_to_all.44, bf16[16,112,256]{2,1,0:T(8,128)(2,1)S(1)} %collective-permute-done.8, ...), kind=kCustom, calls=%fused_computation.3 | custom fusion | bytes 10436612 | tf_op jit(solution)/shard_map/site/pallas_call | solution.py:64
  160.3 3.7 %collective-permute-start.9 = (bf16[112,256]{1,0:T(8,128)(2,1)S(1)}, bf16[112,256]{1,0:T(8,128)(2,1)S(1)}, u32[]{:S(2)}, u32[]{:S(2)}) collective-permute-start(bf16[112,256]{1,0:T(8,128)(2,1)S(1)} %get-tuple-element.76), channel_id=1, source_target_pairs={{0,32},{32,64},{64,96},{1,33},{33,65},{65,97},{2,34},{34,66},{66,9... | collective-permute-start | bytes 172040 | tf_op jit(solution)/shard_map/ppermute | solution.py:112
  164.0 1.2 collective-permute-done.9
  165.4 17.0 %all_to_all.45 = bf16[16,112,256]{2,1,0:T(8,128)(2,1)S(1)} all-to-all(bf16[16,112,256]{2,1,0:T(8,128)(2,1)S(1)} %broadcast_in_dim.31), channel_id=1, replica_groups={{0,2,4,6,8,10,12,14,16,18,20,22,24,26,28,30},{1,3,5,7,9,11,13,15,17,19,..., dimensions={0} | all-to-all | bytes 1835008 | tf_op jit(solution)/shard_map/all_to_all | solution.py:101
  182.4 2.3 collective-permute-start.10
  184.9 2.0 collective-permute-done.10
  186.9 5.0 %site.9 = (f32[7,96,256]{2,1,0:T(8,128)S(1)}, bf16[112,256]{1,0:T(8,128)(2,1)S(1)}, f32[8,256]{1,0:T(8,128)S(1)}) fusion(f32[7,96,256]{2,1,0:T(8,128)S(1)} %get-tuple-element.75, s32[1]{0:T(128)} %bitcast.core_ref, bf16[16,112,256]{2,1,0:T(8,128)(2,1)S(1)} %all_to_all.45, bf16[16,112,256]{2,1,0:T(8,128)(2,1)S(1)} %collective-permute-done.10, ...), kind=kCustom, calls=%fused_computation.2 | custom fusion | bytes 10436612 | tf_op jit(solution)/shard_map/site/pallas_call | solution.py:64
  191.9 3.9 %collective-permute-start.11 = (bf16[112,256]{1,0:T(8,128)(2,1)S(1)}, bf16[112,256]{1,0:T(8,128)(2,1)S(1)}, u32[]{:S(2)}, u32[]{:S(2)}) collective-permute-start(bf16[112,256]{1,0:T(8,128)(2,1)S(1)} %get-tuple-element.63), channel_id=1, source_target_pairs={{0,32},{32,64},{64,96},{1,33},{33,65},{65,97},{2,34},{34,66},{66,9... | collective-permute-start | bytes 172040 | tf_op jit(solution)/shard_map/ppermute | solution.py:112
  195.8 1.2 collective-permute-done.11
  197.2 17.3 %all_to_all.46 = bf16[16,112,256]{2,1,0:T(8,128)(2,1)S(1)} all-to-all(bf16[16,112,256]{2,1,0:T(8,128)(2,1)S(1)} %broadcast_in_dim.32), channel_id=1, replica_groups={{0,2,4,6,8,10,12,14,16,18,20,22,24,26,28,30},{1,3,5,7,9,11,13,15,17,19,..., dimensions={0} | all-to-all | bytes 1835008 | tf_op jit(solution)/shard_map/all_to_all | solution.py:101
  214.6 2.0 collective-permute-start.12
  216.7 1.9 collective-permute-done.12
  218.7 5.7 %site.8 = (f32[7,96,256]{2,1,0:T(8,128)S(1)}, f32[8,256]{1,0:T(8,128)S(1)}, bf16[112,256]{1,0:T(8,128)(2,1)}) fusion(f32[7,96,256]{2,1,0:T(8,128)S(1)} %get-tuple-element.62, s32[1]{0:T(128)} %bitcast.core_ref, bf16[16,112,256]{2,1,0:T(8,128)(2,1)S(1)} %all_to_all.46, bf16[16,112,256]{2,1,0:T(8,128)(2,1)S(1)} %collective-permute-done.12, ...), kind=kCustom, calls=%fused_computation.1 | custom fusion | bytes 10436612 | tf_op jit(solution)/shard_map/site/pallas_call | solution.py:64
  224.4 10.6 %all_to_all.47 = f32[32,4,96]{2,1,0:T(4,128)S(1)} all-to-all(f32[32,4,96]{2,1,0:T(4,128)S(1)} %broadcast_in_dim.33), channel_id=1, replica_groups=mesh['segment'=4,'col'=32] {'col'}, dimensions={0} | all-to-all | bytes 98304 | tf_op jit(solution)/shard_map/all_to_all | solution.py:115
  235.0 0.8 divide_convert_fusion
  235.8 0.6 log.14
  (35 shorter events, 1.7 us)
Async XLA Ops:
  25.0 3.9 %collective-permute-start = (bf16[16,112,256]{2,1,0:T(8,128)(2,1)S(1)}, bf16[16,112,256]{2,1,0:T(8,128)(2,1)S(1)}, u32[]{:S(2)}, u32[]{:S(2)}) collective-permute-start(bf16[16,112,256]{2,1,0:T(8,128)(2,1)S(1)} %all_to_all.40.own_ref), channel_id=1, source_target_pairs={{0,1},{1,0},{2,3},{3,2},{4,5},{5,4},{6,7},{7,6},{8,9},{9,8},{10,11... | collective-permute-start | bytes 2752520 | tf_op jit(solution)/shard_map/ppermute | solution.py:105
  29.0 3.4 %copy-start = (bf16[1,2,8192,256]{3,2,1,0:T(8,128)(2,1)S(1)}, bf16[1,2,8192,256]{3,2,1,0:T(8,128)(2,1)}, u32[]{:S(2)}) copy-start(bf16[1,2,8192,256]{3,2,1,0:T(8,128)(2,1)} %param.5) | copy-start | bytes 25165828
  34.0 4.4 %collective-permute-start.1 = (bf16[112,256]{1,0:T(8,128)(2,1)S(1)}, bf16[112,256]{1,0:T(8,128)(2,1)S(1)}, u32[]{:S(2)}, u32[]{:S(2)}) collective-permute-start(bf16[112,256]{1,0:T(8,128)(2,1)S(1)} %get-tuple-element.23), channel_id=1, source_target_pairs={{0,32},{32,64},{64,96},{1,33},{33,65},{65,97},{2,34},{34,66},{66,9... | collective-permute-start | bytes 172040 | tf_op jit(solution)/shard_map/ppermute | solution.py:112
  55.5 4.5 %collective-permute-start.2 = (bf16[16,112,256]{2,1,0:T(8,128)(2,1)S(1)}, bf16[16,112,256]{2,1,0:T(8,128)(2,1)S(1)}, u32[]{:S(2)}, u32[]{:S(2)}) collective-permute-start(bf16[16,112,256]{2,1,0:T(8,128)(2,1)S(1)} %all_to_all.41), channel_id=1, source_target_pairs={{0,1},{1,0},{2,3},{3,2},{4,5},{5,4},{6,7},{7,6},{8,9},{9,8},{10,11... | collective-permute-start | bytes 2752520 | tf_op jit(solution)/shard_map/ppermute | solution.py:105
  65.0 5.1 %collective-permute-start.3 = (bf16[112,256]{1,0:T(8,128)(2,1)S(1)}, bf16[112,256]{1,0:T(8,128)(2,1)S(1)}, u32[]{:S(2)}, u32[]{:S(2)}) collective-permute-start(bf16[112,256]{1,0:T(8,128)(2,1)S(1)} %get-tuple-element.51), channel_id=1, source_target_pairs={{0,32},{32,64},{64,96},{1,33},{33,65},{65,97},{2,34},{34,66},{66,9... | collective-permute-start | bytes 172040 | tf_op jit(solution)/shard_map/ppermute | solution.py:112
  87.6 4.2 %collective-permute-start.4 = (bf16[16,112,256]{2,1,0:T(8,128)(2,1)S(1)}, bf16[16,112,256]{2,1,0:T(8,128)(2,1)S(1)}, u32[]{:S(2)}, u32[]{:S(2)}) collective-permute-start(bf16[16,112,256]{2,1,0:T(8,128)(2,1)S(1)} %all_to_all.42), channel_id=1, source_target_pairs={{0,1},{1,0},{2,3},{3,2},{4,5},{5,4},{6,7},{7,6},{8,9},{9,8},{10,11... | collective-permute-start | bytes 2752520 | tf_op jit(solution)/shard_map/ppermute | solution.py:105
  96.8 5.0 %collective-permute-start.5 = (bf16[112,256]{1,0:T(8,128)(2,1)S(1)}, bf16[112,256]{1,0:T(8,128)(2,1)S(1)}, u32[]{:S(2)}, u32[]{:S(2)}) collective-permute-start(bf16[112,256]{1,0:T(8,128)(2,1)S(1)} %get-tuple-element.45), channel_id=1, source_target_pairs={{0,32},{32,64},{64,96},{1,33},{33,65},{65,97},{2,34},{34,66},{66,9... | collective-permute-start | bytes 172040 | tf_op jit(solution)/shard_map/ppermute | solution.py:112
  119.0 4.4 %collective-permute-start.6 = (bf16[16,112,256]{2,1,0:T(8,128)(2,1)S(1)}, bf16[16,112,256]{2,1,0:T(8,128)(2,1)S(1)}, u32[]{:S(2)}, u32[]{:S(2)}) collective-permute-start(bf16[16,112,256]{2,1,0:T(8,128)(2,1)S(1)} %all_to_all.43), channel_id=1, source_target_pairs={{0,1},{1,0},{2,3},{3,2},{4,5},{5,4},{6,7},{7,6},{8,9},{9,8},{10,11... | collective-permute-start | bytes 2752520 | tf_op jit(solution)/shard_map/ppermute | solution.py:105
  128.5 5.2 %collective-permute-start.7 = (bf16[112,256]{1,0:T(8,128)(2,1)S(1)}, bf16[112,256]{1,0:T(8,128)(2,1)S(1)}, u32[]{:S(2)}, u32[]{:S(2)}) collective-permute-start(bf16[112,256]{1,0:T(8,128)(2,1)S(1)} %get-tuple-element.57), channel_id=1, source_target_pairs={{0,32},{32,64},{64,96},{1,33},{33,65},{65,97},{2,34},{34,66},{66,9... | collective-permute-start | bytes 172040 | tf_op jit(solution)/shard_map/ppermute | solution.py:112
  151.1 4.1 %collective-permute-start.8 = (bf16[16,112,256]{2,1,0:T(8,128)(2,1)S(1)}, bf16[16,112,256]{2,1,0:T(8,128)(2,1)S(1)}, u32[]{:S(2)}, u32[]{:S(2)}) collective-permute-start(bf16[16,112,256]{2,1,0:T(8,128)(2,1)S(1)} %all_to_all.44), channel_id=1, source_target_pairs={{0,1},{1,0},{2,3},{3,2},{4,5},{5,4},{6,7},{7,6},{8,9},{9,8},{10,11... | collective-permute-start | bytes 2752520 | tf_op jit(solution)/shard_map/ppermute | solution.py:105
  160.3 5.0 %collective-permute-start.9 = (bf16[112,256]{1,0:T(8,128)(2,1)S(1)}, bf16[112,256]{1,0:T(8,128)(2,1)S(1)}, u32[]{:S(2)}, u32[]{:S(2)}) collective-permute-start(bf16[112,256]{1,0:T(8,128)(2,1)S(1)} %get-tuple-element.76), channel_id=1, source_target_pairs={{0,32},{32,64},{64,96},{1,33},{33,65},{65,97},{2,34},{34,66},{66,9... | collective-permute-start | bytes 172040 | tf_op jit(solution)/shard_map/ppermute | solution.py:112
  182.4 4.4 %collective-permute-start.10 = (bf16[16,112,256]{2,1,0:T(8,128)(2,1)S(1)}, bf16[16,112,256]{2,1,0:T(8,128)(2,1)S(1)}, u32[]{:S(2)}, u32[]{:S(2)}) collective-permute-start(bf16[16,112,256]{2,1,0:T(8,128)(2,1)S(1)} %all_to_all.45), channel_id=1, source_target_pairs={{0,1},{1,0},{2,3},{3,2},{4,5},{5,4},{6,7},{7,6},{8,9},{9,8},{10,11... | collective-permute-start | bytes 2752520 | tf_op jit(solution)/shard_map/ppermute | solution.py:105
  191.9 5.2 %collective-permute-start.11 = (bf16[112,256]{1,0:T(8,128)(2,1)S(1)}, bf16[112,256]{1,0:T(8,128)(2,1)S(1)}, u32[]{:S(2)}, u32[]{:S(2)}) collective-permute-start(bf16[112,256]{1,0:T(8,128)(2,1)S(1)} %get-tuple-element.63), channel_id=1, source_target_pairs={{0,32},{32,64},{64,96},{1,33},{33,65},{65,97},{2,34},{34,66},{66,9... | collective-permute-start | bytes 172040 | tf_op jit(solution)/shard_map/ppermute | solution.py:112
  214.6 4.1 %collective-permute-start.12 = (bf16[16,112,256]{2,1,0:T(8,128)(2,1)S(1)}, bf16[16,112,256]{2,1,0:T(8,128)(2,1)S(1)}, u32[]{:S(2)}, u32[]{:S(2)}) collective-permute-start(bf16[16,112,256]{2,1,0:T(8,128)(2,1)S(1)} %all_to_all.46), channel_id=1, source_target_pairs={{0,1},{1,0},{2,3},{3,2},{4,5},{5,4},{6,7},{7,6},{8,9},{9,8},{10,11... | collective-permute-start | bytes 2752520 | tf_op jit(solution)/shard_map/ppermute | solution.py:105

commit v2 on v1

v2 whole, which is shorter than its diff:
```python
import functools

import jax
import jax.numpy as jnp
from jax import lax
from jax.experimental import pallas as pl
from jax.experimental.pallas import tpu as pltpu
from jax.sharding import PartitionSpec as P

KINDS = "a"
BATCHES = 3
RING = 4
STEPS = (0, 1, 3, 2)

epsilon = 1e-06


def pieces_of(kind, z, y, core, refs):
    if kind == "a":
        own_ref, other_ref = refs
        for chip in range(RING * RING):
            yield chip, ((own_ref, chip, core), (other_ref, chip, 1 - core))
        return
    for index, ref in enumerate(refs):
        holder = core ^ (index // RING)
        from_z = (z - STEPS[index % RING]) & (RING - 1)
        for step in range(2):
            from_y = (y - 2 * holder - step) & (RING - 1)
            yield from_z * RING + from_y, tuple(
                (ref, 2 * step + side, holder ^ side) for side in range(2)
            )


def site_kernel(kind, slot, batches, tick, following, place_ref, *refs):
    count = 2 if kind == "a" else 2 * RING
    held_refs = refs[:count]
    bit_ref, left_ref, tensor_ref, block_ref, product_ref, largest_ref, *streaming = refs[count:]
    near_ref, arrived = streaming or (tensor_ref, None)
    rows, width = product_ref.shape
    segment, z, y, core = (place_ref[i] for i in range(4))
    work = []
    for k, (chip, pieces) in enumerate(pieces_of(kind, z, y, core, held_refs)):
        start = chip * 2 * width
        if not isinstance(start, int):
            start = pl.multiple_of(start, 2 * width)
        if not streaming:
            work.append((start, None, pieces))
            continue
        copy = pltpu.make_async_copy(
            tensor_ref.at[:, pl.ds(start, 2 * width), :],
            near_ref.at[:, k * 2 * width:(k + 1) * 2 * width, :],
            arrived.at[k],
        )
        copy.start()
        work.append((k * 2 * width, copy, pieces))
    zero = jnp.zeros((rows, width), jnp.float32)
    one = jnp.zeros((rows, width), jnp.float32)
    largest = jnp.zeros((rows, width), jnp.bfloat16)
    for base, copy, pieces in work:
        if copy is not None:
            copy.wait()
        for ref, index, side in pieces:
            start = pl.multiple_of(base + side * width, width)
            piece = ref[index]
            zero += jnp.dot(piece, near_ref[0, pl.ds(start, width), :], preferred_element_type=jnp.float32)
            one += jnp.dot(piece, near_ref[1, pl.ds(start, width), :], preferred_element_type=jnp.float32)
            largest = jnp.maximum(largest, jnp.abs(piece))
    divisor = jnp.max(largest.astype(jnp.float32), axis=1, keepdims=True) + epsilon
    divisor = jnp.where(segment == 0, 1.0, divisor)
    position = slot + jnp.clip(tick - segment, 0, batches - 1)
    bits = bit_ref[pl.ds(pl.multiple_of(position * rows, 8), rows), :]
    product = jnp.where(bits == 1, one, zero) / divisor
    product_ref[...] = product
    local = jnp.max(jnp.abs(product), axis=1, keepdims=True) + epsilon
    local = jnp.concatenate([local, jnp.zeros((width - rows, 1), jnp.float32)], axis=0)
    largest_ref[...] = jnp.broadcast_to(local, (width, 128)).T[0:8]
    following = left_ref[following * rows:(following + 1) * rows, :]
    block_ref[...] = jnp.where(segment == RING - 1, following, product.astype(jnp.bfloat16))


def site(kind, slot, batches, tick, following, place, held, bits, left, tensor):
    rows, width = held[0].shape[1:]
    vmem = pl.BlockSpec(memory_space=pltpu.VMEM)
    streaming = len(KINDS) > 1
    return pl.pallas_call(
        functools.partial(site_kernel, kind, slot, batches, tick, following),
        out_shape=(
            jax.ShapeDtypeStruct((rows, width), jnp.bfloat16),
            jax.ShapeDtypeStruct((rows, width), jnp.float32),
            jax.ShapeDtypeStruct((8, width), jnp.float32),
        ),
        in_specs=[pl.BlockSpec(memory_space=pltpu.SMEM)]
        + [vmem] * (len(held) + 2)
        + [pl.BlockSpec(memory_space=pltpu.HBM if streaming else pltpu.VMEM)],
        out_specs=(vmem, vmem, vmem),
        scratch_shapes=[
            pltpu.VMEM(tensor.shape, tensor.dtype),
            pltpu.SemaphoreType.DMA((RING * RING,)),
        ] if streaming else [],
        compiler_params=pltpu.CompilerParams(vmem_limit_bytes=24 * 1024 * 1024),
        name="site",
    )(place, *held, bits, left, tensor)


def collect_kernel(ticks, place_ref, *refs):
    largest_refs, maxima_ref = refs[:-1], refs[-1]
    batches = ticks - RING + 1
    lanes = maxima_ref.shape[2]
    for segment in range(RING):
        @pl.when(place_ref[0] == segment)
        def _():
            taken = [
                largest_refs[stream * ticks + batch + segment][0:1, :lanes]
                for stream in range(len(largest_refs) // ticks)
                for batch in range(batches)
            ]
            taken = jnp.concatenate(taken, axis=0)
            for i in range(maxima_ref.shape[0]):
                maxima_ref[i] = taken


def collect(cols, ticks, count, place, largest):
    vmem = pl.BlockSpec(memory_space=pltpu.VMEM)
    return pl.pallas_call(
        functools.partial(collect_kernel, ticks),
        out_shape=jax.ShapeDtypeStruct((cols, count, 128), jnp.float32),
        in_specs=[pl.BlockSpec(memory_space=pltpu.SMEM)] + [vmem] * len(largest),
        out_specs=vmem,
        name="collect",
    )(place, *largest)


def finish_kernel(ticks, place_ref, maxima_ref, *refs):
    product_refs, (env_ref, log_ref) = refs[:-2], refs[-2:]
    batches = ticks - RING + 1
    rows, width = product_refs[0].shape
    maximum = jnp.max(maxima_ref[...], axis=0)
    log_ref[...] = jnp.log(maximum)
    for slot in range(maximum.shape[0]):
        column = jnp.broadcast_to(maximum[slot:slot + 1], (8, maximum.shape[1])).T[:rows, 0:1]
        stream, batch = slot // batches, slot % batches
        for segment in range(RING):
            @pl.when(place_ref[0] == segment)
            def _():
                product = product_refs[stream * ticks + batch + segment][...]
                env_ref[slot * rows:(slot + 1) * rows, :] = (product / column).astype(jnp.bfloat16)


def finish(ticks, place, maxima, products):
    rows, width = products[0].shape
    count = maxima.shape[1]
    vmem = pl.BlockSpec(memory_space=pltpu.VMEM)
    return pl.pallas_call(
        functools.partial(finish_kernel, ticks),
        out_shape=(
            jax.ShapeDtypeStruct((count * rows, width), jnp.bfloat16),
            jax.ShapeDtypeStruct((count, maxima.shape[2]), jnp.float32),
        ),
        in_specs=[pl.BlockSpec(memory_space=pltpu.SMEM)] + [vmem] * (1 + len(products)),
        out_specs=(vmem, vmem),
        compiler_params=pltpu.CompilerParams(vmem_limit_bytes=16 * 1024 * 1024),
        name="finish",
    )(place, maxima, *products)


def moved(value, where):
    places = [
        (s, z, y, c)
        for s in range(RING) for z in range(RING) for y in range(RING) for c in range(2)
    ]
    number = {place: i for i, place in enumerate(places)}
    pairs = []
    for place in places:
        s, z, y, c = where(*place)
        pairs.append((number[place], number[(s % RING, z % RING, y % RING, c)]))
    return lax.ppermute(value, ("segment", "col"), pairs)


def swapped(value):
    return moved(value, lambda s, z, y, c: (s, z, y, 1 - c))


def after(values, *others):
    return lax.optimization_barrier((tuple(values), others))[0]


def local(left_env, bit_strings, site_tensors):
    cols = lax.axis_size("col")
    col = lax.axis_index("col")
    place = jnp.stack(
        [lax.axis_index("segment"), col // (2 * RING), (col // 2) % RING, col % 2]
    ).astype(jnp.int32)
    row_count, width = left_env.shape
    streams = len(KINDS)
    rows = row_count // (streams * BATCHES)
    ticks = BATCHES + RING - 1
    tensor = site_tensors[0]
    same_core = [[2 * i + c for i in range(cols // 2)] for c in range(2)]
    products = [[] for _ in range(streams)]
    largest = [[] for _ in range(streams)]
    last = None

    def ordered(values):
        return values if last is None or streams == 1 else after(values, last)

    def hop(kind, block):
        if kind == "a":
            return block, [moved(block, lambda s, z, y, c: (s + 1, z, y, c))]
        both = jnp.stack([block, swapped(block)])
        return both, [
            moved(both, lambda s, z, y, c, d=d: (s + 1, z, y + 2 * c + d, c)) for d in range(2)
        ]

    def spread(kind, arriving):
        if kind == "a":
            many = jnp.broadcast_to(arriving[0][None], (cols // 2, *arriving[0].shape))
            return many, [
                lax.all_to_all(many, "col", 0, 0, axis_index_groups=same_core, tiled=True)
            ]
        own = jnp.concatenate(arriving)
        return own, [
            own if d == 0 else moved(own, lambda s, z, y, c, d=d: (s, z + d, y, c)) for d in STEPS
        ]

    def compute(stream, tick, held):
        held = list(held)
        held = held + [swapped(piece) for piece in held]
        following = stream * BATCHES + min(tick + 1, BATCHES - 1)
        block, product, most = site(
            KINDS[stream], stream * BATCHES, BATCHES, tick, following, place, held,
            bit_strings, left_env, tensor,
        )
        products[stream].append(product)
        largest[stream].append(most)
        return block

    held = [None] * streams
    for stream, kind in enumerate(KINDS):
        start = stream * BATCHES * rows
        block = left_env[start:start + rows]
        arriving = [block] if kind == "a" else hop(kind, block)[1]
        last, held[stream] = spread(kind, arriving)
    for tick in range(ticks):
        for stream, kind in enumerate(KINDS):
            last = compute(stream, tick, ordered(held[stream]))
            if tick + 1 < ticks:
                last, arriving = hop(kind, last)
                last, held[stream] = spread(kind, arriving)

    maxima = collect(cols, ticks, streams * BATCHES, place, sum(largest, []))
    everything = lax.all_to_all(maxima, "col", 0, 0, tiled=True)
    env, log = finish(ticks, place, everything, sum(products, []))
    return env[None], log[:, :rows].reshape(1, row_count)


def solution(mesh):
    placed = (P(None, "col"), P(None, "segment"), P("segment", None, None, "col"))
    return jax.shard_map(
        local,
        mesh=mesh,
        in_specs=placed,
        out_specs=(P("segment", None, "col"), P("segment", None)),
        check_vma=False,
    )
```

time: 237 us -> 203 us (0.86)
  local copies, waits for them, and re-layouts: 38.1 us -> 8.36 us
  starting transfers between devices: 37.2 us -> 16.4 us
  Pallas kernels: 1.66 us -> 16.5 us
  waiting for transfers between devices: 20.4 us -> 33.2 us
  blocking collectives: 137 us -> 127 us
    pallas_call x6 -> x0, local copies, waits for them, and re-layouts: 30.9 us -> none  [site(): pl.pallas_call(functools.partial(kernel, blocks), out_shape=(jax.ShapeDty...]
    ppermute x13 -> x11, starting transfers between devices: 37.2 us -> 16.4 us  [moved(): return lax.ppermute(value, ('segment', 'col'), pairs)]
    pallas_call x1 -> x8, Pallas kernels: 1.66 us -> 16.5 us  [the longest x6 13.2 us: site(): pl.pallas_call(functools.partial(site_kernel, kind, slot, batches, tick,...]
    ppermute x13 -> x11, waiting for transfers between devices: 20.4 us -> 33.2 us  [moved(): return lax.ppermute(value, ('segment', 'col'), pairs)]
    all_to_all x8 -> x7, blocking collectives: 137 us -> 127 us  [the longest x6 116 us: spread(): lax.all_to_all(many, 'col', 0, 0, axis_index_groups=same_core, tiled=True)]
    unnamed x10 -> x24, local copies, waits for them, and re-layouts: 4.12 us -> 6.95 us
  transfers between devices with their start and end apart: 13 -> 11, of which waited for: 13 -> 11; matrix products, arithmetic and copies ran while one was open for 1% -> 0% of each run, Pallas kernels for 0% -> 0%
where the time goes in v2:
time: 203 us; the launch traced here: 202 us
  blocking collectives  127 us (63%)
  waiting for transfers between devices  33.2 us (16%)
  Pallas kernels  16.5 us (8%)
  starting transfers between devices  16.4 us (8%)
  local copies, waits for them, and re-layouts  8.36 us (4%)
    all_to_all x6, blocking collectives, spread(): lax.all_to_all(many, 'col', 0, 0, axis_index_groups=same_core, tiled=True)  116 us
    ppermute x11, waiting for transfers between devices, moved(): return lax.ppermute(value, ('segment', 'col'), pairs)  33.2 us
    ppermute x11, starting transfers between devices, moved(): return lax.ppermute(value, ('segment', 'col'), pairs)  16.4 us
    pallas_call x6, Pallas kernels, site(): pl.pallas_call(functools.partial(site_kernel, kind, slot, batches, tick,...  13.2 us
    all_to_all x1, blocking collectives, local(): everything = lax.all_to_all(maxima, 'col', 0, 0, tiled=True)  11.3 us
    unnamed x24, local copies, waits for them, and re-layouts  6.95 us
  transfers between devices with their start and end apart: 11, of which 11 were waited for; matrix products, arithmetic and copies ran while one was open for 0% of the time, Pallas kernels for 0%

profile of v2, /device:TPU:1, one launch (start us, length us, event | category | flops | bytes accessed | tf_op | source)
XLA Modules:
  0.0 202.3 jit_solution(13466782336241109229)
XLA Ops:
  0.6 0.8 slice.3
  1.5 0.1 broadcast_in_dim.14
  1.6 24.5 %all_to_all.35.refs_0_ = bf16[16,128,256]{2,1,0:T(8,128)(2,1)S(1)} all-to-all(bf16[16,128,256]{2,1,0:T(8,128)(2,1)S(1)} %broadcast_in_dim.14), channel_id=1, replica_groups={{0,2,4,6,8,10,12,14,16,18,20,22,24,26,28,30},{1,3,5,7,9,11,13,15,17,19,..., dimensions={0} | all-to-all | bytes 2097152 | tf_op jit(solution)/shard_map/all_to_all | solution.py:218
  26.1 2.0 collective-permute-start
  28.1 0.8 copy.5.refs_2_
  28.9 0.1 pad_add_fusion.place_ref
  29.0 1.4 collective-permute-done.refs_1_
  30.4 3.4 %copy-done = bf16[1,2,8192,256]{3,2,1,0:T(8,128)(2,1)S(1)} copy-done((bf16[1,2,8192,256]{3,2,1,0:T(8,128)(2,1)S(1)}, bf16[1,2,8192,256]{3,2,1,0:T(8,128)(2,1)}, u32[]{:S(2)}) %copy-start) | copy-done | bytes 8388632
  33.8 0.9 copy-done.2
  34.7 2.2 %site.6 = (bf16[128,256]{1,0:T(8,128)(2,1)S(1)}, f32[128,256]{1,0:T(8,128)S(1)}, f32[8,256]{1,0:T(8,128)S(1)}) custom-call(s32[4]{0:T(128)S(1)} %pad_add_fusion.place_ref, bf16[16,128,256]{2,1,0:T(8,128)(2,1)S(1)} %all_to_all.35.refs_0_, bf16[16,128,256]{2,1,0:T(8,128)(2,1)S(1)} %collective-permute-done.refs_1_, s32[384,1]{1,0:T(8,128)S(1)} %copy.5.refs_2_, ...), custom_call_target="tpu_custom_call" | custom-call | tf_op jit(solution)/shard_map/site/pallas_call | solution.py:85
  36.8 1.3 collective-permute-start.1
  38.1 3.1 %collective-permute-done.1 = bf16[128,256]{1,0:T(8,128)(2,1)S(1)} collective-permute-done((bf16[128,256]{1,0:T(8,128)(2,1)S(1)}, bf16[128,256]{1,0:T(8,128)(2,1)S(1)}, u32[]{:S(2)}, u32[]{:S(2)}) %collective-permute-start.1) | collective-permute-done | bytes 65568 | tf_op jit(solution)/shard_map/ppermute | solution.py:176
  41.2 0.1 broadcast_in_dim.15
  41.3 18.2 %all_to_all.36.refs_0_ = bf16[16,128,256]{2,1,0:T(8,128)(2,1)S(1)} all-to-all(bf16[16,128,256]{2,1,0:T(8,128)(2,1)S(1)} %broadcast_in_dim.15), channel_id=1, replica_groups={{0,2,4,6,8,10,12,14,16,18,20,22,24,26,28,30},{1,3,5,7,9,11,13,15,17,19,..., dimensions={0} | all-to-all | bytes 2097152 | tf_op jit(solution)/shard_map/all_to_all | solution.py:218
  59.5 2.7 %collective-permute-start.2 = (bf16[16,128,256]{2,1,0:T(8,128)(2,1)S(1)}, bf16[16,128,256]{2,1,0:T(8,128)(2,1)S(1)}, u32[]{:S(2)}, u32[]{:S(2)}) collective-permute-start(bf16[16,128,256]{2,1,0:T(8,128)(2,1)S(1)} %all_to_all.36.refs_0_), channel_id=1, source_target_pairs={{0,1},{1,0},{2,3},{3,2},{4,5},{5,4},{6,7},{7,6},{8,9},{9,8},{10,11... | collective-permute-start | bytes 3145736 | tf_op jit(solution)/shard_map/ppermute | solution.py:176
  62.2 2.3 %collective-permute-done.2.refs_1_ = bf16[16,128,256]{2,1,0:T(8,128)(2,1)S(1)} collective-permute-done((bf16[16,128,256]{2,1,0:T(8,128)(2,1)S(1)}, bf16[16,128,256]{2,1,0:T(8,128)(2,1)S(1)}, u32[]{:S(2)}, u32[]{:S(2)}) %collective-permute-start.2) | collective-permute-done | bytes 1048608 | tf_op jit(solution)/shard_map/ppermute | solution.py:176
  64.5 2.2 %site.7 = (bf16[128,256]{1,0:T(8,128)(2,1)S(1)}, f32[128,256]{1,0:T(8,128)S(1)}, f32[8,256]{1,0:T(8,128)S(1)}) custom-call(s32[4]{0:T(128)S(1)} %pad_add_fusion.place_ref, bf16[16,128,256]{2,1,0:T(8,128)(2,1)S(1)} %all_to_all.36.refs_0_, bf16[16,128,256]{2,1,0:T(8,128)(2,1)S(1)} %collective-permute-done.2.refs_1_, s32[384,1]{1,0:T(8,128)S(1)} %copy.5.refs_2_, ...), custom_call_target="tpu_custom_call" | custom-call | tf_op jit(solution)/shard_map/site/pallas_call | solution.py:85
  66.6 0.1 collective-permute-start.3
  66.7 4.3 %collective-permute-done.3 = bf16[128,256]{1,0:T(8,128)(2,1)S(1)} collective-permute-done((bf16[128,256]{1,0:T(8,128)(2,1)S(1)}, bf16[128,256]{1,0:T(8,128)(2,1)S(1)}, u32[]{:S(2)}, u32[]{:S(2)}) %collective-permute-start.3) | collective-permute-done | bytes 65568 | tf_op jit(solution)/shard_map/ppermute | solution.py:176
  71.0 0.1 broadcast_in_dim.16
  71.1 18.2 %all_to_all.37.refs_0_ = bf16[16,128,256]{2,1,0:T(8,128)(2,1)S(1)} all-to-all(bf16[16,128,256]{2,1,0:T(8,128)(2,1)S(1)} %broadcast_in_dim.16), channel_id=1, replica_groups={{0,2,4,6,8,10,12,14,16,18,20,22,24,26,28,30},{1,3,5,7,9,11,13,15,17,19,..., dimensions={0} | all-to-all | bytes 2097152 | tf_op jit(solution)/shard_map/all_to_all | solution.py:218
  89.3 2.6 %collective-permute-start.4 = (bf16[16,128,256]{2,1,0:T(8,128)(2,1)S(1)}, bf16[16,128,256]{2,1,0:T(8,128)(2,1)S(1)}, u32[]{:S(2)}, u32[]{:S(2)}) collective-permute-start(bf16[16,128,256]{2,1,0:T(8,128)(2,1)S(1)} %all_to_all.37.refs_0_), channel_id=1, source_target_pairs={{0,1},{1,0},{2,3},{3,2},{4,5},{5,4},{6,7},{7,6},{8,9},{9,8},{10,11... | collective-permute-start | bytes 3145736 | tf_op jit(solution)/shard_map/ppermute | solution.py:176
  91.9 2.3 %collective-permute-done.4.refs_1_ = bf16[16,128,256]{2,1,0:T(8,128)(2,1)S(1)} collective-permute-done((bf16[16,128,256]{2,1,0:T(8,128)(2,1)S(1)}, bf16[16,128,256]{2,1,0:T(8,128)(2,1)S(1)}, u32[]{:S(2)}, u32[]{:S(2)}) %collective-permute-start.4) | collective-permute-done | bytes 1048608 | tf_op jit(solution)/shard_map/ppermute | solution.py:176
  94.2 2.2 %site.8 = (bf16[128,256]{1,0:T(8,128)(2,1)S(1)}, f32[128,256]{1,0:T(8,128)S(1)}, f32[8,256]{1,0:T(8,128)S(1)}) custom-call(s32[4]{0:T(128)S(1)} %pad_add_fusion.place_ref, bf16[16,128,256]{2,1,0:T(8,128)(2,1)S(1)} %all_to_all.37.refs_0_, bf16[16,128,256]{2,1,0:T(8,128)(2,1)S(1)} %collective-permute-done.4.refs_1_, s32[384,1]{1,0:T(8,128)S(1)} %copy.5.refs_2_, ...), custom_call_target="tpu_custom_call" | custom-call | tf_op jit(solution)/shard_map/site/pallas_call | solution.py:85
  96.5 4.3 %collective-permute-done.5 = bf16[128,256]{1,0:T(8,128)(2,1)S(1)} collective-permute-done((bf16[128,256]{1,0:T(8,128)(2,1)S(1)}, bf16[128,256]{1,0:T(8,128)(2,1)S(1)}, u32[]{:S(2)}, u32[]{:S(2)}) %collective-permute-start.5) | collective-permute-done | bytes 65568 | tf_op jit(solution)/shard_map/ppermute | solution.py:176
  100.8 0.1 broadcast_in_dim.17
  100.9 18.3 %all_to_all.38.refs_0_ = bf16[16,128,256]{2,1,0:T(8,128)(2,1)S(1)} all-to-all(bf16[16,128,256]{2,1,0:T(8,128)(2,1)S(1)} %broadcast_in_dim.17), channel_id=1, replica_groups={{0,2,4,6,8,10,12,14,16,18,20,22,24,26,28,30},{1,3,5,7,9,11,13,15,17,19,..., dimensions={0} | all-to-all | bytes 2097152 | tf_op jit(solution)/shard_map/all_to_all | solution.py:218
  119.2 2.6 %collective-permute-start.6 = (bf16[16,128,256]{2,1,0:T(8,128)(2,1)S(1)}, bf16[16,128,256]{2,1,0:T(8,128)(2,1)S(1)}, u32[]{:S(2)}, u32[]{:S(2)}) collective-permute-start(bf16[16,128,256]{2,1,0:T(8,128)(2,1)S(1)} %all_to_all.38.refs_0_), channel_id=1, source_target_pairs={{0,1},{1,0},{2,3},{3,2},{4,5},{5,4},{6,7},{7,6},{8,9},{9,8},{10,11... | collective-permute-start | bytes 3145736 | tf_op jit(solution)/shard_map/ppermute | solution.py:176
  121.7 2.3 %collective-permute-done.6.refs_1_ = bf16[16,128,256]{2,1,0:T(8,128)(2,1)S(1)} collective-permute-done((bf16[16,128,256]{2,1,0:T(8,128)(2,1)S(1)}, bf16[16,128,256]{2,1,0:T(8,128)(2,1)S(1)}, u32[]{:S(2)}, u32[]{:S(2)}) %collective-permute-start.6) | collective-permute-done | bytes 1048608 | tf_op jit(solution)/shard_map/ppermute | solution.py:176
  124.0 2.1 %site.9 = (bf16[128,256]{1,0:T(8,128)(2,1)S(1)}, f32[128,256]{1,0:T(8,128)S(1)}, f32[8,256]{1,0:T(8,128)S(1)}) custom-call(s32[4]{0:T(128)S(1)} %pad_add_fusion.place_ref, bf16[16,128,256]{2,1,0:T(8,128)(2,1)S(1)} %all_to_all.38.refs_0_, bf16[16,128,256]{2,1,0:T(8,128)(2,1)S(1)} %collective-permute-done.6.refs_1_, s32[384,1]{1,0:T(8,128)S(1)} %copy.5.refs_2_, ...), custom_call_target="tpu_custom_call" | custom-call | tf_op jit(solution)/shard_map/site/pallas_call | solution.py:85
  126.2 4.3 %collective-permute-done.7 = bf16[128,256]{1,0:T(8,128)(2,1)S(1)} collective-permute-done((bf16[128,256]{1,0:T(8,128)(2,1)S(1)}, bf16[128,256]{1,0:T(8,128)(2,1)S(1)}, u32[]{:S(2)}, u32[]{:S(2)}) %collective-permute-start.7) | collective-permute-done | bytes 65568 | tf_op jit(solution)/shard_map/ppermute | solution.py:176
  130.5 0.1 broadcast_in_dim.18
  130.6 18.3 %all_to_all.39.refs_0_ = bf16[16,128,256]{2,1,0:T(8,128)(2,1)S(1)} all-to-all(bf16[16,128,256]{2,1,0:T(8,128)(2,1)S(1)} %broadcast_in_dim.18), channel_id=1, replica_groups={{0,2,4,6,8,10,12,14,16,18,20,22,24,26,28,30},{1,3,5,7,9,11,13,15,17,19,..., dimensions={0} | all-to-all | bytes 2097152 | tf_op jit(solution)/shard_map/all_to_all | solution.py:218
  148.9 2.5 %collective-permute-start.8 = (bf16[16,128,256]{2,1,0:T(8,128)(2,1)S(1)}, bf16[16,128,256]{2,1,0:T(8,128)(2,1)S(1)}, u32[]{:S(2)}, u32[]{:S(2)}) collective-permute-start(bf16[16,128,256]{2,1,0:T(8,128)(2,1)S(1)} %all_to_all.39.refs_0_), channel_id=1, source_target_pairs={{0,1},{1,0},{2,3},{3,2},{4,5},{5,4},{6,7},{7,6},{8,9},{9,8},{10,11... | collective-permute-start | bytes 3145736 | tf_op jit(solution)/shard_map/ppermute | solution.py:176
  151.4 2.3 %collective-permute-done.8.refs_1_ = bf16[16,128,256]{2,1,0:T(8,128)(2,1)S(1)} collective-permute-done((bf16[16,128,256]{2,1,0:T(8,128)(2,1)S(1)}, bf16[16,128,256]{2,1,0:T(8,128)(2,1)S(1)}, u32[]{:S(2)}, u32[]{:S(2)}) %collective-permute-start.8) | collective-permute-done | bytes 1048608 | tf_op jit(solution)/shard_map/ppermute | solution.py:176
  153.7 2.1 %site.10 = (bf16[128,256]{1,0:T(8,128)(2,1)S(1)}, f32[128,256]{1,0:T(8,128)S(1)}, f32[8,256]{1,0:T(8,128)S(1)}) custom-call(s32[4]{0:T(128)S(1)} %pad_add_fusion.place_ref, bf16[16,128,256]{2,1,0:T(8,128)(2,1)S(1)} %all_to_all.39.refs_0_, bf16[16,128,256]{2,1,0:T(8,128)(2,1)S(1)} %collective-permute-done.8.refs_1_, s32[384,1]{1,0:T(8,128)S(1)} %copy.5.refs_2_, ...), custom_call_target="tpu_custom_call" | custom-call | tf_op jit(solution)/shard_map/site/pallas_call | solution.py:85
  155.8 4.3 %collective-permute-done.9 = bf16[128,256]{1,0:T(8,128)(2,1)S(1)} collective-permute-done((bf16[128,256]{1,0:T(8,128)(2,1)S(1)}, bf16[128,256]{1,0:T(8,128)(2,1)S(1)}, u32[]{:S(2)}, u32[]{:S(2)}) %collective-permute-start.9) | collective-permute-done | bytes 65568 | tf_op jit(solution)/shard_map/ppermute | solution.py:176
  160.2 0.1 broadcast_in_dim.19
  160.3 18.3 %all_to_all.40.refs_0_ = bf16[16,128,256]{2,1,0:T(8,128)(2,1)S(1)} all-to-all(bf16[16,128,256]{2,1,0:T(8,128)(2,1)S(1)} %broadcast_in_dim.19), channel_id=1, replica_groups={{0,2,4,6,8,10,12,14,16,18,20,22,24,26,28,30},{1,3,5,7,9,11,13,15,17,19,..., dimensions={0} | all-to-all | bytes 2097152 | tf_op jit(solution)/shard_map/all_to_all | solution.py:218
  178.5 2.6 %collective-permute-start.10 = (bf16[16,128,256]{2,1,0:T(8,128)(2,1)S(1)}, bf16[16,128,256]{2,1,0:T(8,128)(2,1)S(1)}, u32[]{:S(2)}, u32[]{:S(2)}) collective-permute-start(bf16[16,128,256]{2,1,0:T(8,128)(2,1)S(1)} %all_to_all.40.refs_0_), channel_id=1, source_target_pairs={{0,1},{1,0},{2,3},{3,2},{4,5},{5,4},{6,7},{7,6},{8,9},{9,8},{10,11... | collective-permute-start | bytes 3145736 | tf_op jit(solution)/shard_map/ppermute | solution.py:176
  181.1 2.3 %collective-permute-done.10.refs_1_ = bf16[16,128,256]{2,1,0:T(8,128)(2,1)S(1)} collective-permute-done((bf16[16,128,256]{2,1,0:T(8,128)(2,1)S(1)}, bf16[16,128,256]{2,1,0:T(8,128)(2,1)S(1)}, u32[]{:S(2)}, u32[]{:S(2)}) %collective-permute-start.10) | collective-permute-done | bytes 1048608 | tf_op jit(solution)/shard_map/ppermute | solution.py:176
  183.4 2.6 %site.11 = (bf16[128,256]{1,0:T(8,128)(2,1)}, f32[128,256]{1,0:T(8,128)S(1)}, f32[8,256]{1,0:T(8,128)S(1)}) custom-call(s32[4]{0:T(128)S(1)} %pad_add_fusion.place_ref, bf16[16,128,256]{2,1,0:T(8,128)(2,1)S(1)} %all_to_all.40.refs_0_, bf16[16,128,256]{2,1,0:T(8,128)(2,1)S(1)} %collective-permute-done.10.refs_1_, s32[384,1]{1,0:T(8,128)S(1)} %copy.5.refs_2_, ...), custom_call_target="tpu_custom_call" | custom-call | tf_op jit(solution)/shard_map/site/pallas_call | solution.py:85
  185.9 0.6 copy-done.10
  186.5 1.5 collect.1
  188.0 11.3 %all_to_all.41.maxima_ref = f32[32,3,128]{2,1,0:T(4,128)S(1)} all-to-all(f32[32,3,128]{2,1,0:T(4,128)} %collect.1), channel_id=1, replica_groups=mesh['segment'=4,'col'=32] {'col'}, dimensions={0} | all-to-all | bytes 98304 | tf_op jit(solution)/shard_map/all_to_all | solution.py:251
  199.3 0.7 copy-done.4
  200.0 1.8 finish.1
  201.8 0.6 copy.13
  (21 shorter events, 0.2 us)
Async XLA Ops:
  26.1 4.3 %collective-permute-start = (bf16[16,128,256]{2,1,0:T(8,128)(2,1)S(1)}, bf16[16,128,256]{2,1,0:T(8,128)(2,1)S(1)}, u32[]{:S(2)}, u32[]{:S(2)}) collective-permute-start(bf16[16,128,256]{2,1,0:T(8,128)(2,1)S(1)} %all_to_all.35.refs_0_), channel_id=1, source_target_pairs={{0,1},{1,0},{2,3},{3,2},{4,5},{5,4},{6,7},{7,6},{8,9},{9,8},{10,11... | collective-permute-start | bytes 3145736 | tf_op jit(solution)/shard_map/ppermute | solution.py:176
  29.0 154.4 %copy-start.3 = (s32[4]{0:T(128)}, s32[4]{0:T(128)S(1)}, u32[]{:S(2)}) copy-start(s32[4]{0:T(128)S(1)} %pad_add_fusion.place_ref) | copy-start | bytes 52
  30.4 3.4 %copy-start = (bf16[1,2,8192,256]{3,2,1,0:T(8,128)(2,1)S(1)}, bf16[1,2,8192,256]{3,2,1,0:T(8,128)(2,1)}, u32[]{:S(2)}) copy-start(bf16[1,2,8192,256]{3,2,1,0:T(8,128)(2,1)} %param.5) | copy-start | bytes 25165828
  33.8 0.9 copy-start.2
  34.7 29.8 %copy-start.1 = (bf16[1,2,8192,256]{3,2,1,0:T(8,128)(2,1)S(1)}, bf16[1,2,8192,256]{3,2,1,0:T(8,128)(2,1)}, u32[]{:S(2)}) copy-start(bf16[1,2,8192,256]{3,2,1,0:T(8,128)(2,1)} %param.5) | copy-start | bytes 25165828
  36.8 52.5 %copy-start.5 = (f32[8,256]{1,0:T(8,128)}, f32[8,256]{1,0:T(8,128)S(1)}, u32[]{:S(2)}) copy-start(f32[8,256]{1,0:T(8,128)S(1)} %get-tuple-element.21.refs_0_) | copy-start | bytes 24580
  36.8 4.4 %collective-permute-start.1 = (bf16[128,256]{1,0:T(8,128)(2,1)S(1)}, bf16[128,256]{1,0:T(8,128)(2,1)S(1)}, u32[]{:S(2)}, u32[]{:S(2)}) collective-permute-start(bf16[128,256]{1,0:T(8,128)(2,1)S(1)} %get-tuple-element.22), channel_id=1, source_target_pairs={{0,32},{1,33},{2,34},{3,35},{4,36},{5,37},{6,38},{7,39},{8,40},{9,... | collective-permute-start | bytes 196616 | tf_op jit(solution)/shard_map/ppermute | solution.py:176
  59.5 5.0 %collective-permute-start.2 = (bf16[16,128,256]{2,1,0:T(8,128)(2,1)S(1)}, bf16[16,128,256]{2,1,0:T(8,128)(2,1)S(1)}, u32[]{:S(2)}, u32[]{:S(2)}) collective-permute-start(bf16[16,128,256]{2,1,0:T(8,128)(2,1)S(1)} %all_to_all.36.refs_0_), channel_id=1, source_target_pairs={{0,1},{1,0},{2,3},{3,2},{4,5},{5,4},{6,7},{7,6},{8,9},{9,8},{10,11... | collective-permute-start | bytes 3145736 | tf_op jit(solution)/shard_map/ppermute | solution.py:176
  66.6 52.5 %copy-start.6 = (f32[8,256]{1,0:T(8,128)}, f32[8,256]{1,0:T(8,128)S(1)}, u32[]{:S(2)}) copy-start(f32[8,256]{1,0:T(8,128)S(1)} %get-tuple-element.23.refs_1_) | copy-start | bytes 24580
  66.6 4.4 %collective-permute-start.3 = (bf16[128,256]{1,0:T(8,128)(2,1)S(1)}, bf16[128,256]{1,0:T(8,128)(2,1)S(1)}, u32[]{:S(2)}, u32[]{:S(2)}) collective-permute-start(bf16[128,256]{1,0:T(8,128)(2,1)S(1)} %get-tuple-element.24), channel_id=1, source_target_pairs={{0,32},{1,33},{2,34},{3,35},{4,36},{5,37},{6,38},{7,39},{8,40},{9,... | collective-permute-start | bytes 196616 | tf_op jit(solution)/shard_map/ppermute | solution.py:176
  89.3 4.9 %collective-permute-start.4 = (bf16[16,128,256]{2,1,0:T(8,128)(2,1)S(1)}, bf16[16,128,256]{2,1,0:T(8,128)(2,1)S(1)}, u32[]{:S(2)}, u32[]{:S(2)}) collective-permute-start(bf16[16,128,256]{2,1,0:T(8,128)(2,1)S(1)} %all_to_all.37.refs_0_), channel_id=1, source_target_pairs={{0,1},{1,0},{2,3},{3,2},{4,5},{5,4},{6,7},{7,6},{8,9},{9,8},{10,11... | collective-permute-start | bytes 3145736 | tf_op jit(solution)/shard_map/ppermute | solution.py:176
  96.4 52.4 %copy-start.7 = (f32[8,256]{1,0:T(8,128)}, f32[8,256]{1,0:T(8,128)S(1)}, u32[]{:S(2)}) copy-start(f32[8,256]{1,0:T(8,128)S(1)} %get-tuple-element.25.refs_2_) | copy-start | bytes 24580
  96.4 4.4 %collective-permute-start.5 = (bf16[128,256]{1,0:T(8,128)(2,1)S(1)}, bf16[128,256]{1,0:T(8,128)(2,1)S(1)}, u32[]{:S(2)}, u32[]{:S(2)}) collective-permute-start(bf16[128,256]{1,0:T(8,128)(2,1)S(1)} %get-tuple-element.26), channel_id=1, source_target_pairs={{0,32},{1,33},{2,34},{3,35},{4,36},{5,37},{6,38},{7,39},{8,40},{9,... | collective-permute-start | bytes 196616 | tf_op jit(solution)/shard_map/ppermute | solution.py:176
  119.2 4.9 %collective-permute-start.6 = (bf16[16,128,256]{2,1,0:T(8,128)(2,1)S(1)}, bf16[16,128,256]{2,1,0:T(8,128)(2,1)S(1)}, u32[]{:S(2)}, u32[]{:S(2)}) collective-permute-start(bf16[16,128,256]{2,1,0:T(8,128)(2,1)S(1)} %all_to_all.38.refs_0_), channel_id=1, source_target_pairs={{0,1},{1,0},{2,3},{3,2},{4,5},{5,4},{6,7},{7,6},{8,9},{9,8},{10,11... | collective-permute-start | bytes 3145736 | tf_op jit(solution)/shard_map/ppermute | solution.py:176
  126.1 52.4 %copy-start.8 = (f32[8,256]{1,0:T(8,128)}, f32[8,256]{1,0:T(8,128)S(1)}, u32[]{:S(2)}) copy-start(f32[8,256]{1,0:T(8,128)S(1)} %get-tuple-element.27.refs_3_) | copy-start | bytes 24580
  126.1 4.4 %collective-permute-start.7 = (bf16[128,256]{1,0:T(8,128)(2,1)S(1)}, bf16[128,256]{1,0:T(8,128)(2,1)S(1)}, u32[]{:S(2)}, u32[]{:S(2)}) collective-permute-start(bf16[128,256]{1,0:T(8,128)(2,1)S(1)} %get-tuple-element.28), channel_id=1, source_target_pairs={{0,32},{1,33},{2,34},{3,35},{4,36},{5,37},{6,38},{7,39},{8,40},{9,... | collective-permute-start | bytes 196616 | tf_op jit(solution)/shard_map/ppermute | solution.py:176
  148.9 4.8 %collective-permute-start.8 = (bf16[16,128,256]{2,1,0:T(8,128)(2,1)S(1)}, bf16[16,128,256]{2,1,0:T(8,128)(2,1)S(1)}, u32[]{:S(2)}, u32[]{:S(2)}) collective-permute-start(bf16[16,128,256]{2,1,0:T(8,128)(2,1)S(1)} %all_to_all.39.refs_0_), channel_id=1, source_target_pairs={{0,1},{1,0},{2,3},{3,2},{4,5},{5,4},{6,7},{7,6},{8,9},{9,8},{10,11... | collective-permute-start | bytes 3145736 | tf_op jit(solution)/shard_map/ppermute | solution.py:176
  155.8 30.1 %copy-start.9 = (f32[8,256]{1,0:T(8,128)}, f32[8,256]{1,0:T(8,128)S(1)}, u32[]{:S(2)}) copy-start(f32[8,256]{1,0:T(8,128)S(1)} %get-tuple-element.29.refs_4_) | copy-start | bytes 24580
  155.8 4.4 %collective-permute-start.9 = (bf16[128,256]{1,0:T(8,128)(2,1)S(1)}, bf16[128,256]{1,0:T(8,128)(2,1)S(1)}, u32[]{:S(2)}, u32[]{:S(2)}) collective-permute-start(bf16[128,256]{1,0:T(8,128)(2,1)S(1)} %get-tuple-element.30), channel_id=1, source_target_pairs={{0,32},{1,33},{2,34},{3,35},{4,36},{5,37},{6,38},{7,39},{8,40},{9,... | collective-permute-start | bytes 196616 | tf_op jit(solution)/shard_map/ppermute | solution.py:176
  178.5 4.9 %collective-permute-start.10 = (bf16[16,128,256]{2,1,0:T(8,128)(2,1)S(1)}, bf16[16,128,256]{2,1,0:T(8,128)(2,1)S(1)}, u32[]{:S(2)}, u32[]{:S(2)}) collective-permute-start(bf16[16,128,256]{2,1,0:T(8,128)(2,1)S(1)} %all_to_all.40.refs_0_), channel_id=1, source_target_pairs={{0,1},{1,0},{2,3},{3,2},{4,5},{5,4},{6,7},{7,6},{8,9},{9,8},{10,11... | collective-permute-start | bytes 3145736 | tf_op jit(solution)/shard_map/ppermute | solution.py:176
  185.9 0.6 copy-start.10
  199.3 0.7 copy-start.4

commit v3 on v0

v3 whole, which is shorter than its diff:
```python
import functools

import jax
import jax.numpy as jnp
from jax import lax
from jax.experimental import pallas as pl
from jax.experimental.pallas import tpu as pltpu
from jax.sharding import PartitionSpec as P

BATCHES = 3
RING = 4

epsilon = 1e-06

VMEM = pl.BlockSpec(memory_space=pltpu.VMEM)
SMEM = pl.BlockSpec(memory_space=pltpu.SMEM)
LIMIT = pltpu.CompilerParams(vmem_limit_bytes=24 * 1024 * 1024)


def chips_of(z, y, holder):
    sign = 1 - 2 * holder
    for step_y, step_z in ((0, 0), (0, sign), (1, 0), (-1, sign)):
        for step in range(2):
            from_y = (y - step_y - 2 * holder) & (RING - 1)
            from_z = (z - step_z - 2 * step) & (RING - 1)
            yield from_z * RING + from_y


def as_column(row, rows):
    lanes = row.shape[1]
    return jnp.broadcast_to(row, (8, lanes)).T[:rows, 0:1]


def as_row(column, lanes):
    rows = column.shape[0]
    if rows < lanes:
        column = jnp.concatenate([column, jnp.zeros((lanes - rows, 1), jnp.float32)], axis=0)
    return jnp.broadcast_to(column, (lanes, 128)).T[0:8]


def hold_kernel(tensor_ref, after_ref, held_ref, arrived):
    copies = []
    pieces = arrived.shape[0]
    depth = tensor_ref.shape[1] // pieces
    for k in range(pieces):
        part = pl.ds(k * depth, depth)
        copy = pltpu.make_async_copy(tensor_ref.at[:, part, :], held_ref.at[:, part, :], arrived.at[k])
        copy.start()
        copies.append(copy)
    for copy in copies:
        copy.wait()


def hold(tensor, after):
    return pl.pallas_call(
        hold_kernel,
        out_shape=jax.ShapeDtypeStruct(tensor.shape, tensor.dtype),
        in_specs=[pl.BlockSpec(memory_space=pltpu.HBM), pl.BlockSpec(memory_space=pl.ANY)],
        out_specs=VMEM,
        scratch_shapes=[pltpu.SemaphoreType.DMA((4,))],
        compiler_params=LIMIT,
        name="hold",
    )(pltpu.with_memory_space_constraint(tensor, pltpu.HBM), after)


def site_kernel(tick, following, batches, place_ref, *refs):
    held_refs, refs = refs[:2 * RING], refs[2 * RING:]
    bit_ref, tensor_ref, refs = refs[0], refs[1], refs[2:]
    rows, width = held_refs[0].shape[1:]
    segment, z, y, core = (place_ref[i] for i in range(4))
    work = []
    for group in range(2):
        holder = core ^ group
        for k, chip in enumerate(chips_of(z, y, holder)):
            for side in range(2):
                start = pl.multiple_of((chip * 2 + (holder ^ side)) * width, width)
                work.append((held_refs[group * RING + k // 2], 2 * (k % 2) + side, start))
    totals = [jnp.zeros((rows, width), jnp.float32) for _ in range(2)]
    largest = jnp.zeros((rows, width), jnp.bfloat16)
    for ref, index, start in work:
        piece = ref[index]
        for bit in range(2):
            totals[bit] += jnp.dot(
                piece, tensor_ref[bit, pl.ds(start, width), :], preferred_element_type=jnp.float32
            )
        largest = jnp.maximum(largest, jnp.abs(piece))
    divisor = jnp.max(largest.astype(jnp.float32), axis=1, keepdims=True) + epsilon
    divisor = jnp.where(segment == 0, 1.0, divisor)
    position = jnp.clip(tick - segment, 0, batches - 1)
    bits = as_column(bit_ref[pl.ds(position, 1), :].astype(jnp.float32), rows)
    product = jnp.where(bits > 0.5, totals[1], totals[0]) / divisor
    local = as_row(jnp.max(jnp.abs(product), axis=1, keepdims=True) + epsilon, width)
    if following is None:
        largest_refs, (product_ref, maxima_ref) = refs[:-2], refs[-2:]
        product_ref[...] = product
        everything = [ref[0:1, :] for ref in largest_refs] + [local[0:1]]
        lanes = maxima_ref.shape[2]
        for segment_here in range(RING):
            @pl.when(segment == segment_here)
            def _():
                taken = jnp.concatenate(everything[segment_here:segment_here + batches], axis=0)
                for i in range(maxima_ref.shape[0]):
                    maxima_ref[i] = taken[:, :lanes]
        return
    left_ref, product_ref, largest_ref, block_ref = refs
    product_ref[...] = product
    largest_ref[...] = local
    block_ref[...] = jnp.where(
        segment == RING - 1, left_ref[pl.ds(following * rows, rows), :], product.astype(jnp.bfloat16)
    )


def site(tick, following, place, held, bits, tensor, extra, cols):
    rows, width = held[0].shape[1:]
    batches = bits.shape[0]
    product = jax.ShapeDtypeStruct((rows, width), jnp.float32)
    if following is None:
        lanes = -(-rows // 128) * 128
        out_shape = (product, jax.ShapeDtypeStruct((cols, batches, lanes), jnp.float32))
    else:
        out_shape = (
            product,
            jax.ShapeDtypeStruct((8, width), jnp.float32),
            jax.ShapeDtypeStruct((rows, width), jnp.bfloat16),
        )
    return pl.pallas_call(
        functools.partial(site_kernel, tick, following, batches),
        out_shape=out_shape,
        in_specs=[SMEM] + [VMEM] * (len(held) + 2 + len(extra)),
        out_specs=(VMEM,) * len(out_shape),
        compiler_params=LIMIT,
        name="site",
    )(place, *held, bits, tensor, *extra)


def finish_kernel(place_ref, maxima_ref, *refs):
    product_refs, (env_ref, log_ref) = refs[:-2], refs[-2:]
    rows, width = product_refs[0].shape
    maximum = jnp.max(maxima_ref[...], axis=0)
    log_ref[...] = jnp.log(maximum)
    for batch in range(maximum.shape[0]):
        column = as_column(maximum[batch:batch + 1], rows)
        for segment in range(RING):
            @pl.when(place_ref[0] == segment)
            def _():
                product = product_refs[batch + segment][...]
                env_ref[0, batch * rows:(batch + 1) * rows, :] = (product / column).astype(jnp.bfloat16)


def finish(place, maxima, products):
    rows, width = products[0].shape
    batches = maxima.shape[1]
    return pl.pallas_call(
        finish_kernel,
        out_shape=(
            jax.ShapeDtypeStruct((1, batches * rows, width), jnp.bfloat16),
            jax.ShapeDtypeStruct((batches, maxima.shape[2]), jnp.float32),
        ),
        in_specs=[SMEM] + [VMEM] * (1 + len(products)),
        out_specs=(VMEM, VMEM),
        compiler_params=LIMIT,
        name="finish",
    )(place, maxima, *products)


def moved(value, where):
    places = [
        (s, z, y, c)
        for s in range(RING) for z in range(RING) for y in range(RING) for c in range(2)
    ]
    number = {place: i for i, place in enumerate(places)}
    pairs = []
    for place in places:
        s, z, y, c = where(*place)
        pairs.append((number[place], number[(s % RING, z % RING, y % RING, c)]))
    return lax.ppermute(value, ("segment", "col"), pairs)


def swapped(value):
    return moved(value, lambda s, z, y, c: (s, z, y, 1 - c))


def gathered(block):
    both = jnp.stack([block, swapped(block)])
    first = jnp.concatenate([
        moved(both, lambda s, z, y, c, d=d: (s + 1, z + 2 * d, y + 2 * c, c)) for d in range(2)
    ])
    return [
        first,
        moved(first, lambda s, z, y, c: (s, z + 1 - 2 * c, y, c)),
        moved(first, lambda s, z, y, c: (s, z, y + 1, c)),
        moved(first, lambda s, z, y, c: (s, z + 1 - 2 * c, y - 1, c)),
    ]


def local(left_env, bit_strings, site_tensors):
    cols = lax.axis_size("col")
    col = lax.axis_index("col")
    place = jnp.stack(
        [lax.axis_index("segment"), col // (2 * RING), (col // 2) % RING, col % 2]
    ).astype(jnp.int32)
    row_count, width = left_env.shape
    rows = row_count // BATCHES
    ticks = BATCHES + RING - 1
    bits = bit_strings.reshape(BATCHES, rows)
    block, tensor = left_env[:rows], None
    products, largest = [], []
    for tick in range(ticks):
        held = gathered(block)
        if tensor is None:
            tensor = hold(site_tensors[0], held[0])
            held, tensor, bits, place = lax.optimization_barrier((held, tensor, bits, place))
        held += [swapped(piece) for piece in held]
        if tick + 1 < ticks:
            following = min(tick + 1, BATCHES - 1)
            product, most, block = site(tick, following, place, held, bits, tensor, [left_env], cols)
            largest.append(most)
        else:
            product, maxima = site(tick, None, place, held, bits, tensor, largest, cols)
        products.append(product)

    maxima = lax.all_to_all(maxima, "col", 0, 0, tiled=True)
    env, log = finish(place, maxima, products)
    return env, log[:, :rows].reshape(1, row_count)


def solution(mesh):
    placed = (P(None, "col"), P(None, "segment"), P("segment", None, None, "col"))
    return jax.shard_map(
        local,
        mesh=mesh,
        in_specs=placed,
        out_specs=(P("segment", None, "col"), P("segment", None)),
        check_vma=False,
    )
```

time: 497 us -> 191 us (0.38)
  waiting for transfers between devices: 303 us -> 98.7 us
  matrix products: 53.1 us -> 0 us
  local copies, waits for them, and re-layouts: 41.3 us -> 1.53 us
  loops' own time: 29.5 us -> 0 us
  starting transfers between devices: 40.3 us -> 59.8 us
  Pallas kernels: 0 us -> 18.1 us
  between operations: 17.7 us -> 0.85 us
  blocking collectives: 0 us -> 11.2 us
  other arithmetic: 11.8 us -> 0.86 us
    all_gather x5 -> x0, waiting for transfers between devices: 265 us -> none  [advance(): gathered_piece = lax.all_gather(arranged_in, 'col', axis=1, tiled=True)]
    ppermute x4 -> x60, waiting for transfers between devices: 6.23 us -> 98.7 us  [moved(): return lax.ppermute(value, ('segment', 'col'), pairs)]
    dot_general x15 -> x0, matrix products: 53.1 us -> none  [one_block(): return jnp.dot(rows_block, weight_block, preferred_element_type=jnp.float32)]
    ppermute x4 -> x60, starting transfers between devices: 12.6 us -> 59.8 us  [moved(): return lax.ppermute(value, ('segment', 'col'), pairs)]
    all_to_all x5 -> x0, waiting for transfers between devices: 30.9 us -> none  [sent_to_all(): lax.all_to_all(jnp.broadcast_to(value[None], (length, *value.shape)), axi...]
    another operation x5 -> x0, loops' own time: 29.5 us -> none  [advance(): result = lax.map(one_block, (pieces, block_bit))]
    all_to_all x5 -> x0, starting transfers between devices: 27.5 us -> none  [sent_to_all(): lax.all_to_all(jnp.broadcast_to(value[None], (length, *value.shape)), axi...]
    pallas_call x0 -> x8, Pallas kernels: none -> 18.1 us  [the longest x6 12.8 us: site(): pl.pallas_call(functools.partial(site_kernel, tick, following, batches),...]
  transfers between devices with their start and end apart: 14 -> 60, of which waited for: 14 -> 43; matrix products, arithmetic and copies ran while one was open for 3% -> 0% of each run, Pallas kernels for 0% -> 2%
where the time goes in v3:
time: 191 us
  waiting for transfers between devices  98.7 us (52%)
  starting transfers between devices  59.8 us (31%)
  Pallas kernels  18.1 us (9%)
  blocking collectives  11.2 us (6%)
    ppermute x60, waiting for transfers between devices, moved(): return lax.ppermute(value, ('segment', 'col'), pairs)  98.7 us
    ppermute x60, starting transfers between devices, moved(): return lax.ppermute(value, ('segment', 'col'), pairs)  59.8 us
    pallas_call x6, Pallas kernels, site(): pl.pallas_call(functools.partial(site_kernel, tick, following, batches),...  12.8 us
    all_to_all x1, blocking collectives, local(): maxima = lax.all_to_all(maxima, 'col', 0, 0, tiled=True)  11.2 us
  transfers between devices with their start and end apart: 60, of which 43 were waited for; matrix products, arithmetic and copies ran while one was open for 0% of the time, Pallas kernels for 2%

profile of v3, /device:TPU:1, one launch (start us, length us, event | category | flops | bytes accessed | tf_op | source)
XLA Modules:
  0.0 191.1 jit_solution(14440789096518516548)
XLA Ops:
  1.5 1.5 collective-permute-start
  3.9 4.0 %collective-permute-start.1 = (bf16[2,128,256]{2,1,0:T(8,128)(2,1)S(1)}, bf16[2,128,256]{2,1,0:T(8,128)(2,1)S(1)}, u32[]{:S(2)}, u32[]{:S(2)}) collective-permute-start(bf16[2,128,256]{2,1,0:T(8,128)(2,1)S(1)} %pad_maximum_fusion), channel_id=1, source_target_pairs={{0,32},{1,37},{2,34},{3,39},{4,36},{5,33},{6,38},{7,35},{8,40},{9,... | collective-permute-start | bytes 393224 | tf_op jit(solution)/shard_map/ppermute | solution.py:176
  7.9 4.3 %collective-permute-start.2 = (bf16[2,128,256]{2,1,0:T(8,128)(2,1)S(1)}, bf16[2,128,256]{2,1,0:T(8,128)(2,1)S(1)}, u32[]{:S(2)}, u32[]{:S(2)}) collective-permute-start(bf16[2,128,256]{2,1,0:T(8,128)(2,1)S(1)} %pad_maximum_fusion), channel_id=1, source_target_pairs={{0,48},{1,53},{2,50},{3,55},{4,52},{5,49},{6,54},{7,51},{8,56},{9,... | collective-permute-start | bytes 393224 | tf_op jit(solution)/shard_map/ppermute | solution.py:176
  12.2 6.8 %collective-permute-done.2 = bf16[2,128,256]{2,1,0:T(8,128)(2,1)S(1)} collective-permute-done((bf16[2,128,256]{2,1,0:T(8,128)(2,1)S(1)}, bf16[2,128,256]{2,1,0:T(8,128)(2,1)S(1)}, u32[]{:S(2)}, u32[]{:S(2)}) %collective-permute-start.2) | collective-permute-done | bytes 131104 | tf_op jit(solution)/shard_map/ppermute | solution.py:176
  19.1 3.1 %collective-permute-start.5 = (bf16[4,128,256]{2,1,0:T(8,128)(2,1)S(1)}, bf16[4,128,256]{2,1,0:T(8,128)(2,1)S(1)}, u32[]{:S(2)}, u32[]{:S(2)}) collective-permute-start(bf16[4,128,256]{2,1,0:T(8,128)(2,1)S(1)} %constant_dynamic-update-slice_fusion.after_ref.refs_0_), channel_id=1, source_target_pairs={{0,14},{1,31},{2,8},{3,25},{4,10},{5,27},{6,12},{7,29},{8,22},{9,7... | collective-permute-start | bytes 786440 | tf_op jit(solution)/shard_map/ppermute | solution.py:176
  23.8 3.5 %hold.1.refs_9_ = bf16[2,8192,256]{2,1,0:T(8,128)(2,1)S(1)} custom-call(bf16[2,8192,256]{2,1,0:T(8,128)(2,1)} %bitcast.36, bf16[4,128,256]{2,1,0:T(8,128)(2,1)S(1)} %constant_dynamic-update-slice_fusion.after_ref.refs_0_), custom_call_target="tpu_custom_call" | custom-call | tf_op jit(solution)/shard_map/hold/pallas_call | solution.py:55
  27.6 3.4 %collective-permute-done.4.refs_2_ = bf16[4,128,256]{2,1,0:T(8,128)(2,1)S(1)} collective-permute-done((bf16[4,128,256]{2,1,0:T(8,128)(2,1)S(1)}, bf16[4,128,256]{2,1,0:T(8,128)(2,1)S(1)}, u32[]{:S(2)}, u32[]{:S(2)}) %collective-permute-start.4) | collective-permute-done | bytes 262176 | tf_op jit(solution)/shard_map/ppermute | solution.py:176
  33.7 2.1 %site.6 = (f32[128,256]{1,0:T(8,128)S(1)}, f32[8,256]{1,0:T(8,128)S(1)}, bf16[128,256]{1,0:T(8,128)(2,1)S(1)}) custom-call(s32[4]{0:T(128)S(1)} %pad_add_fusion.place_ref, bf16[4,128,256]{2,1,0:T(8,128)(2,1)S(1)} %constant_dynamic-update-slice_fusion.after_ref.refs_0_, bf16[4,128,256]{2,1,0:T(8,128)(2,1)S(1)} %collective-permute-done.3.refs_1_, ...), custom_call_target="tpu_custom_call" | custom-call | tf_op jit(solution)/shard_map/site/pallas_call | solution.py:126
  37.6 3.6 %collective-permute-start.12 = (bf16[2,128,256]{2,1,0:T(8,128)(2,1)S(1)}, bf16[2,128,256]{2,1,0:T(8,128)(2,1)S(1)}, u32[]{:S(2)}, u32[]{:S(2)}) collective-permute-start(bf16[2,128,256]{2,1,0:T(8,128)(2,1)S(1)} %pad_maximum_fusion.1), channel_id=1, source_target_pairs={{0,48},{1,53},{2,50},{3,55},{4,52},{5,49},{6,54},{7,51},{8,56},{9,... | collective-permute-start | bytes 393224 | tf_op jit(solution)/shard_map/ppermute | solution.py:176
  41.1 5.0 %collective-permute-done.11 = bf16[2,128,256]{2,1,0:T(8,128)(2,1)S(1)} collective-permute-done((bf16[2,128,256]{2,1,0:T(8,128)(2,1)S(1)}, bf16[2,128,256]{2,1,0:T(8,128)(2,1)S(1)}, u32[]{:S(2)}, u32[]{:S(2)}) %collective-permute-start.11) | collective-permute-done | bytes 131104 | tf_op jit(solution)/shard_map/ppermute | solution.py:176
  46.1 2.0 %collective-permute-done.12 = bf16[2,128,256]{2,1,0:T(8,128)(2,1)S(1)} collective-permute-done((bf16[2,128,256]{2,1,0:T(8,128)(2,1)S(1)}, bf16[2,128,256]{2,1,0:T(8,128)(2,1)S(1)}, u32[]{:S(2)}, u32[]{:S(2)}) %collective-permute-start.12) | collective-permute-done | bytes 131104 | tf_op jit(solution)/shard_map/ppermute | solution.py:176
  48.1 2.5 %collective-permute-start.15 = (bf16[4,128,256]{2,1,0:T(8,128)(2,1)S(1)}, bf16[4,128,256]{2,1,0:T(8,128)(2,1)S(1)}, u32[]{:S(2)}, u32[]{:S(2)}) collective-permute-start(bf16[4,128,256]{2,1,0:T(8,128)(2,1)S(1)} %constant_dynamic-update-slice_fusion.2.refs_0_), channel_id=1, source_target_pairs={{0,14},{1,31},{2,8},{3,25},{4,10},{5,27},{6,12},{7,29},{8,22},{9,7... | collective-permute-start | bytes 786440 | tf_op jit(solution)/shard_map/ppermute | solution.py:176
  50.6 2.1 %collective-permute-start.13 = (bf16[4,128,256]{2,1,0:T(8,128)(2,1)S(1)}, bf16[4,128,256]{2,1,0:T(8,128)(2,1)S(1)}, u32[]{:S(2)}, u32[]{:S(2)}) collective-permute-start(bf16[4,128,256]{2,1,0:T(8,128)(2,1)S(1)} %constant_dynamic-update-slice_fusion.2.refs_0_), channel_id=1, source_target_pairs={{0,8},{1,25},{2,10},{3,27},{4,12},{5,29},{6,14},{7,31},{8,16},{9,1... | collective-permute-start | bytes 786440 | tf_op jit(solution)/shard_map/ppermute | solution.py:176
  53.1 3.1 %collective-permute-done.15.refs_3_ = bf16[4,128,256]{2,1,0:T(8,128)(2,1)S(1)} collective-permute-done((bf16[4,128,256]{2,1,0:T(8,128)(2,1)S(1)}, bf16[4,128,256]{2,1,0:T(8,128)(2,1)S(1)}, u32[]{:S(2)}, u32[]{:S(2)}) %collective-permute-start.15) | collective-permute-done | bytes 262176 | tf_op jit(solution)/shard_map/ppermute | solution.py:176
  57.1 1.8 collective-permute-done.14.refs_2_
  59.0 1.6 collective-permute-start.18
  62.1 2.2 %site.7 = (f32[128,256]{1,0:T(8,128)S(1)}, f32[8,256]{1,0:T(8,128)S(1)}, bf16[128,256]{1,0:T(8,128)(2,1)S(1)}) custom-call(s32[4]{0:T(128)S(1)} %pad_add_fusion.place_ref, bf16[4,128,256]{2,1,0:T(8,128)(2,1)S(1)} %constant_dynamic-update-slice_fusion.2.refs_0_, bf16[4,128,256]{2,1,0:T(8,128)(2,1)S(1)} %collective-permute-done.13.refs_1_, ...), custom_call_target="tpu_custom_call" | custom-call | tf_op jit(solution)/shard_map/site/pallas_call | solution.py:126
  65.7 2.7 %collective-permute-start.22 = (bf16[2,128,256]{2,1,0:T(8,128)(2,1)S(1)}, bf16[2,128,256]{2,1,0:T(8,128)(2,1)S(1)}, u32[]{:S(2)}, u32[]{:S(2)}) collective-permute-start(bf16[2,128,256]{2,1,0:T(8,128)(2,1)S(1)} %pad_maximum_fusion.2), channel_id=1, source_target_pairs={{0,48},{1,53},{2,50},{3,55},{4,52},{5,49},{6,54},{7,51},{8,56},{9,... | collective-permute-start | bytes 393224 | tf_op jit(solution)/shard_map/ppermute | solution.py:176
  68.4 6.1 %collective-permute-done.21 = bf16[2,128,256]{2,1,0:T(8,128)(2,1)S(1)} collective-permute-done((bf16[2,128,256]{2,1,0:T(8,128)(2,1)S(1)}, bf16[2,128,256]{2,1,0:T(8,128)(2,1)S(1)}, u32[]{:S(2)}, u32[]{:S(2)}) %collective-permute-start.21) | collective-permute-done | bytes 131104 | tf_op jit(solution)/shard_map/ppermute | solution.py:176
  74.5 2.4 %collective-permute-done.22 = bf16[2,128,256]{2,1,0:T(8,128)(2,1)S(1)} collective-permute-done((bf16[2,128,256]{2,1,0:T(8,128)(2,1)S(1)}, bf16[2,128,256]{2,1,0:T(8,128)(2,1)S(1)}, u32[]{:S(2)}, u32[]{:S(2)}) %collective-permute-start.22) | collective-permute-done | bytes 131104 | tf_op jit(solution)/shard_map/ppermute | solution.py:176
  76.9 3.1 %collective-permute-start.25 = (bf16[4,128,256]{2,1,0:T(8,128)(2,1)S(1)}, bf16[4,128,256]{2,1,0:T(8,128)(2,1)S(1)}, u32[]{:S(2)}, u32[]{:S(2)}) collective-permute-start(bf16[4,128,256]{2,1,0:T(8,128)(2,1)S(1)} %constant_dynamic-update-slice_fusion.4.refs_0_), channel_id=1, source_target_pairs={{0,14},{1,31},{2,8},{3,25},{4,10},{5,27},{6,12},{7,29},{8,22},{9,7... | collective-permute-start | bytes 786440 | tf_op jit(solution)/shard_map/ppermute | solution.py:176
  80.0 5.8 %collective-permute-done.25.refs_3_ = bf16[4,128,256]{2,1,0:T(8,128)(2,1)S(1)} collective-permute-done((bf16[4,128,256]{2,1,0:T(8,128)(2,1)S(1)}, bf16[4,128,256]{2,1,0:T(8,128)(2,1)S(1)}, u32[]{:S(2)}, u32[]{:S(2)}) %collective-permute-start.25) | collective-permute-done | bytes 262176 | tf_op jit(solution)/shard_map/ppermute | solution.py:176
  85.8 1.2 collective-permute-start.29
  87.0 1.9 collective-permute-done.24.refs_2_
  90.8 2.2 %site.8 = (f32[128,256]{1,0:T(8,128)S(1)}, f32[8,256]{1,0:T(8,128)S(1)}, bf16[128,256]{1,0:T(8,128)(2,1)S(1)}) custom-call(s32[4]{0:T(128)S(1)} %pad_add_fusion.place_ref, bf16[4,128,256]{2,1,0:T(8,128)(2,1)S(1)} %constant_dynamic-update-slice_fusion.4.refs_0_, bf16[4,128,256]{2,1,0:T(8,128)(2,1)S(1)} %collective-permute-done.23.refs_1_, ...), custom_call_target="tpu_custom_call" | custom-call | tf_op jit(solution)/shard_map/site/pallas_call | solution.py:126
  94.4 2.4 %collective-permute-start.32 = (bf16[2,128,256]{2,1,0:T(8,128)(2,1)S(1)}, bf16[2,128,256]{2,1,0:T(8,128)(2,1)S(1)}, u32[]{:S(2)}, u32[]{:S(2)}) collective-permute-start(bf16[2,128,256]{2,1,0:T(8,128)(2,1)S(1)} %pad_maximum_fusion.3), channel_id=1, source_target_pairs={{0,48},{1,53},{2,50},{3,55},{4,52},{5,49},{6,54},{7,51},{8,56},{9,... | collective-permute-start | bytes 393224 | tf_op jit(solution)/shard_map/ppermute | solution.py:176
  96.9 6.0 %collective-permute-done.31 = bf16[2,128,256]{2,1,0:T(8,128)(2,1)S(1)} collective-permute-done((bf16[2,128,256]{2,1,0:T(8,128)(2,1)S(1)}, bf16[2,128,256]{2,1,0:T(8,128)(2,1)S(1)}, u32[]{:S(2)}, u32[]{:S(2)}) %collective-permute-start.31) | collective-permute-done | bytes 131104 | tf_op jit(solution)/shard_map/ppermute | solution.py:176
  102.9 2.7 %collective-permute-done.32 = bf16[2,128,256]{2,1,0:T(8,128)(2,1)S(1)} collective-permute-done((bf16[2,128,256]{2,1,0:T(8,128)(2,1)S(1)}, bf16[2,128,256]{2,1,0:T(8,128)(2,1)S(1)}, u32[]{:S(2)}, u32[]{:S(2)}) %collective-permute-start.32) | collective-permute-done | bytes 131104 | tf_op jit(solution)/shard_map/ppermute | solution.py:176
  105.5 2.0 %collective-permute-start.35 = (bf16[4,128,256]{2,1,0:T(8,128)(2,1)S(1)}, bf16[4,128,256]{2,1,0:T(8,128)(2,1)S(1)}, u32[]{:S(2)}, u32[]{:S(2)}) collective-permute-start(bf16[4,128,256]{2,1,0:T(8,128)(2,1)S(1)} %constant_dynamic-update-slice_fusion.6.refs_0_), channel_id=1, source_target_pairs={{0,14},{1,31},{2,8},{3,25},{4,10},{5,27},{6,12},{7,29},{8,22},{9,7... | collective-permute-start | bytes 786440 | tf_op jit(solution)/shard_map/ppermute | solution.py:176
  109.2 5.4 %collective-permute-done.35.refs_3_ = bf16[4,128,256]{2,1,0:T(8,128)(2,1)S(1)} collective-permute-done((bf16[4,128,256]{2,1,0:T(8,128)(2,1)S(1)}, bf16[4,128,256]{2,1,0:T(8,128)(2,1)S(1)}, u32[]{:S(2)}, u32[]{:S(2)}) %collective-permute-start.35) | collective-permute-done | bytes 262176 | tf_op jit(solution)/shard_map/ppermute | solution.py:176
  114.6 1.3 collective-permute-start.39
  119.0 2.2 %site.9 = (f32[128,256]{1,0:T(8,128)S(1)}, f32[8,256]{1,0:T(8,128)S(1)}, bf16[128,256]{1,0:T(8,128)(2,1)S(1)}) custom-call(s32[4]{0:T(128)S(1)} %pad_add_fusion.place_ref, bf16[4,128,256]{2,1,0:T(8,128)(2,1)S(1)} %constant_dynamic-update-slice_fusion.6.refs_0_, bf16[4,128,256]{2,1,0:T(8,128)(2,1)S(1)} %collective-permute-done.33.refs_1_, ...), custom_call_target="tpu_custom_call" | custom-call | tf_op jit(solution)/shard_map/site/pallas_call | solution.py:126
  122.6 1.8 collective-permute-start.42
  124.4 6.4 %collective-permute-done.41 = bf16[2,128,256]{2,1,0:T(8,128)(2,1)S(1)} collective-permute-done((bf16[2,128,256]{2,1,0:T(8,128)(2,1)S(1)}, bf16[2,128,256]{2,1,0:T(8,128)(2,1)S(1)}, u32[]{:S(2)}, u32[]{:S(2)}) %collective-permute-start.41) | collective-permute-done | bytes 131104 | tf_op jit(solution)/shard_map/ppermute | solution.py:176
  130.8 2.9 %collective-permute-done.42 = bf16[2,128,256]{2,1,0:T(8,128)(2,1)S(1)} collective-permute-done((bf16[2,128,256]{2,1,0:T(8,128)(2,1)S(1)}, bf16[2,128,256]{2,1,0:T(8,128)(2,1)S(1)}, u32[]{:S(2)}, u32[]{:S(2)}) %collective-permute-start.42) | collective-permute-done | bytes 131104 | tf_op jit(solution)/shard_map/ppermute | solution.py:176
  133.8 3.0 %collective-permute-start.45 = (bf16[4,128,256]{2,1,0:T(8,128)(2,1)S(1)}, bf16[4,128,256]{2,1,0:T(8,128)(2,1)S(1)}, u32[]{:S(2)}, u32[]{:S(2)}) collective-permute-start(bf16[4,128,256]{2,1,0:T(8,128)(2,1)S(1)} %constant_dynamic-update-slice_fusion.8.refs_0_), channel_id=1, source_target_pairs={{0,14},{1,31},{2,8},{3,25},{4,10},{5,27},{6,12},{7,29},{8,22},{9,7... | collective-permute-start | bytes 786440 | tf_op jit(solution)/shard_map/ppermute | solution.py:176
  137.2 5.5 %collective-permute-done.45.refs_3_ = bf16[4,128,256]{2,1,0:T(8,128)(2,1)S(1)} collective-permute-done((bf16[4,128,256]{2,1,0:T(8,128)(2,1)S(1)}, bf16[4,128,256]{2,1,0:T(8,128)(2,1)S(1)}, u32[]{:S(2)}, u32[]{:S(2)}) %collective-permute-start.45) | collective-permute-done | bytes 262176 | tf_op jit(solution)/shard_map/ppermute | solution.py:176
  142.7 1.3 collective-permute-start.49
  147.0 2.2 %site.10 = (f32[128,256]{1,0:T(8,128)S(1)}, f32[8,256]{1,0:T(8,128)S(1)}, bf16[128,256]{1,0:T(8,128)(2,1)S(1)}) custom-call(s32[4]{0:T(128)S(1)} %pad_add_fusion.place_ref, bf16[4,128,256]{2,1,0:T(8,128)(2,1)S(1)} %constant_dynamic-update-slice_fusion.8.refs_0_, bf16[4,128,256]{2,1,0:T(8,128)(2,1)S(1)} %collective-permute-done.43.refs_1_, ...), custom_call_target="tpu_custom_call" | custom-call | tf_op jit(solution)/shard_map/site/pallas_call | solution.py:126
  150.6 2.6 %collective-permute-start.52 = (bf16[2,128,256]{2,1,0:T(8,128)(2,1)S(1)}, bf16[2,128,256]{2,1,0:T(8,128)(2,1)S(1)}, u32[]{:S(2)}, u32[]{:S(2)}) collective-permute-start(bf16[2,128,256]{2,1,0:T(8,128)(2,1)S(1)} %pad_maximum_fusion.5), channel_id=1, source_target_pairs={{0,48},{1,53},{2,50},{3,55},{4,52},{5,49},{6,54},{7,51},{8,56},{9,... | collective-permute-start | bytes 393224 | tf_op jit(solution)/shard_map/ppermute | solution.py:176
  153.1 6.4 %collective-permute-done.51 = bf16[2,128,256]{2,1,0:T(8,128)(2,1)S(1)} collective-permute-done((bf16[2,128,256]{2,1,0:T(8,128)(2,1)S(1)}, bf16[2,128,256]{2,1,0:T(8,128)(2,1)S(1)}, u32[]{:S(2)}, u32[]{:S(2)}) %collective-permute-start.51) | collective-permute-done | bytes 131104 | tf_op jit(solution)/shard_map/ppermute | solution.py:176
  159.5 2.4 %collective-permute-done.52 = bf16[2,128,256]{2,1,0:T(8,128)(2,1)S(1)} collective-permute-done((bf16[2,128,256]{2,1,0:T(8,128)(2,1)S(1)}, bf16[2,128,256]{2,1,0:T(8,128)(2,1)S(1)}, u32[]{:S(2)}, u32[]{:S(2)}) %collective-permute-start.52) | collective-permute-done | bytes 131104 | tf_op jit(solution)/shard_map/ppermute | solution.py:176
  161.9 2.5 %collective-permute-start.55 = (bf16[4,128,256]{2,1,0:T(8,128)(2,1)S(1)}, bf16[4,128,256]{2,1,0:T(8,128)(2,1)S(1)}, u32[]{:S(2)}, u32[]{:S(2)}) collective-permute-start(bf16[4,128,256]{2,1,0:T(8,128)(2,1)S(1)} %constant_dynamic-update-slice_fusion.10.refs_0_), channel_id=1, source_target_pairs={{0,14},{1,31},{2,8},{3,25},{4,10},{5,27},{6,12},{7,29},{8,22},{9,7... | collective-permute-start | bytes 786440 | tf_op jit(solution)/shard_map/ppermute | solution.py:176
  165.5 5.3 %collective-permute-done.55.refs_3_ = bf16[4,128,256]{2,1,0:T(8,128)(2,1)S(1)} collective-permute-done((bf16[4,128,256]{2,1,0:T(8,128)(2,1)S(1)}, bf16[4,128,256]{2,1,0:T(8,128)(2,1)S(1)}, u32[]{:S(2)}, u32[]{:S(2)}) %collective-permute-start.55) | collective-permute-done | bytes 262176 | tf_op jit(solution)/shard_map/ppermute | solution.py:176
  170.8 1.7 collective-permute-start.59
  175.5 2.0 %site.11 = (f32[128,256]{1,0:T(8,128)S(1)}, f32[32,3,128]{2,1,0:T(4,128)S(1)}) custom-call(s32[4]{0:T(128)S(1)} %pad_add_fusion.place_ref, bf16[4,128,256]{2,1,0:T(8,128)(2,1)S(1)} %constant_dynamic-update-slice_fusion.10.refs_0_, bf16[4,128,256]{2,1,0:T(8,128)(2,1)S(1)} %collective-permute-done.53.refs_1_, ...), custom_call_target="tpu_custom_call" | custom-call | tf_op jit(solution)/shard_map/site/pallas_call | solution.py:126
  177.5 11.2 %all_to_all.5.maxima_ref = f32[32,3,128]{2,1,0:T(4,128)S(1)} all-to-all(f32[32,3,128]{2,1,0:T(4,128)S(1)} %get-tuple-element.45), channel_id=1, replica_groups=mesh['segment'=4,'col'=32] {'col'}, dimensions={0} | all-to-all | bytes 98304 | tf_op jit(solution)/shard_map/all_to_all | solution.py:222
  188.7 1.8 finish.1
  (105 shorter events, 31.5 us)
Async XLA Ops:
  1.5 2.4 %collective-permute-start = (bf16[128,256]{1,0:T(8,128)(2,1)S(1)}, bf16[128,256]{1,0:T(8,128)(2,1)S(1)}, u32[]{:S(2)}, u32[]{:S(2)}) collective-permute-start(bf16[128,256]{1,0:T(8,128)(2,1)S(1)} %get-tuple-element.55), channel_id=1, source_target_pairs={{0,1},{1,0},{2,3},{3,2},{4,5},{5,4},{6,7},{7,6},{8,9},{9,8},{10,11... | collective-permute-start | bytes 196616 | tf_op jit(solution)/shard_map/ppermute | solution.py:176
  3.9 8.3 %collective-permute-start.1 = (bf16[2,128,256]{2,1,0:T(8,128)(2,1)S(1)}, bf16[2,128,256]{2,1,0:T(8,128)(2,1)S(1)}, u32[]{:S(2)}, u32[]{:S(2)}) collective-permute-start(bf16[2,128,256]{2,1,0:T(8,128)(2,1)S(1)} %pad_maximum_fusion), channel_id=1, source_target_pairs={{0,32},{1,37},{2,34},{3,39},{4,36},{5,33},{6,38},{7,35},{8,40},{9,... | collective-permute-start | bytes 393224 | tf_op jit(solution)/shard_map/ppermute | solution.py:176
  7.9 11.2 %collective-permute-start.2 = (bf16[2,128,256]{2,1,0:T(8,128)(2,1)S(1)}, bf16[2,128,256]{2,1,0:T(8,128)(2,1)S(1)}, u32[]{:S(2)}, u32[]{:S(2)}) collective-permute-start(bf16[2,128,256]{2,1,0:T(8,128)(2,1)S(1)} %pad_maximum_fusion), channel_id=1, source_target_pairs={{0,48},{1,53},{2,50},{3,55},{4,52},{5,49},{6,54},{7,51},{8,56},{9,... | collective-permute-start | bytes 393224 | tf_op jit(solution)/shard_map/ppermute | solution.py:176
  19.1 8.6 %collective-permute-start.5 = (bf16[4,128,256]{2,1,0:T(8,128)(2,1)S(1)}, bf16[4,128,256]{2,1,0:T(8,128)(2,1)S(1)}, u32[]{:S(2)}, u32[]{:S(2)}) collective-permute-start(bf16[4,128,256]{2,1,0:T(8,128)(2,1)S(1)} %constant_dynamic-update-slice_fusion.after_ref.refs_0_), channel_id=1, source_target_pairs={{0,14},{1,31},{2,8},{3,25},{4,10},{5,27},{6,12},{7,29},{8,22},{9,7... | collective-permute-start | bytes 786440 | tf_op jit(solution)/shard_map/ppermute | solution.py:176
  22.2 8.9 %collective-permute-start.4 = (bf16[4,128,256]{2,1,0:T(8,128)(2,1)S(1)}, bf16[4,128,256]{2,1,0:T(8,128)(2,1)S(1)}, u32[]{:S(2)}, u32[]{:S(2)}) collective-permute-start(bf16[4,128,256]{2,1,0:T(8,128)(2,1)S(1)} %constant_dynamic-update-slice_fusion.after_ref.refs_0_), channel_id=1, source_target_pairs={{0,2},{1,3},{2,4},{3,5},{4,6},{5,7},{6,0},{7,1},{8,10},{9,11},{10,... | collective-permute-start | bytes 786440 | tf_op jit(solution)/shard_map/ppermute | solution.py:176
  22.9 8.2 %collective-permute-start.3 = (bf16[4,128,256]{2,1,0:T(8,128)(2,1)S(1)}, bf16[4,128,256]{2,1,0:T(8,128)(2,1)S(1)}, u32[]{:S(2)}, u32[]{:S(2)}) collective-permute-start(bf16[4,128,256]{2,1,0:T(8,128)(2,1)S(1)} %constant_dynamic-update-slice_fusion.after_ref.refs_0_), channel_id=1, source_target_pairs={{0,8},{1,25},{2,10},{3,27},{4,12},{5,29},{6,14},{7,31},{8,16},{9,1... | collective-permute-start | bytes 786440 | tf_op jit(solution)/shard_map/ppermute | solution.py:176
  31.1 1.6 collective-permute-start.6
  31.6 1.8 collective-permute-start.8
  32.0 1.8 collective-permute-start.9
  37.2 8.9 %collective-permute-start.11 = (bf16[2,128,256]{2,1,0:T(8,128)(2,1)S(1)}, bf16[2,128,256]{2,1,0:T(8,128)(2,1)S(1)}, u32[]{:S(2)}, u32[]{:S(2)}) collective-permute-start(bf16[2,128,256]{2,1,0:T(8,128)(2,1)S(1)} %pad_maximum_fusion.1), channel_id=1, source_target_pairs={{0,32},{1,37},{2,34},{3,39},{4,36},{5,33},{6,38},{7,35},{8,40},{9,... | collective-permute-start | bytes 393224 | tf_op jit(solution)/shard_map/ppermute | solution.py:176
  37.6 10.5 %collective-permute-start.12 = (bf16[2,128,256]{2,1,0:T(8,128)(2,1)S(1)}, bf16[2,128,256]{2,1,0:T(8,128)(2,1)S(1)}, u32[]{:S(2)}, u32[]{:S(2)}) collective-permute-start(bf16[2,128,256]{2,1,0:T(8,128)(2,1)S(1)} %pad_maximum_fusion.1), channel_id=1, source_target_pairs={{0,48},{1,53},{2,50},{3,55},{4,52},{5,49},{6,54},{7,51},{8,56},{9,... | collective-permute-start | bytes 393224 | tf_op jit(solution)/shard_map/ppermute | solution.py:176
  48.1 8.2 %collective-permute-start.15 = (bf16[4,128,256]{2,1,0:T(8,128)(2,1)S(1)}, bf16[4,128,256]{2,1,0:T(8,128)(2,1)S(1)}, u32[]{:S(2)}, u32[]{:S(2)}) collective-permute-start(bf16[4,128,256]{2,1,0:T(8,128)(2,1)S(1)} %constant_dynamic-update-slice_fusion.2.refs_0_), channel_id=1, source_target_pairs={{0,14},{1,31},{2,8},{3,25},{4,10},{5,27},{6,12},{7,29},{8,22},{9,7... | collective-permute-start | bytes 786440 | tf_op jit(solution)/shard_map/ppermute | solution.py:176
  50.6 8.3 %collective-permute-start.14 = (bf16[4,128,256]{2,1,0:T(8,128)(2,1)S(1)}, bf16[4,128,256]{2,1,0:T(8,128)(2,1)S(1)}, u32[]{:S(2)}, u32[]{:S(2)}) collective-permute-start(bf16[4,128,256]{2,1,0:T(8,128)(2,1)S(1)} %constant_dynamic-update-slice_fusion.2.refs_0_), channel_id=1, source_target_pairs={{0,2},{1,3},{2,4},{3,5},{4,6},{5,7},{6,0},{7,1},{8,10},{9,11},{10,... | collective-permute-start | bytes 786440 | tf_op jit(solution)/shard_map/ppermute | solution.py:176
  50.6 9.9 %collective-permute-start.13 = (bf16[4,128,256]{2,1,0:T(8,128)(2,1)S(1)}, bf16[4,128,256]{2,1,0:T(8,128)(2,1)S(1)}, u32[]{:S(2)}, u32[]{:S(2)}) collective-permute-start(bf16[4,128,256]{2,1,0:T(8,128)(2,1)S(1)} %constant_dynamic-update-slice_fusion.2.refs_0_), channel_id=1, source_target_pairs={{0,8},{1,25},{2,10},{3,27},{4,12},{5,29},{6,14},{7,31},{8,16},{9,1... | collective-permute-start | bytes 786440 | tf_op jit(solution)/shard_map/ppermute | solution.py:176
  52.7 7.9 %collective-permute-start.16 = (bf16[4,128,256]{2,1,0:T(8,128)(2,1)S(1)}, bf16[4,128,256]{2,1,0:T(8,128)(2,1)S(1)}, u32[]{:S(2)}, u32[]{:S(2)}) collective-permute-start(bf16[4,128,256]{2,1,0:T(8,128)(2,1)S(1)} %constant_dynamic-update-slice_fusion.2.refs_0_), channel_id=1, source_target_pairs={{0,1},{1,0},{2,3},{3,2},{4,5},{5,4},{6,7},{7,6},{8,9},{9,8},{10,11... | collective-permute-start | bytes 786440 | tf_op jit(solution)/shard_map/ppermute | solution.py:176
  56.3 4.3 %collective-permute-start.19 = (bf16[4,128,256]{2,1,0:T(8,128)(2,1)S(1)}, bf16[4,128,256]{2,1,0:T(8,128)(2,1)S(1)}, u32[]{:S(2)}, u32[]{:S(2)}) collective-permute-start(bf16[4,128,256]{2,1,0:T(8,128)(2,1)S(1)} %collective-permute-done.15.refs_3_), channel_id=1, source_target_pairs={{0,1},{1,0},{2,3},{3,2},{4,5},{5,4},{6,7},{7,6},{8,9},{9,8},{10,11... | collective-permute-start | bytes 786440 | tf_op jit(solution)/shard_map/ppermute | solution.py:176
  59.0 2.7 %collective-permute-start.18 = (bf16[4,128,256]{2,1,0:T(8,128)(2,1)S(1)}, bf16[4,128,256]{2,1,0:T(8,128)(2,1)S(1)}, u32[]{:S(2)}, u32[]{:S(2)}) collective-permute-start(bf16[4,128,256]{2,1,0:T(8,128)(2,1)S(1)} %collective-permute-done.14.refs_2_), channel_id=1, source_target_pairs={{0,1},{1,0},{2,3},{3,2},{4,5},{5,4},{6,7},{7,6},{8,9},{9,8},{10,11... | collective-permute-start | bytes 786440 | tf_op jit(solution)/shard_map/ppermute | solution.py:176
  65.6 8.9 %collective-permute-start.21 = (bf16[2,128,256]{2,1,0:T(8,128)(2,1)S(1)}, bf16[2,128,256]{2,1,0:T(8,128)(2,1)S(1)}, u32[]{:S(2)}, u32[]{:S(2)}) collective-permute-start(bf16[2,128,256]{2,1,0:T(8,128)(2,1)S(1)} %pad_maximum_fusion.2), channel_id=1, source_target_pairs={{0,32},{1,37},{2,34},{3,39},{4,36},{5,33},{6,38},{7,35},{8,40},{9,... | collective-permute-start | bytes 393224 | tf_op jit(solution)/shard_map/ppermute | solution.py:176
  65.7 11.2 %collective-permute-start.22 = (bf16[2,128,256]{2,1,0:T(8,128)(2,1)S(1)}, bf16[2,128,256]{2,1,0:T(8,128)(2,1)S(1)}, u32[]{:S(2)}, u32[]{:S(2)}) collective-permute-start(bf16[2,128,256]{2,1,0:T(8,128)(2,1)S(1)} %pad_maximum_fusion.2), channel_id=1, source_target_pairs={{0,48},{1,53},{2,50},{3,55},{4,52},{5,49},{6,54},{7,51},{8,56},{9,... | collective-permute-start | bytes 393224 | tf_op jit(solution)/shard_map/ppermute | solution.py:176
  76.9 8.9 %collective-permute-start.25 = (bf16[4,128,256]{2,1,0:T(8,128)(2,1)S(1)}, bf16[4,128,256]{2,1,0:T(8,128)(2,1)S(1)}, u32[]{:S(2)}, u32[]{:S(2)}) collective-permute-start(bf16[4,128,256]{2,1,0:T(8,128)(2,1)S(1)} %constant_dynamic-update-slice_fusion.4.refs_0_), channel_id=1, source_target_pairs={{0,14},{1,31},{2,8},{3,25},{4,10},{5,27},{6,12},{7,29},{8,22},{9,7... | collective-permute-start | bytes 786440 | tf_op jit(solution)/shard_map/ppermute | solution.py:176
  80.0 8.9 %collective-permute-start.24 = (bf16[4,128,256]{2,1,0:T(8,128)(2,1)S(1)}, bf16[4,128,256]{2,1,0:T(8,128)(2,1)S(1)}, u32[]{:S(2)}, u32[]{:S(2)}) collective-permute-start(bf16[4,128,256]{2,1,0:T(8,128)(2,1)S(1)} %constant_dynamic-update-slice_fusion.4.refs_0_), channel_id=1, source_target_pairs={{0,2},{1,3},{2,4},{3,5},{4,6},{5,7},{6,0},{7,1},{8,10},{9,11},{10,... | collective-permute-start | bytes 786440 | tf_op jit(solution)/shard_map/ppermute | solution.py:176
  80.0 9.3 %collective-permute-start.23 = (bf16[4,128,256]{2,1,0:T(8,128)(2,1)S(1)}, bf16[4,128,256]{2,1,0:T(8,128)(2,1)S(1)}, u32[]{:S(2)}, u32[]{:S(2)}) collective-permute-start(bf16[4,128,256]{2,1,0:T(8,128)(2,1)S(1)} %constant_dynamic-update-slice_fusion.4.refs_0_), channel_id=1, source_target_pairs={{0,8},{1,25},{2,10},{3,27},{4,12},{5,29},{6,14},{7,31},{8,16},{9,1... | collective-permute-start | bytes 786440 | tf_op jit(solution)/shard_map/ppermute | solution.py:176
  80.0 9.4 %collective-permute-start.26 = (bf16[4,128,256]{2,1,0:T(8,128)(2,1)S(1)}, bf16[4,128,256]{2,1,0:T(8,128)(2,1)S(1)}, u32[]{:S(2)}, u32[]{:S(2)}) collective-permute-start(bf16[4,128,256]{2,1,0:T(8,128)(2,1)S(1)} %constant_dynamic-update-slice_fusion.4.refs_0_), channel_id=1, source_target_pairs={{0,1},{1,0},{2,3},{3,2},{4,5},{5,4},{6,7},{7,6},{8,9},{9,8},{10,11... | collective-permute-start | bytes 786440 | tf_op jit(solution)/shard_map/ppermute | solution.py:176
  85.8 3.6 %collective-permute-start.29 = (bf16[4,128,256]{2,1,0:T(8,128)(2,1)S(1)}, bf16[4,128,256]{2,1,0:T(8,128)(2,1)S(1)}, u32[]{:S(2)}, u32[]{:S(2)}) collective-permute-start(bf16[4,128,256]{2,1,0:T(8,128)(2,1)S(1)} %collective-permute-done.25.refs_3_), channel_id=1, source_target_pairs={{0,1},{1,0},{2,3},{3,2},{4,5},{5,4},{6,7},{7,6},{8,9},{9,8},{10,11... | collective-permute-start | bytes 786440 | tf_op jit(solution)/shard_map/ppermute | solution.py:176
  94.3 8.5 %collective-permute-start.31 = (bf16[2,128,256]{2,1,0:T(8,128)(2,1)S(1)}, bf16[2,128,256]{2,1,0:T(8,128)(2,1)S(1)}, u32[]{:S(2)}, u32[]{:S(2)}) collective-permute-start(bf16[2,128,256]{2,1,0:T(8,128)(2,1)S(1)} %pad_maximum_fusion.3), channel_id=1, source_target_pairs={{0,32},{1,37},{2,34},{3,39},{4,36},{5,33},{6,38},{7,35},{8,40},{9,... | collective-permute-start | bytes 393224 | tf_op jit(solution)/shard_map/ppermute | solution.py:176
  94.4 11.1 %collective-permute-start.32 = (bf16[2,128,256]{2,1,0:T(8,128)(2,1)S(1)}, bf16[2,128,256]{2,1,0:T(8,128)(2,1)S(1)}, u32[]{:S(2)}, u32[]{:S(2)}) collective-permute-start(bf16[2,128,256]{2,1,0:T(8,128)(2,1)S(1)} %pad_maximum_fusion.3), channel_id=1, source_target_pairs={{0,48},{1,53},{2,50},{3,55},{4,52},{5,49},{6,54},{7,51},{8,56},{9,... | collective-permute-start | bytes 393224 | tf_op jit(solution)/shard_map/ppermute | solution.py:176
  105.5 9.0 %collective-permute-start.35 = (bf16[4,128,256]{2,1,0:T(8,128)(2,1)S(1)}, bf16[4,128,256]{2,1,0:T(8,128)(2,1)S(1)}, u32[]{:S(2)}, u32[]{:S(2)}) collective-permute-start(bf16[4,128,256]{2,1,0:T(8,128)(2,1)S(1)} %constant_dynamic-update-slice_fusion.6.refs_0_), channel_id=1, source_target_pairs={{0,14},{1,31},{2,8},{3,25},{4,10},{5,27},{6,12},{7,29},{8,22},{9,7... | collective-permute-start | bytes 786440 | tf_op jit(solution)/shard_map/ppermute | solution.py:176
  107.6 8.8 %collective-permute-start.34 = (bf16[4,128,256]{2,1,0:T(8,128)(2,1)S(1)}, bf16[4,128,256]{2,1,0:T(8,128)(2,1)S(1)}, u32[]{:S(2)}, u32[]{:S(2)}) collective-permute-start(bf16[4,128,256]{2,1,0:T(8,128)(2,1)S(1)} %constant_dynamic-update-slice_fusion.6.refs_0_), channel_id=1, source_target_pairs={{0,2},{1,3},{2,4},{3,5},{4,6},{5,7},{6,0},{7,1},{8,10},{9,11},{10,... | collective-permute-start | bytes 786440 | tf_op jit(solution)/shard_map/ppermute | solution.py:176
  107.9 9.6 %collective-permute-start.33 = (bf16[4,128,256]{2,1,0:T(8,128)(2,1)S(1)}, bf16[4,128,256]{2,1,0:T(8,128)(2,1)S(1)}, u32[]{:S(2)}, u32[]{:S(2)}) collective-permute-start(bf16[4,128,256]{2,1,0:T(8,128)(2,1)S(1)} %constant_dynamic-update-slice_fusion.6.refs_0_), channel_id=1, source_target_pairs={{0,8},{1,25},{2,10},{3,27},{4,12},{5,29},{6,14},{7,31},{8,16},{9,1... | collective-permute-start | bytes 786440 | tf_op jit(solution)/shard_map/ppermute | solution.py:176
  108.9 8.6 %collective-permute-start.36 = (bf16[4,128,256]{2,1,0:T(8,128)(2,1)S(1)}, bf16[4,128,256]{2,1,0:T(8,128)(2,1)S(1)}, u32[]{:S(2)}, u32[]{:S(2)}) collective-permute-start(bf16[4,128,256]{2,1,0:T(8,128)(2,1)S(1)} %constant_dynamic-update-slice_fusion.6.refs_0_), channel_id=1, source_target_pairs={{0,1},{1,0},{2,3},{3,2},{4,5},{5,4},{6,7},{7,6},{8,9},{9,8},{10,11... | collective-permute-start | bytes 786440 | tf_op jit(solution)/shard_map/ppermute | solution.py:176
  114.6 2.9 %collective-permute-start.39 = (bf16[4,128,256]{2,1,0:T(8,128)(2,1)S(1)}, bf16[4,128,256]{2,1,0:T(8,128)(2,1)S(1)}, u32[]{:S(2)}, u32[]{:S(2)}) collective-permute-start(bf16[4,128,256]{2,1,0:T(8,128)(2,1)S(1)} %collective-permute-done.35.refs_3_), channel_id=1, source_target_pairs={{0,1},{1,0},{2,3},{3,2},{4,5},{5,4},{6,7},{7,6},{8,9},{9,8},{10,11... | collective-permute-start | bytes 786440 | tf_op jit(solution)/shard_map/ppermute | solution.py:176
  116.4 2.3 %collective-permute-start.38 = (bf16[4,128,256]{2,1,0:T(8,128)(2,1)S(1)}, bf16[4,128,256]{2,1,0:T(8,128)(2,1)S(1)}, u32[]{:S(2)}, u32[]{:S(2)}) collective-permute-start(bf16[4,128,256]{2,1,0:T(8,128)(2,1)S(1)} %collective-permute-done.34.refs_2_), channel_id=1, source_target_pairs={{0,1},{1,0},{2,3},{3,2},{4,5},{5,4},{6,7},{7,6},{8,9},{9,8},{10,11... | collective-permute-start | bytes 786440 | tf_op jit(solution)/shard_map/ppermute | solution.py:176
  122.6 8.3 %collective-permute-start.41 = (bf16[2,128,256]{2,1,0:T(8,128)(2,1)S(1)}, bf16[2,128,256]{2,1,0:T(8,128)(2,1)S(1)}, u32[]{:S(2)}, u32[]{:S(2)}) collective-permute-start(bf16[2,128,256]{2,1,0:T(8,128)(2,1)S(1)} %pad_maximum_fusion.4), channel_id=1, source_target_pairs={{0,32},{1,37},{2,34},{3,39},{4,36},{5,33},{6,38},{7,35},{8,40},{9,... | collective-permute-start | bytes 393224 | tf_op jit(solution)/shard_map/ppermute | solution.py:176
  122.6 11.1 %collective-permute-start.42 = (bf16[2,128,256]{2,1,0:T(8,128)(2,1)S(1)}, bf16[2,128,256]{2,1,0:T(8,128)(2,1)S(1)}, u32[]{:S(2)}, u32[]{:S(2)}) collective-permute-start(bf16[2,128,256]{2,1,0:T(8,128)(2,1)S(1)} %pad_maximum_fusion.4), channel_id=1, source_target_pairs={{0,48},{1,53},{2,50},{3,55},{4,52},{5,49},{6,54},{7,51},{8,56},{9,... | collective-permute-start | bytes 393224 | tf_op jit(solution)/shard_map/ppermute | solution.py:176
  133.8 9.0 %collective-permute-start.45 = (bf16[4,128,256]{2,1,0:T(8,128)(2,1)S(1)}, bf16[4,128,256]{2,1,0:T(8,128)(2,1)S(1)}, u32[]{:S(2)}, u32[]{:S(2)}) collective-permute-start(bf16[4,128,256]{2,1,0:T(8,128)(2,1)S(1)} %constant_dynamic-update-slice_fusion.8.refs_0_), channel_id=1, source_target_pairs={{0,14},{1,31},{2,8},{3,25},{4,10},{5,27},{6,12},{7,29},{8,22},{9,7... | collective-permute-start | bytes 786440 | tf_op jit(solution)/shard_map/ppermute | solution.py:176
  136.8 8.2 %collective-permute-start.44 = (bf16[4,128,256]{2,1,0:T(8,128)(2,1)S(1)}, bf16[4,128,256]{2,1,0:T(8,128)(2,1)S(1)}, u32[]{:S(2)}, u32[]{:S(2)}) collective-permute-start(bf16[4,128,256]{2,1,0:T(8,128)(2,1)S(1)} %constant_dynamic-update-slice_fusion.8.refs_0_), channel_id=1, source_target_pairs={{0,2},{1,3},{2,4},{3,5},{4,6},{5,7},{6,0},{7,1},{8,10},{9,11},{10,... | collective-permute-start | bytes 786440 | tf_op jit(solution)/shard_map/ppermute | solution.py:176
  136.8 8.2 %collective-permute-start.43 = (bf16[4,128,256]{2,1,0:T(8,128)(2,1)S(1)}, bf16[4,128,256]{2,1,0:T(8,128)(2,1)S(1)}, u32[]{:S(2)}, u32[]{:S(2)}) collective-permute-start(bf16[4,128,256]{2,1,0:T(8,128)(2,1)S(1)} %constant_dynamic-update-slice_fusion.8.refs_0_), channel_id=1, source_target_pairs={{0,8},{1,25},{2,10},{3,27},{4,12},{5,29},{6,14},{7,31},{8,16},{9,1... | collective-permute-start | bytes 786440 | tf_op jit(solution)/shard_map/ppermute | solution.py:176
  137.2 8.3 %collective-permute-start.46 = (bf16[4,128,256]{2,1,0:T(8,128)(2,1)S(1)}, bf16[4,128,256]{2,1,0:T(8,128)(2,1)S(1)}, u32[]{:S(2)}, u32[]{:S(2)}) collective-permute-start(bf16[4,128,256]{2,1,0:T(8,128)(2,1)S(1)} %constant_dynamic-update-slice_fusion.8.refs_0_), channel_id=1, source_target_pairs={{0,1},{1,0},{2,3},{3,2},{4,5},{5,4},{6,7},{7,6},{8,9},{9,8},{10,11... | collective-permute-start | bytes 786440 | tf_op jit(solution)/shard_map/ppermute | solution.py:176
  142.7 2.8 %collective-permute-start.49 = (bf16[4,128,256]{2,1,0:T(8,128)(2,1)S(1)}, bf16[4,128,256]{2,1,0:T(8,128)(2,1)S(1)}, u32[]{:S(2)}, u32[]{:S(2)}) collective-permute-start(bf16[4,128,256]{2,1,0:T(8,128)(2,1)S(1)} %collective-permute-done.45.refs_3_), channel_id=1, source_target_pairs={{0,1},{1,0},{2,3},{3,2},{4,5},{5,4},{6,7},{7,6},{8,9},{9,8},{10,11... | collective-permute-start | bytes 786440 | tf_op jit(solution)/shard_map/ppermute | solution.py:176
  145.1 1.9 collective-permute-start.47
  150.5 9.1 %collective-permute-start.51 = (bf16[2,128,256]{2,1,0:T(8,128)(2,1)S(1)}, bf16[2,128,256]{2,1,0:T(8,128)(2,1)S(1)}, u32[]{:S(2)}, u32[]{:S(2)}) collective-permute-start(bf16[2,128,256]{2,1,0:T(8,128)(2,1)S(1)} %pad_maximum_fusion.5), channel_id=1, source_target_pairs={{0,32},{1,37},{2,34},{3,39},{4,36},{5,33},{6,38},{7,35},{8,40},{9,... | collective-permute-start | bytes 393224 | tf_op jit(solution)/shard_map/ppermute | solution.py:176
  150.6 11.4 %collective-permute-start.52 = (bf16[2,128,256]{2,1,0:T(8,128)(2,1)S(1)}, bf16[2,128,256]{2,1,0:T(8,128)(2,1)S(1)}, u32[]{:S(2)}, u32[]{:S(2)}) collective-permute-start(bf16[2,128,256]{2,1,0:T(8,128)(2,1)S(1)} %pad_maximum_fusion.5), channel_id=1, source_target_pairs={{0,48},{1,53},{2,50},{3,55},{4,52},{5,49},{6,54},{7,51},{8,56},{9,... | collective-permute-start | bytes 393224 | tf_op jit(solution)/shard_map/ppermute | solution.py:176
  161.9 8.9 %collective-permute-start.55 = (bf16[4,128,256]{2,1,0:T(8,128)(2,1)S(1)}, bf16[4,128,256]{2,1,0:T(8,128)(2,1)S(1)}, u32[]{:S(2)}, u32[]{:S(2)}) collective-permute-start(bf16[4,128,256]{2,1,0:T(8,128)(2,1)S(1)} %constant_dynamic-update-slice_fusion.10.refs_0_), channel_id=1, source_target_pairs={{0,14},{1,31},{2,8},{3,25},{4,10},{5,27},{6,12},{7,29},{8,22},{9,7... | collective-permute-start | bytes 786440 | tf_op jit(solution)/shard_map/ppermute | solution.py:176
  164.4 9.1 %collective-permute-start.54 = (bf16[4,128,256]{2,1,0:T(8,128)(2,1)S(1)}, bf16[4,128,256]{2,1,0:T(8,128)(2,1)S(1)}, u32[]{:S(2)}, u32[]{:S(2)}) collective-permute-start(bf16[4,128,256]{2,1,0:T(8,128)(2,1)S(1)} %constant_dynamic-update-slice_fusion.10.refs_0_), channel_id=1, source_target_pairs={{0,2},{1,3},{2,4},{3,5},{4,6},{5,7},{6,0},{7,1},{8,10},{9,11},{10,... | collective-permute-start | bytes 786440 | tf_op jit(solution)/shard_map/ppermute | solution.py:176
  164.4 9.5 %collective-permute-start.53 = (bf16[4,128,256]{2,1,0:T(8,128)(2,1)S(1)}, bf16[4,128,256]{2,1,0:T(8,128)(2,1)S(1)}, u32[]{:S(2)}, u32[]{:S(2)}) collective-permute-start(bf16[4,128,256]{2,1,0:T(8,128)(2,1)S(1)} %constant_dynamic-update-slice_fusion.10.refs_0_), channel_id=1, source_target_pairs={{0,8},{1,25},{2,10},{3,27},{4,12},{5,29},{6,14},{7,31},{8,16},{9,1... | collective-permute-start | bytes 786440 | tf_op jit(solution)/shard_map/ppermute | solution.py:176
  165.4 8.7 %collective-permute-start.56 = (bf16[4,128,256]{2,1,0:T(8,128)(2,1)S(1)}, bf16[4,128,256]{2,1,0:T(8,128)(2,1)S(1)}, u32[]{:S(2)}, u32[]{:S(2)}) collective-permute-start(bf16[4,128,256]{2,1,0:T(8,128)(2,1)S(1)} %constant_dynamic-update-slice_fusion.10.refs_0_), channel_id=1, source_target_pairs={{0,1},{1,0},{2,3},{3,2},{4,5},{5,4},{6,7},{7,6},{8,9},{9,8},{10,11... | collective-permute-start | bytes 786440 | tf_op jit(solution)/shard_map/ppermute | solution.py:176
  170.8 3.3 %collective-permute-start.59 = (bf16[4,128,256]{2,1,0:T(8,128)(2,1)S(1)}, bf16[4,128,256]{2,1,0:T(8,128)(2,1)S(1)}, u32[]{:S(2)}, u32[]{:S(2)}) collective-permute-start(bf16[4,128,256]{2,1,0:T(8,128)(2,1)S(1)} %collective-permute-done.55.refs_3_), channel_id=1, source_target_pairs={{0,1},{1,0},{2,3},{3,2},{4,5},{5,4},{6,7},{7,6},{8,9},{9,8},{10,11... | collective-permute-start | bytes 786440 | tf_op jit(solution)/shard_map/ppermute | solution.py:176
  173.6 1.6 collective-permute-start.58
  (13 other events, 27.3 us)

commit v4 on v3

--- a/solution.py
+++ b/solution.py
@@ -36,6 +36,10 @@
     if rows < lanes:
         column = jnp.concatenate([column, jnp.zeros((lanes - rows, 1), jnp.float32)], axis=0)
     return jnp.broadcast_to(column, (lanes, 128)).T[0:8]
+
+
+def largest_lanes(rows):
+    return -(-rows // 128) * 128
 
 
 def hold_kernel(tensor_ref, after_ref, held_ref, arrived):
@@ -88,19 +92,19 @@
     divisor = jnp.where(segment == 0, 1.0, divisor)
     position = jnp.clip(tick - segment, 0, batches - 1)
     bits = as_column(bit_ref[pl.ds(position, 1), :].astype(jnp.float32), rows)
-    product = jnp.where(bits > 0.5, totals[1], totals[0]) / divisor
-    local = as_row(jnp.max(jnp.abs(product), axis=1, keepdims=True) + epsilon, width)
+    product = jnp.where(bits > 0.5, totals[1], totals[0]) * (1.0 / divisor)
+    lanes = largest_lanes(rows)
+    local = as_row(jnp.max(jnp.abs(product), axis=1, keepdims=True) + epsilon, lanes)
     if following is None:
         largest_refs, (product_ref, maxima_ref) = refs[:-2], refs[-2:]
         product_ref[...] = product
         everything = [ref[0:1, :] for ref in largest_refs] + [local[0:1]]
-        lanes = maxima_ref.shape[2]
         for segment_here in range(RING):
             @pl.when(segment == segment_here)
             def _():
                 taken = jnp.concatenate(everything[segment_here:segment_here + batches], axis=0)
                 for i in range(maxima_ref.shape[0]):
-                    maxima_ref[i] = taken[:, :lanes]
+                    maxima_ref[i] = taken
         return
     left_ref, product_ref, largest_ref, block_ref = refs
     product_ref[...] = product
@@ -115,12 +119,14 @@
     batches = bits.shape[0]
     product = jax.ShapeDtypeStruct((rows, width), jnp.float32)
     if following is None:
-        lanes = -(-rows // 128) * 128
-        out_shape = (product, jax.ShapeDtypeStruct((cols, batches, lanes), jnp.float32))
+        out_shape = (
+            product,
+            jax.ShapeDtypeStruct((cols, batches, largest_lanes(rows)), jnp.float32),
+        )
     else:
         out_shape = (
             product,
-            jax.ShapeDtypeStruct((8, width), jnp.float32),
+            jax.ShapeDtypeStruct((8, largest_lanes(rows)), jnp.float32),
             jax.ShapeDtypeStruct((rows, width), jnp.bfloat16),
         )
     return pl.pallas_call(
@@ -137,14 +143,16 @@
     product_refs, (env_ref, log_ref) = refs[:-2], refs[-2:]
     rows, width = product_refs[0].shape
     maximum = jnp.max(maxima_ref[...], axis=0)
-    log_ref[...] = jnp.log(maximum)
+    logs = jnp.log(maximum)
+    inverse = 1.0 / maximum
     for batch in range(maximum.shape[0]):
-        column = as_column(maximum[batch:batch + 1], rows)
+        log_ref[0:1, batch * rows:(batch + 1) * rows] = logs[batch:batch + 1, :rows]
+        column = as_column(inverse[batch:batch + 1], rows)
         for segment in range(RING):
             @pl.when(place_ref[0] == segment)
             def _():
                 product = product_refs[batch + segment][...]
-                env_ref[0, batch * rows:(batch + 1) * rows, :] = (product / column).astype(jnp.bfloat16)
+                env_ref[0, batch * rows:(batch + 1) * rows, :] = (product * column).astype(jnp.bfloat16)
 
 
 def finish(place, maxima, products):
@@ -154,7 +162,7 @@
         finish_kernel,
         out_shape=(
             jax.ShapeDtypeStruct((1, batches * rows, width), jnp.bfloat16),
-            jax.ShapeDtypeStruct((batches, maxima.shape[2]), jnp.float32),
+            jax.ShapeDtypeStruct((1, batches * rows), jnp.float32),
         ),
         in_specs=[SMEM] + [VMEM] * (1 + len(products)),
         out_specs=(VMEM, VMEM),
@@ -180,8 +188,8 @@
     return moved(value, lambda s, z, y, c: (s, z, y, 1 - c))
 
 
-def gathered(block):
-    both = jnp.stack([block, swapped(block)])
+def gathered(block, other):
+    both = jnp.stack([block, other])
     first = jnp.concatenate([
         moved(both, lambda s, z, y, c, d=d: (s + 1, z + 2 * d, y + 2 * c, c)) for d in range(2)
     ])
@@ -203,10 +211,11 @@
     rows = row_count // BATCHES
     ticks = BATCHES + RING - 1
     bits = bit_strings.reshape(BATCHES, rows)
-    block, tensor = left_env[:rows], None
+    tensor = None
+    block, other = left_env[:rows], swapped(left_env)[:rows]
     products, largest = [], []
     for tick in range(ticks):
-        held = gathered(block)
+        held = gathered(block, swapped(block) if tick > 0 else other)
         if tensor is None:
             tensor = hold(site_tensors[0], held[0])
             held, tensor, bits, place = lax.optimization_barrier((held, tensor, bits, place))
@@ -220,8 +229,7 @@
         products.append(product)
 
     maxima = lax.all_to_all(maxima, "col", 0, 0, tiled=True)
-    env, log = finish(place, maxima, products)
-    return env, log[:, :rows].reshape(1, row_count)
+    return finish(place, maxima, products)
 
 
 def solution(mesh):

time: 191 us -> 190 us (level)
  transfers between devices with their start and end apart: 60 -> 60, of which waited for: 43 -> 43; matrix products, arithmetic and copies ran while one was open for 0% -> 1% of each run, Pallas kernels for 2% -> 2%
where the time goes in v4:
time: 190 us
  waiting for transfers between devices  98.6 us (52%)
  starting transfers between devices  59.7 us (31%)
  Pallas kernels  17.6 us (9%)
  blocking collectives  11.1 us (6%)
    ppermute x60, waiting for transfers between devices, moved(): return lax.ppermute(value, ('segment', 'col'), pairs)  98.6 us
    ppermute x60, starting transfers between devices, moved(): return lax.ppermute(value, ('segment', 'col'), pairs)  59.7 us
    pallas_call x6, Pallas kernels, site(): pl.pallas_call(functools.partial(site_kernel, tick, following, batches),...  12.3 us
    all_to_all x1, blocking collectives, local(): maxima = lax.all_to_all(maxima, 'col', 0, 0, tiled=True)  11.1 us
  transfers between devices with their start and end apart: 60, of which 43 were waited for; matrix products, arithmetic and copies ran while one was open for 1% of the time, Pallas kernels for 2%

profile of v4, /device:TPU:1, one launch (start us, length us, event | category | flops | bytes accessed | tf_op | source)
XLA Modules:
  0.0 189.6 jit_solution(3641568092726630812)
XLA Ops:
  0.6 1.5 collective-permute-start
  3.4 4.0 %collective-permute-start.1 = (bf16[2,128,256]{2,1,0:T(8,128)(2,1)S(1)}, bf16[2,128,256]{2,1,0:T(8,128)(2,1)S(1)}, u32[]{:S(2)}, u32[]{:S(2)}) collective-permute-start(bf16[2,128,256]{2,1,0:T(8,128)(2,1)S(1)} %pad_maximum_fusion), channel_id=1, source_target_pairs={{0,32},{1,37},{2,34},{3,39},{4,36},{5,33},{6,38},{7,35},{8,40},{9,... | collective-permute-start | bytes 393224 | tf_op jit(solution)/shard_map/ppermute | solution.py:184
  7.4 4.3 %collective-permute-start.2 = (bf16[2,128,256]{2,1,0:T(8,128)(2,1)S(1)}, bf16[2,128,256]{2,1,0:T(8,128)(2,1)S(1)}, u32[]{:S(2)}, u32[]{:S(2)}) collective-permute-start(bf16[2,128,256]{2,1,0:T(8,128)(2,1)S(1)} %pad_maximum_fusion), channel_id=1, source_target_pairs={{0,48},{1,53},{2,50},{3,55},{4,52},{5,49},{6,54},{7,51},{8,56},{9,... | collective-permute-start | bytes 393224 | tf_op jit(solution)/shard_map/ppermute | solution.py:184
  11.7 6.8 %collective-permute-done.2 = bf16[2,128,256]{2,1,0:T(8,128)(2,1)S(1)} collective-permute-done((bf16[2,128,256]{2,1,0:T(8,128)(2,1)S(1)}, bf16[2,128,256]{2,1,0:T(8,128)(2,1)S(1)}, u32[]{:S(2)}, u32[]{:S(2)}) %collective-permute-start.2) | collective-permute-done | bytes 131104 | tf_op jit(solution)/shard_map/ppermute | solution.py:184
  18.6 3.1 %collective-permute-start.5 = (bf16[4,128,256]{2,1,0:T(8,128)(2,1)S(1)}, bf16[4,128,256]{2,1,0:T(8,128)(2,1)S(1)}, u32[]{:S(2)}, u32[]{:S(2)}) collective-permute-start(bf16[4,128,256]{2,1,0:T(8,128)(2,1)S(1)} %constant_dynamic-update-slice_fusion.after_ref.refs_0_), channel_id=1, source_target_pairs={{0,14},{1,31},{2,8},{3,25},{4,10},{5,27},{6,12},{7,29},{8,22},{9,7... | collective-permute-start | bytes 786440 | tf_op jit(solution)/shard_map/ppermute | solution.py:184
  23.3 3.5 %hold.1.refs_9_ = bf16[2,8192,256]{2,1,0:T(8,128)(2,1)S(1)} custom-call(bf16[2,8192,256]{2,1,0:T(8,128)(2,1)} %bitcast.31, bf16[4,128,256]{2,1,0:T(8,128)(2,1)S(1)} %constant_dynamic-update-slice_fusion.after_ref.refs_0_), custom_call_target="tpu_custom_call" | custom-call | tf_op jit(solution)/shard_map/hold/pallas_call | solution.py:59
  27.2 3.4 %collective-permute-done.4.refs_2_ = bf16[4,128,256]{2,1,0:T(8,128)(2,1)S(1)} collective-permute-done((bf16[4,128,256]{2,1,0:T(8,128)(2,1)S(1)}, bf16[4,128,256]{2,1,0:T(8,128)(2,1)S(1)}, u32[]{:S(2)}, u32[]{:S(2)}) %collective-permute-start.4) | collective-permute-done | bytes 262176 | tf_op jit(solution)/shard_map/ppermute | solution.py:184
  33.3 2.1 %site.6 = (f32[128,256]{1,0:T(8,128)S(1)}, f32[8,128]{1,0:T(8,128)S(1)}, bf16[128,256]{1,0:T(8,128)(2,1)S(1)}) custom-call(s32[4]{0:T(128)S(1)} %pad_add_fusion.place_ref, bf16[4,128,256]{2,1,0:T(8,128)(2,1)S(1)} %constant_dynamic-update-slice_fusion.after_ref.refs_0_, bf16[4,128,256]{2,1,0:T(8,128)(2,1)S(1)} %collective-permute-done.3.refs_1_, ...), custom_call_target="tpu_custom_call" | custom-call | tf_op jit(solution)/shard_map/site/pallas_call | solution.py:132
  37.1 3.6 %collective-permute-start.12 = (bf16[2,128,256]{2,1,0:T(8,128)(2,1)S(1)}, bf16[2,128,256]{2,1,0:T(8,128)(2,1)S(1)}, u32[]{:S(2)}, u32[]{:S(2)}) collective-permute-start(bf16[2,128,256]{2,1,0:T(8,128)(2,1)S(1)} %pad_maximum_fusion.1), channel_id=1, source_target_pairs={{0,48},{1,53},{2,50},{3,55},{4,52},{5,49},{6,54},{7,51},{8,56},{9,... | collective-permute-start | bytes 393224 | tf_op jit(solution)/shard_map/ppermute | solution.py:184
  40.8 4.9 %collective-permute-done.11 = bf16[2,128,256]{2,1,0:T(8,128)(2,1)S(1)} collective-permute-done((bf16[2,128,256]{2,1,0:T(8,128)(2,1)S(1)}, bf16[2,128,256]{2,1,0:T(8,128)(2,1)S(1)}, u32[]{:S(2)}, u32[]{:S(2)}) %collective-permute-start.11) | collective-permute-done | bytes 131104 | tf_op jit(solution)/shard_map/ppermute | solution.py:184
  45.7 2.1 %collective-permute-done.12 = bf16[2,128,256]{2,1,0:T(8,128)(2,1)S(1)} collective-permute-done((bf16[2,128,256]{2,1,0:T(8,128)(2,1)S(1)}, bf16[2,128,256]{2,1,0:T(8,128)(2,1)S(1)}, u32[]{:S(2)}, u32[]{:S(2)}) %collective-permute-start.12) | collective-permute-done | bytes 131104 | tf_op jit(solution)/shard_map/ppermute | solution.py:184
  47.7 2.5 %collective-permute-start.15 = (bf16[4,128,256]{2,1,0:T(8,128)(2,1)S(1)}, bf16[4,128,256]{2,1,0:T(8,128)(2,1)S(1)}, u32[]{:S(2)}, u32[]{:S(2)}) collective-permute-start(bf16[4,128,256]{2,1,0:T(8,128)(2,1)S(1)} %constant_dynamic-update-slice_fusion.2.refs_0_), channel_id=1, source_target_pairs={{0,14},{1,31},{2,8},{3,25},{4,10},{5,27},{6,12},{7,29},{8,22},{9,7... | collective-permute-start | bytes 786440 | tf_op jit(solution)/shard_map/ppermute | solution.py:184
  50.2 2.1 %collective-permute-start.13 = (bf16[4,128,256]{2,1,0:T(8,128)(2,1)S(1)}, bf16[4,128,256]{2,1,0:T(8,128)(2,1)S(1)}, u32[]{:S(2)}, u32[]{:S(2)}) collective-permute-start(bf16[4,128,256]{2,1,0:T(8,128)(2,1)S(1)} %constant_dynamic-update-slice_fusion.2.refs_0_), channel_id=1, source_target_pairs={{0,8},{1,25},{2,10},{3,27},{4,12},{5,29},{6,14},{7,31},{8,16},{9,1... | collective-permute-start | bytes 786440 | tf_op jit(solution)/shard_map/ppermute | solution.py:184
  52.7 3.3 %collective-permute-done.15.refs_3_ = bf16[4,128,256]{2,1,0:T(8,128)(2,1)S(1)} collective-permute-done((bf16[4,128,256]{2,1,0:T(8,128)(2,1)S(1)}, bf16[4,128,256]{2,1,0:T(8,128)(2,1)S(1)}, u32[]{:S(2)}, u32[]{:S(2)}) %collective-permute-start.15) | collective-permute-done | bytes 262176 | tf_op jit(solution)/shard_map/ppermute | solution.py:184
  56.7 1.8 collective-permute-done.14.refs_2_
  58.5 1.6 collective-permute-start.18
  61.7 2.1 %site.7 = (f32[128,256]{1,0:T(8,128)S(1)}, f32[8,128]{1,0:T(8,128)S(1)}, bf16[128,256]{1,0:T(8,128)(2,1)S(1)}) custom-call(s32[4]{0:T(128)S(1)} %pad_add_fusion.place_ref, bf16[4,128,256]{2,1,0:T(8,128)(2,1)S(1)} %constant_dynamic-update-slice_fusion.2.refs_0_, bf16[4,128,256]{2,1,0:T(8,128)(2,1)S(1)} %collective-permute-done.13.refs_1_, ...), custom_call_target="tpu_custom_call" | custom-call | tf_op jit(solution)/shard_map/site/pallas_call | solution.py:132
  65.1 2.7 %collective-permute-start.22 = (bf16[2,128,256]{2,1,0:T(8,128)(2,1)S(1)}, bf16[2,128,256]{2,1,0:T(8,128)(2,1)S(1)}, u32[]{:S(2)}, u32[]{:S(2)}) collective-permute-start(bf16[2,128,256]{2,1,0:T(8,128)(2,1)S(1)} %pad_maximum_fusion.2), channel_id=1, source_target_pairs={{0,48},{1,53},{2,50},{3,55},{4,52},{5,49},{6,54},{7,51},{8,56},{9,... | collective-permute-start | bytes 393224 | tf_op jit(solution)/shard_map/ppermute | solution.py:184
  67.8 6.1 %collective-permute-done.21 = bf16[2,128,256]{2,1,0:T(8,128)(2,1)S(1)} collective-permute-done((bf16[2,128,256]{2,1,0:T(8,128)(2,1)S(1)}, bf16[2,128,256]{2,1,0:T(8,128)(2,1)S(1)}, u32[]{:S(2)}, u32[]{:S(2)}) %collective-permute-start.21) | collective-permute-done | bytes 131104 | tf_op jit(solution)/shard_map/ppermute | solution.py:184
  74.0 2.4 %collective-permute-done.22 = bf16[2,128,256]{2,1,0:T(8,128)(2,1)S(1)} collective-permute-done((bf16[2,128,256]{2,1,0:T(8,128)(2,1)S(1)}, bf16[2,128,256]{2,1,0:T(8,128)(2,1)S(1)}, u32[]{:S(2)}, u32[]{:S(2)}) %collective-permute-start.22) | collective-permute-done | bytes 131104 | tf_op jit(solution)/shard_map/ppermute | solution.py:184
  76.4 3.1 %collective-permute-start.25 = (bf16[4,128,256]{2,1,0:T(8,128)(2,1)S(1)}, bf16[4,128,256]{2,1,0:T(8,128)(2,1)S(1)}, u32[]{:S(2)}, u32[]{:S(2)}) collective-permute-start(bf16[4,128,256]{2,1,0:T(8,128)(2,1)S(1)} %constant_dynamic-update-slice_fusion.4.refs_0_), channel_id=1, source_target_pairs={{0,14},{1,31},{2,8},{3,25},{4,10},{5,27},{6,12},{7,29},{8,22},{9,7... | collective-permute-start | bytes 786440 | tf_op jit(solution)/shard_map/ppermute | solution.py:184
  79.5 5.8 %collective-permute-done.25.refs_3_ = bf16[4,128,256]{2,1,0:T(8,128)(2,1)S(1)} collective-permute-done((bf16[4,128,256]{2,1,0:T(8,128)(2,1)S(1)}, bf16[4,128,256]{2,1,0:T(8,128)(2,1)S(1)}, u32[]{:S(2)}, u32[]{:S(2)}) %collective-permute-start.25) | collective-permute-done | bytes 262176 | tf_op jit(solution)/shard_map/ppermute | solution.py:184
  86.5 1.8 collective-permute-done.24.refs_2_
  90.2 2.1 %site.8 = (f32[128,256]{1,0:T(8,128)S(1)}, f32[8,128]{1,0:T(8,128)S(1)}, bf16[128,256]{1,0:T(8,128)(2,1)S(1)}) custom-call(s32[4]{0:T(128)S(1)} %pad_add_fusion.place_ref, bf16[4,128,256]{2,1,0:T(8,128)(2,1)S(1)} %constant_dynamic-update-slice_fusion.4.refs_0_, bf16[4,128,256]{2,1,0:T(8,128)(2,1)S(1)} %collective-permute-done.23.refs_1_, ...), custom_call_target="tpu_custom_call" | custom-call | tf_op jit(solution)/shard_map/site/pallas_call | solution.py:132
  93.7 2.5 %collective-permute-start.32 = (bf16[2,128,256]{2,1,0:T(8,128)(2,1)S(1)}, bf16[2,128,256]{2,1,0:T(8,128)(2,1)S(1)}, u32[]{:S(2)}, u32[]{:S(2)}) collective-permute-start(bf16[2,128,256]{2,1,0:T(8,128)(2,1)S(1)} %pad_maximum_fusion.3), channel_id=1, source_target_pairs={{0,48},{1,53},{2,50},{3,55},{4,52},{5,49},{6,54},{7,51},{8,56},{9,... | collective-permute-start | bytes 393224 | tf_op jit(solution)/shard_map/ppermute | solution.py:184
  96.2 6.0 %collective-permute-done.31 = bf16[2,128,256]{2,1,0:T(8,128)(2,1)S(1)} collective-permute-done((bf16[2,128,256]{2,1,0:T(8,128)(2,1)S(1)}, bf16[2,128,256]{2,1,0:T(8,128)(2,1)S(1)}, u32[]{:S(2)}, u32[]{:S(2)}) %collective-permute-start.31) | collective-permute-done | bytes 131104 | tf_op jit(solution)/shard_map/ppermute | solution.py:184
  102.2 2.6 %collective-permute-done.32 = bf16[2,128,256]{2,1,0:T(8,128)(2,1)S(1)} collective-permute-done((bf16[2,128,256]{2,1,0:T(8,128)(2,1)S(1)}, bf16[2,128,256]{2,1,0:T(8,128)(2,1)S(1)}, u32[]{:S(2)}, u32[]{:S(2)}) %collective-permute-start.32) | collective-permute-done | bytes 131104 | tf_op jit(solution)/shard_map/ppermute | solution.py:184
  104.8 2.1 %collective-permute-start.35 = (bf16[4,128,256]{2,1,0:T(8,128)(2,1)S(1)}, bf16[4,128,256]{2,1,0:T(8,128)(2,1)S(1)}, u32[]{:S(2)}, u32[]{:S(2)}) collective-permute-start(bf16[4,128,256]{2,1,0:T(8,128)(2,1)S(1)} %constant_dynamic-update-slice_fusion.6.refs_0_), channel_id=1, source_target_pairs={{0,14},{1,31},{2,8},{3,25},{4,10},{5,27},{6,12},{7,29},{8,22},{9,7... | collective-permute-start | bytes 786440 | tf_op jit(solution)/shard_map/ppermute | solution.py:184
  108.5 5.3 %collective-permute-done.35.refs_3_ = bf16[4,128,256]{2,1,0:T(8,128)(2,1)S(1)} collective-permute-done((bf16[4,128,256]{2,1,0:T(8,128)(2,1)S(1)}, bf16[4,128,256]{2,1,0:T(8,128)(2,1)S(1)}, u32[]{:S(2)}, u32[]{:S(2)}) %collective-permute-start.35) | collective-permute-done | bytes 262176 | tf_op jit(solution)/shard_map/ppermute | solution.py:184
  113.8 1.4 collective-permute-start.39
  118.4 2.1 %site.9 = (f32[128,256]{1,0:T(8,128)S(1)}, f32[8,128]{1,0:T(8,128)S(1)}, bf16[128,256]{1,0:T(8,128)(2,1)S(1)}) custom-call(s32[4]{0:T(128)S(1)} %pad_add_fusion.place_ref, bf16[4,128,256]{2,1,0:T(8,128)(2,1)S(1)} %constant_dynamic-update-slice_fusion.6.refs_0_, bf16[4,128,256]{2,1,0:T(8,128)(2,1)S(1)} %collective-permute-done.33.refs_1_, ...), custom_call_target="tpu_custom_call" | custom-call | tf_op jit(solution)/shard_map/site/pallas_call | solution.py:132
  121.8 1.8 collective-permute-start.42
  123.6 6.4 %collective-permute-done.41 = bf16[2,128,256]{2,1,0:T(8,128)(2,1)S(1)} collective-permute-done((bf16[2,128,256]{2,1,0:T(8,128)(2,1)S(1)}, bf16[2,128,256]{2,1,0:T(8,128)(2,1)S(1)}, u32[]{:S(2)}, u32[]{:S(2)}) %collective-permute-start.41) | collective-permute-done | bytes 131104 | tf_op jit(solution)/shard_map/ppermute | solution.py:184
  130.0 2.9 %collective-permute-done.42 = bf16[2,128,256]{2,1,0:T(8,128)(2,1)S(1)} collective-permute-done((bf16[2,128,256]{2,1,0:T(8,128)(2,1)S(1)}, bf16[2,128,256]{2,1,0:T(8,128)(2,1)S(1)}, u32[]{:S(2)}, u32[]{:S(2)}) %collective-permute-start.42) | collective-permute-done | bytes 131104 | tf_op jit(solution)/shard_map/ppermute | solution.py:184
  132.9 3.1 %collective-permute-start.45 = (bf16[4,128,256]{2,1,0:T(8,128)(2,1)S(1)}, bf16[4,128,256]{2,1,0:T(8,128)(2,1)S(1)}, u32[]{:S(2)}, u32[]{:S(2)}) collective-permute-start(bf16[4,128,256]{2,1,0:T(8,128)(2,1)S(1)} %constant_dynamic-update-slice_fusion.8.refs_0_), channel_id=1, source_target_pairs={{0,14},{1,31},{2,8},{3,25},{4,10},{5,27},{6,12},{7,29},{8,22},{9,7... | collective-permute-start | bytes 786440 | tf_op jit(solution)/shard_map/ppermute | solution.py:184
  136.4 5.5 %collective-permute-done.45.refs_3_ = bf16[4,128,256]{2,1,0:T(8,128)(2,1)S(1)} collective-permute-done((bf16[4,128,256]{2,1,0:T(8,128)(2,1)S(1)}, bf16[4,128,256]{2,1,0:T(8,128)(2,1)S(1)}, u32[]{:S(2)}, u32[]{:S(2)}) %collective-permute-start.45) | collective-permute-done | bytes 262176 | tf_op jit(solution)/shard_map/ppermute | solution.py:184
  141.9 1.3 collective-permute-start.49
  146.0 2.1 %site.10 = (f32[128,256]{1,0:T(8,128)S(1)}, f32[8,128]{1,0:T(8,128)S(1)}, bf16[128,256]{1,0:T(8,128)(2,1)S(1)}) custom-call(s32[4]{0:T(128)S(1)} %pad_add_fusion.place_ref, bf16[4,128,256]{2,1,0:T(8,128)(2,1)S(1)} %constant_dynamic-update-slice_fusion.8.refs_0_, bf16[4,128,256]{2,1,0:T(8,128)(2,1)S(1)} %collective-permute-done.43.refs_1_, ...), custom_call_target="tpu_custom_call" | custom-call | tf_op jit(solution)/shard_map/site/pallas_call | solution.py:132
  149.5 2.7 %collective-permute-start.52 = (bf16[2,128,256]{2,1,0:T(8,128)(2,1)S(1)}, bf16[2,128,256]{2,1,0:T(8,128)(2,1)S(1)}, u32[]{:S(2)}, u32[]{:S(2)}) collective-permute-start(bf16[2,128,256]{2,1,0:T(8,128)(2,1)S(1)} %pad_maximum_fusion.5), channel_id=1, source_target_pairs={{0,48},{1,53},{2,50},{3,55},{4,52},{5,49},{6,54},{7,51},{8,56},{9,... | collective-permute-start | bytes 393224 | tf_op jit(solution)/shard_map/ppermute | solution.py:184
  152.2 6.4 %collective-permute-done.51 = bf16[2,128,256]{2,1,0:T(8,128)(2,1)S(1)} collective-permute-done((bf16[2,128,256]{2,1,0:T(8,128)(2,1)S(1)}, bf16[2,128,256]{2,1,0:T(8,128)(2,1)S(1)}, u32[]{:S(2)}, u32[]{:S(2)}) %collective-permute-start.51) | collective-permute-done | bytes 131104 | tf_op jit(solution)/shard_map/ppermute | solution.py:184
  158.6 2.4 %collective-permute-done.52 = bf16[2,128,256]{2,1,0:T(8,128)(2,1)S(1)} collective-permute-done((bf16[2,128,256]{2,1,0:T(8,128)(2,1)S(1)}, bf16[2,128,256]{2,1,0:T(8,128)(2,1)S(1)}, u32[]{:S(2)}, u32[]{:S(2)}) %collective-permute-start.52) | collective-permute-done | bytes 131104 | tf_op jit(solution)/shard_map/ppermute | solution.py:184
  161.0 2.4 %collective-permute-start.55 = (bf16[4,128,256]{2,1,0:T(8,128)(2,1)S(1)}, bf16[4,128,256]{2,1,0:T(8,128)(2,1)S(1)}, u32[]{:S(2)}, u32[]{:S(2)}) collective-permute-start(bf16[4,128,256]{2,1,0:T(8,128)(2,1)S(1)} %constant_dynamic-update-slice_fusion.10.refs_0_), channel_id=1, source_target_pairs={{0,14},{1,31},{2,8},{3,25},{4,10},{5,27},{6,12},{7,29},{8,22},{9,7... | collective-permute-start | bytes 786440 | tf_op jit(solution)/shard_map/ppermute | solution.py:184
  164.5 5.5 %collective-permute-done.55.refs_3_ = bf16[4,128,256]{2,1,0:T(8,128)(2,1)S(1)} collective-permute-done((bf16[4,128,256]{2,1,0:T(8,128)(2,1)S(1)}, bf16[4,128,256]{2,1,0:T(8,128)(2,1)S(1)}, u32[]{:S(2)}, u32[]{:S(2)}) %collective-permute-start.55) | collective-permute-done | bytes 262176 | tf_op jit(solution)/shard_map/ppermute | solution.py:184
  170.0 1.5 collective-permute-start.59
  171.5 1.3 collective-permute-done.54.refs_2_
  174.8 1.9 %site.11 = (f32[128,256]{1,0:T(8,128)S(1)}, f32[32,3,128]{2,1,0:T(4,128)S(1)}) custom-call(s32[4]{0:T(128)S(1)} %pad_add_fusion.place_ref, bf16[4,128,256]{2,1,0:T(8,128)(2,1)S(1)} %constant_dynamic-update-slice_fusion.10.refs_0_, bf16[4,128,256]{2,1,0:T(8,128)(2,1)S(1)} %collective-permute-done.53.refs_1_, ...), custom_call_target="tpu_custom_call" | custom-call | tf_op jit(solution)/shard_map/site/pallas_call | solution.py:132
  176.7 11.1 %all_to_all.5.maxima_ref = f32[32,3,128]{2,1,0:T(4,128)S(1)} all-to-all(f32[32,3,128]{2,1,0:T(4,128)S(1)} %get-tuple-element.43), channel_id=1, replica_groups=mesh['segment'=4,'col'=32] {'col'}, dimensions={0} | all-to-all | bytes 98304 | tf_op jit(solution)/shard_map/all_to_all | solution.py:231
  187.8 1.8 finish.1
  (105 shorter events, 30.2 us)
Async XLA Ops:
  0.6 2.8 %collective-permute-start = (bf16[384,256]{1,0:T(8,128)(2,1)}, bf16[384,256]{1,0:T(8,128)(2,1)S(1)}, u32[]{:S(2)}, u32[]{:S(2)}) collective-permute-start(bf16[384,256]{1,0:T(8,128)(2,1)} %refs_10_.9), channel_id=1, source_target_pairs={{0,1},{1,0},{2,3},{3,2},{4,5},{5,4},{6,7},{7,6},{8,9},{9,8},{10,11... | collective-permute-start | bytes 589832 | tf_op jit(solution)/shard_map/ppermute | solution.py:184
  3.4 8.3 %collective-permute-start.1 = (bf16[2,128,256]{2,1,0:T(8,128)(2,1)S(1)}, bf16[2,128,256]{2,1,0:T(8,128)(2,1)S(1)}, u32[]{:S(2)}, u32[]{:S(2)}) collective-permute-start(bf16[2,128,256]{2,1,0:T(8,128)(2,1)S(1)} %pad_maximum_fusion), channel_id=1, source_target_pairs={{0,32},{1,37},{2,34},{3,39},{4,36},{5,33},{6,38},{7,35},{8,40},{9,... | collective-permute-start | bytes 393224 | tf_op jit(solution)/shard_map/ppermute | solution.py:184
  7.4 11.2 %collective-permute-start.2 = (bf16[2,128,256]{2,1,0:T(8,128)(2,1)S(1)}, bf16[2,128,256]{2,1,0:T(8,128)(2,1)S(1)}, u32[]{:S(2)}, u32[]{:S(2)}) collective-permute-start(bf16[2,128,256]{2,1,0:T(8,128)(2,1)S(1)} %pad_maximum_fusion), channel_id=1, source_target_pairs={{0,48},{1,53},{2,50},{3,55},{4,52},{5,49},{6,54},{7,51},{8,56},{9,... | collective-permute-start | bytes 393224 | tf_op jit(solution)/shard_map/ppermute | solution.py:184
  18.6 8.6 %collective-permute-start.5 = (bf16[4,128,256]{2,1,0:T(8,128)(2,1)S(1)}, bf16[4,128,256]{2,1,0:T(8,128)(2,1)S(1)}, u32[]{:S(2)}, u32[]{:S(2)}) collective-permute-start(bf16[4,128,256]{2,1,0:T(8,128)(2,1)S(1)} %constant_dynamic-update-slice_fusion.after_ref.refs_0_), channel_id=1, source_target_pairs={{0,14},{1,31},{2,8},{3,25},{4,10},{5,27},{6,12},{7,29},{8,22},{9,7... | collective-permute-start | bytes 786440 | tf_op jit(solution)/shard_map/ppermute | solution.py:184
  21.7 8.9 %collective-permute-start.4 = (bf16[4,128,256]{2,1,0:T(8,128)(2,1)S(1)}, bf16[4,128,256]{2,1,0:T(8,128)(2,1)S(1)}, u32[]{:S(2)}, u32[]{:S(2)}) collective-permute-start(bf16[4,128,256]{2,1,0:T(8,128)(2,1)S(1)} %constant_dynamic-update-slice_fusion.after_ref.refs_0_), channel_id=1, source_target_pairs={{0,2},{1,3},{2,4},{3,5},{4,6},{5,7},{6,0},{7,1},{8,10},{9,11},{10,... | collective-permute-start | bytes 786440 | tf_op jit(solution)/shard_map/ppermute | solution.py:184
  22.4 8.2 %collective-permute-start.3 = (bf16[4,128,256]{2,1,0:T(8,128)(2,1)S(1)}, bf16[4,128,256]{2,1,0:T(8,128)(2,1)S(1)}, u32[]{:S(2)}, u32[]{:S(2)}) collective-permute-start(bf16[4,128,256]{2,1,0:T(8,128)(2,1)S(1)} %constant_dynamic-update-slice_fusion.after_ref.refs_0_), channel_id=1, source_target_pairs={{0,8},{1,25},{2,10},{3,27},{4,12},{5,29},{6,14},{7,31},{8,16},{9,1... | collective-permute-start | bytes 786440 | tf_op jit(solution)/shard_map/ppermute | solution.py:184
  30.6 1.6 collective-permute-start.6
  31.1 1.8 collective-permute-start.8
  31.5 1.8 collective-permute-start.9
  36.7 8.9 %collective-permute-start.11 = (bf16[2,128,256]{2,1,0:T(8,128)(2,1)S(1)}, bf16[2,128,256]{2,1,0:T(8,128)(2,1)S(1)}, u32[]{:S(2)}, u32[]{:S(2)}) collective-permute-start(bf16[2,128,256]{2,1,0:T(8,128)(2,1)S(1)} %pad_maximum_fusion.1), channel_id=1, source_target_pairs={{0,32},{1,37},{2,34},{3,39},{4,36},{5,33},{6,38},{7,35},{8,40},{9,... | collective-permute-start | bytes 393224 | tf_op jit(solution)/shard_map/ppermute | solution.py:184
  37.1 10.6 %collective-permute-start.12 = (bf16[2,128,256]{2,1,0:T(8,128)(2,1)S(1)}, bf16[2,128,256]{2,1,0:T(8,128)(2,1)S(1)}, u32[]{:S(2)}, u32[]{:S(2)}) collective-permute-start(bf16[2,128,256]{2,1,0:T(8,128)(2,1)S(1)} %pad_maximum_fusion.1), channel_id=1, source_target_pairs={{0,48},{1,53},{2,50},{3,55},{4,52},{5,49},{6,54},{7,51},{8,56},{9,... | collective-permute-start | bytes 393224 | tf_op jit(solution)/shard_map/ppermute | solution.py:184
  47.7 8.3 %collective-permute-start.15 = (bf16[4,128,256]{2,1,0:T(8,128)(2,1)S(1)}, bf16[4,128,256]{2,1,0:T(8,128)(2,1)S(1)}, u32[]{:S(2)}, u32[]{:S(2)}) collective-permute-start(bf16[4,128,256]{2,1,0:T(8,128)(2,1)S(1)} %constant_dynamic-update-slice_fusion.2.refs_0_), channel_id=1, source_target_pairs={{0,14},{1,31},{2,8},{3,25},{4,10},{5,27},{6,12},{7,29},{8,22},{9,7... | collective-permute-start | bytes 786440 | tf_op jit(solution)/shard_map/ppermute | solution.py:184
  50.2 8.4 %collective-permute-start.14 = (bf16[4,128,256]{2,1,0:T(8,128)(2,1)S(1)}, bf16[4,128,256]{2,1,0:T(8,128)(2,1)S(1)}, u32[]{:S(2)}, u32[]{:S(2)}) collective-permute-start(bf16[4,128,256]{2,1,0:T(8,128)(2,1)S(1)} %constant_dynamic-update-slice_fusion.2.refs_0_), channel_id=1, source_target_pairs={{0,2},{1,3},{2,4},{3,5},{4,6},{5,7},{6,0},{7,1},{8,10},{9,11},{10,... | collective-permute-start | bytes 786440 | tf_op jit(solution)/shard_map/ppermute | solution.py:184
  50.2 9.9 %collective-permute-start.13 = (bf16[4,128,256]{2,1,0:T(8,128)(2,1)S(1)}, bf16[4,128,256]{2,1,0:T(8,128)(2,1)S(1)}, u32[]{:S(2)}, u32[]{:S(2)}) collective-permute-start(bf16[4,128,256]{2,1,0:T(8,128)(2,1)S(1)} %constant_dynamic-update-slice_fusion.2.refs_0_), channel_id=1, source_target_pairs={{0,8},{1,25},{2,10},{3,27},{4,12},{5,29},{6,14},{7,31},{8,16},{9,1... | collective-permute-start | bytes 786440 | tf_op jit(solution)/shard_map/ppermute | solution.py:184
  52.2 7.9 %collective-permute-start.16 = (bf16[4,128,256]{2,1,0:T(8,128)(2,1)S(1)}, bf16[4,128,256]{2,1,0:T(8,128)(2,1)S(1)}, u32[]{:S(2)}, u32[]{:S(2)}) collective-permute-start(bf16[4,128,256]{2,1,0:T(8,128)(2,1)S(1)} %constant_dynamic-update-slice_fusion.2.refs_0_), channel_id=1, source_target_pairs={{0,1},{1,0},{2,3},{3,2},{4,5},{5,4},{6,7},{7,6},{8,9},{9,8},{10,11... | collective-permute-start | bytes 786440 | tf_op jit(solution)/shard_map/ppermute | solution.py:184
  56.0 4.1 %collective-permute-start.19 = (bf16[4,128,256]{2,1,0:T(8,128)(2,1)S(1)}, bf16[4,128,256]{2,1,0:T(8,128)(2,1)S(1)}, u32[]{:S(2)}, u32[]{:S(2)}) collective-permute-start(bf16[4,128,256]{2,1,0:T(8,128)(2,1)S(1)} %collective-permute-done.15.refs_3_), channel_id=1, source_target_pairs={{0,1},{1,0},{2,3},{3,2},{4,5},{5,4},{6,7},{7,6},{8,9},{9,8},{10,11... | collective-permute-start | bytes 786440 | tf_op jit(solution)/shard_map/ppermute | solution.py:184
  58.5 2.7 %collective-permute-start.18 = (bf16[4,128,256]{2,1,0:T(8,128)(2,1)S(1)}, bf16[4,128,256]{2,1,0:T(8,128)(2,1)S(1)}, u32[]{:S(2)}, u32[]{:S(2)}) collective-permute-start(bf16[4,128,256]{2,1,0:T(8,128)(2,1)S(1)} %collective-permute-done.14.refs_2_), channel_id=1, source_target_pairs={{0,1},{1,0},{2,3},{3,2},{4,5},{5,4},{6,7},{7,6},{8,9},{9,8},{10,11... | collective-permute-start | bytes 786440 | tf_op jit(solution)/shard_map/ppermute | solution.py:184
  65.1 8.9 %collective-permute-start.21 = (bf16[2,128,256]{2,1,0:T(8,128)(2,1)S(1)}, bf16[2,128,256]{2,1,0:T(8,128)(2,1)S(1)}, u32[]{:S(2)}, u32[]{:S(2)}) collective-permute-start(bf16[2,128,256]{2,1,0:T(8,128)(2,1)S(1)} %pad_maximum_fusion.2), channel_id=1, source_target_pairs={{0,32},{1,37},{2,34},{3,39},{4,36},{5,33},{6,38},{7,35},{8,40},{9,... | collective-permute-start | bytes 393224 | tf_op jit(solution)/shard_map/ppermute | solution.py:184
  65.1 11.2 %collective-permute-start.22 = (bf16[2,128,256]{2,1,0:T(8,128)(2,1)S(1)}, bf16[2,128,256]{2,1,0:T(8,128)(2,1)S(1)}, u32[]{:S(2)}, u32[]{:S(2)}) collective-permute-start(bf16[2,128,256]{2,1,0:T(8,128)(2,1)S(1)} %pad_maximum_fusion.2), channel_id=1, source_target_pairs={{0,48},{1,53},{2,50},{3,55},{4,52},{5,49},{6,54},{7,51},{8,56},{9,... | collective-permute-start | bytes 393224 | tf_op jit(solution)/shard_map/ppermute | solution.py:184
  76.4 8.9 %collective-permute-start.25 = (bf16[4,128,256]{2,1,0:T(8,128)(2,1)S(1)}, bf16[4,128,256]{2,1,0:T(8,128)(2,1)S(1)}, u32[]{:S(2)}, u32[]{:S(2)}) collective-permute-start(bf16[4,128,256]{2,1,0:T(8,128)(2,1)S(1)} %constant_dynamic-update-slice_fusion.4.refs_0_), channel_id=1, source_target_pairs={{0,14},{1,31},{2,8},{3,25},{4,10},{5,27},{6,12},{7,29},{8,22},{9,7... | collective-permute-start | bytes 786440 | tf_op jit(solution)/shard_map/ppermute | solution.py:184
  79.5 8.8 %collective-permute-start.24 = (bf16[4,128,256]{2,1,0:T(8,128)(2,1)S(1)}, bf16[4,128,256]{2,1,0:T(8,128)(2,1)S(1)}, u32[]{:S(2)}, u32[]{:S(2)}) collective-permute-start(bf16[4,128,256]{2,1,0:T(8,128)(2,1)S(1)} %constant_dynamic-update-slice_fusion.4.refs_0_), channel_id=1, source_target_pairs={{0,2},{1,3},{2,4},{3,5},{4,6},{5,7},{6,0},{7,1},{8,10},{9,11},{10,... | collective-permute-start | bytes 786440 | tf_op jit(solution)/shard_map/ppermute | solution.py:184
  79.5 9.2 %collective-permute-start.23 = (bf16[4,128,256]{2,1,0:T(8,128)(2,1)S(1)}, bf16[4,128,256]{2,1,0:T(8,128)(2,1)S(1)}, u32[]{:S(2)}, u32[]{:S(2)}) collective-permute-start(bf16[4,128,256]{2,1,0:T(8,128)(2,1)S(1)} %constant_dynamic-update-slice_fusion.4.refs_0_), channel_id=1, source_target_pairs={{0,8},{1,25},{2,10},{3,27},{4,12},{5,29},{6,14},{7,31},{8,16},{9,1... | collective-permute-start | bytes 786440 | tf_op jit(solution)/shard_map/ppermute | solution.py:184
  79.5 9.3 %collective-permute-start.26 = (bf16[4,128,256]{2,1,0:T(8,128)(2,1)S(1)}, bf16[4,128,256]{2,1,0:T(8,128)(2,1)S(1)}, u32[]{:S(2)}, u32[]{:S(2)}) collective-permute-start(bf16[4,128,256]{2,1,0:T(8,128)(2,1)S(1)} %constant_dynamic-update-slice_fusion.4.refs_0_), channel_id=1, source_target_pairs={{0,1},{1,0},{2,3},{3,2},{4,5},{5,4},{6,7},{7,6},{8,9},{9,8},{10,11... | collective-permute-start | bytes 786440 | tf_op jit(solution)/shard_map/ppermute | solution.py:184
  85.3 3.5 %collective-permute-start.29 = (bf16[4,128,256]{2,1,0:T(8,128)(2,1)S(1)}, bf16[4,128,256]{2,1,0:T(8,128)(2,1)S(1)}, u32[]{:S(2)}, u32[]{:S(2)}) collective-permute-start(bf16[4,128,256]{2,1,0:T(8,128)(2,1)S(1)} %collective-permute-done.25.refs_3_), channel_id=1, source_target_pairs={{0,1},{1,0},{2,3},{3,2},{4,5},{5,4},{6,7},{7,6},{8,9},{9,8},{10,11... | collective-permute-start | bytes 786440 | tf_op jit(solution)/shard_map/ppermute | solution.py:184
  93.6 8.6 %collective-permute-start.31 = (bf16[2,128,256]{2,1,0:T(8,128)(2,1)S(1)}, bf16[2,128,256]{2,1,0:T(8,128)(2,1)S(1)}, u32[]{:S(2)}, u32[]{:S(2)}) collective-permute-start(bf16[2,128,256]{2,1,0:T(8,128)(2,1)S(1)} %pad_maximum_fusion.3), channel_id=1, source_target_pairs={{0,32},{1,37},{2,34},{3,39},{4,36},{5,33},{6,38},{7,35},{8,40},{9,... | collective-permute-start | bytes 393224 | tf_op jit(solution)/shard_map/ppermute | solution.py:184
  93.7 11.1 %collective-permute-start.32 = (bf16[2,128,256]{2,1,0:T(8,128)(2,1)S(1)}, bf16[2,128,256]{2,1,0:T(8,128)(2,1)S(1)}, u32[]{:S(2)}, u32[]{:S(2)}) collective-permute-start(bf16[2,128,256]{2,1,0:T(8,128)(2,1)S(1)} %pad_maximum_fusion.3), channel_id=1, source_target_pairs={{0,48},{1,53},{2,50},{3,55},{4,52},{5,49},{6,54},{7,51},{8,56},{9,... | collective-permute-start | bytes 393224 | tf_op jit(solution)/shard_map/ppermute | solution.py:184
  104.8 9.0 %collective-permute-start.35 = (bf16[4,128,256]{2,1,0:T(8,128)(2,1)S(1)}, bf16[4,128,256]{2,1,0:T(8,128)(2,1)S(1)}, u32[]{:S(2)}, u32[]{:S(2)}) collective-permute-start(bf16[4,128,256]{2,1,0:T(8,128)(2,1)S(1)} %constant_dynamic-update-slice_fusion.6.refs_0_), channel_id=1, source_target_pairs={{0,14},{1,31},{2,8},{3,25},{4,10},{5,27},{6,12},{7,29},{8,22},{9,7... | collective-permute-start | bytes 786440 | tf_op jit(solution)/shard_map/ppermute | solution.py:184
  106.9 8.8 %collective-permute-start.34 = (bf16[4,128,256]{2,1,0:T(8,128)(2,1)S(1)}, bf16[4,128,256]{2,1,0:T(8,128)(2,1)S(1)}, u32[]{:S(2)}, u32[]{:S(2)}) collective-permute-start(bf16[4,128,256]{2,1,0:T(8,128)(2,1)S(1)} %constant_dynamic-update-slice_fusion.6.refs_0_), channel_id=1, source_target_pairs={{0,2},{1,3},{2,4},{3,5},{4,6},{5,7},{6,0},{7,1},{8,10},{9,11},{10,... | collective-permute-start | bytes 786440 | tf_op jit(solution)/shard_map/ppermute | solution.py:184
  107.2 9.6 %collective-permute-start.33 = (bf16[4,128,256]{2,1,0:T(8,128)(2,1)S(1)}, bf16[4,128,256]{2,1,0:T(8,128)(2,1)S(1)}, u32[]{:S(2)}, u32[]{:S(2)}) collective-permute-start(bf16[4,128,256]{2,1,0:T(8,128)(2,1)S(1)} %constant_dynamic-update-slice_fusion.6.refs_0_), channel_id=1, source_target_pairs={{0,8},{1,25},{2,10},{3,27},{4,12},{5,29},{6,14},{7,31},{8,16},{9,1... | collective-permute-start | bytes 786440 | tf_op jit(solution)/shard_map/ppermute | solution.py:184
  108.2 8.7 %collective-permute-start.36 = (bf16[4,128,256]{2,1,0:T(8,128)(2,1)S(1)}, bf16[4,128,256]{2,1,0:T(8,128)(2,1)S(1)}, u32[]{:S(2)}, u32[]{:S(2)}) collective-permute-start(bf16[4,128,256]{2,1,0:T(8,128)(2,1)S(1)} %constant_dynamic-update-slice_fusion.6.refs_0_), channel_id=1, source_target_pairs={{0,1},{1,0},{2,3},{3,2},{4,5},{5,4},{6,7},{7,6},{8,9},{9,8},{10,11... | collective-permute-start | bytes 786440 | tf_op jit(solution)/shard_map/ppermute | solution.py:184
  113.8 3.0 %collective-permute-start.39 = (bf16[4,128,256]{2,1,0:T(8,128)(2,1)S(1)}, bf16[4,128,256]{2,1,0:T(8,128)(2,1)S(1)}, u32[]{:S(2)}, u32[]{:S(2)}) collective-permute-start(bf16[4,128,256]{2,1,0:T(8,128)(2,1)S(1)} %collective-permute-done.35.refs_3_), channel_id=1, source_target_pairs={{0,1},{1,0},{2,3},{3,2},{4,5},{5,4},{6,7},{7,6},{8,9},{9,8},{10,11... | collective-permute-start | bytes 786440 | tf_op jit(solution)/shard_map/ppermute | solution.py:184
  115.6 2.3 %collective-permute-start.38 = (bf16[4,128,256]{2,1,0:T(8,128)(2,1)S(1)}, bf16[4,128,256]{2,1,0:T(8,128)(2,1)S(1)}, u32[]{:S(2)}, u32[]{:S(2)}) collective-permute-start(bf16[4,128,256]{2,1,0:T(8,128)(2,1)S(1)} %collective-permute-done.34.refs_2_), channel_id=1, source_target_pairs={{0,1},{1,0},{2,3},{3,2},{4,5},{5,4},{6,7},{7,6},{8,9},{9,8},{10,11... | collective-permute-start | bytes 786440 | tf_op jit(solution)/shard_map/ppermute | solution.py:184
  121.8 8.2 %collective-permute-start.41 = (bf16[2,128,256]{2,1,0:T(8,128)(2,1)S(1)}, bf16[2,128,256]{2,1,0:T(8,128)(2,1)S(1)}, u32[]{:S(2)}, u32[]{:S(2)}) collective-permute-start(bf16[2,128,256]{2,1,0:T(8,128)(2,1)S(1)} %pad_maximum_fusion.4), channel_id=1, source_target_pairs={{0,32},{1,37},{2,34},{3,39},{4,36},{5,33},{6,38},{7,35},{8,40},{9,... | collective-permute-start | bytes 393224 | tf_op jit(solution)/shard_map/ppermute | solution.py:184
  121.8 11.1 %collective-permute-start.42 = (bf16[2,128,256]{2,1,0:T(8,128)(2,1)S(1)}, bf16[2,128,256]{2,1,0:T(8,128)(2,1)S(1)}, u32[]{:S(2)}, u32[]{:S(2)}) collective-permute-start(bf16[2,128,256]{2,1,0:T(8,128)(2,1)S(1)} %pad_maximum_fusion.4), channel_id=1, source_target_pairs={{0,48},{1,53},{2,50},{3,55},{4,52},{5,49},{6,54},{7,51},{8,56},{9,... | collective-permute-start | bytes 393224 | tf_op jit(solution)/shard_map/ppermute | solution.py:184
  132.9 9.0 %collective-permute-start.45 = (bf16[4,128,256]{2,1,0:T(8,128)(2,1)S(1)}, bf16[4,128,256]{2,1,0:T(8,128)(2,1)S(1)}, u32[]{:S(2)}, u32[]{:S(2)}) collective-permute-start(bf16[4,128,256]{2,1,0:T(8,128)(2,1)S(1)} %constant_dynamic-update-slice_fusion.8.refs_0_), channel_id=1, source_target_pairs={{0,14},{1,31},{2,8},{3,25},{4,10},{5,27},{6,12},{7,29},{8,22},{9,7... | collective-permute-start | bytes 786440 | tf_op jit(solution)/shard_map/ppermute | solution.py:184
  136.0 8.1 %collective-permute-start.44 = (bf16[4,128,256]{2,1,0:T(8,128)(2,1)S(1)}, bf16[4,128,256]{2,1,0:T(8,128)(2,1)S(1)}, u32[]{:S(2)}, u32[]{:S(2)}) collective-permute-start(bf16[4,128,256]{2,1,0:T(8,128)(2,1)S(1)} %constant_dynamic-update-slice_fusion.8.refs_0_), channel_id=1, source_target_pairs={{0,2},{1,3},{2,4},{3,5},{4,6},{5,7},{6,0},{7,1},{8,10},{9,11},{10,... | collective-permute-start | bytes 786440 | tf_op jit(solution)/shard_map/ppermute | solution.py:184
  136.0 8.1 %collective-permute-start.43 = (bf16[4,128,256]{2,1,0:T(8,128)(2,1)S(1)}, bf16[4,128,256]{2,1,0:T(8,128)(2,1)S(1)}, u32[]{:S(2)}, u32[]{:S(2)}) collective-permute-start(bf16[4,128,256]{2,1,0:T(8,128)(2,1)S(1)} %constant_dynamic-update-slice_fusion.8.refs_0_), channel_id=1, source_target_pairs={{0,8},{1,25},{2,10},{3,27},{4,12},{5,29},{6,14},{7,31},{8,16},{9,1... | collective-permute-start | bytes 786440 | tf_op jit(solution)/shard_map/ppermute | solution.py:184
  136.4 8.2 %collective-permute-start.46 = (bf16[4,128,256]{2,1,0:T(8,128)(2,1)S(1)}, bf16[4,128,256]{2,1,0:T(8,128)(2,1)S(1)}, u32[]{:S(2)}, u32[]{:S(2)}) collective-permute-start(bf16[4,128,256]{2,1,0:T(8,128)(2,1)S(1)} %constant_dynamic-update-slice_fusion.8.refs_0_), channel_id=1, source_target_pairs={{0,1},{1,0},{2,3},{3,2},{4,5},{5,4},{6,7},{7,6},{8,9},{9,8},{10,11... | collective-permute-start | bytes 786440 | tf_op jit(solution)/shard_map/ppermute | solution.py:184
  141.9 2.8 %collective-permute-start.49 = (bf16[4,128,256]{2,1,0:T(8,128)(2,1)S(1)}, bf16[4,128,256]{2,1,0:T(8,128)(2,1)S(1)}, u32[]{:S(2)}, u32[]{:S(2)}) collective-permute-start(bf16[4,128,256]{2,1,0:T(8,128)(2,1)S(1)} %collective-permute-done.45.refs_3_), channel_id=1, source_target_pairs={{0,1},{1,0},{2,3},{3,2},{4,5},{5,4},{6,7},{7,6},{8,9},{9,8},{10,11... | collective-permute-start | bytes 786440 | tf_op jit(solution)/shard_map/ppermute | solution.py:184
  144.1 1.9 %collective-permute-start.47 = (bf16[4,128,256]{2,1,0:T(8,128)(2,1)S(1)}, bf16[4,128,256]{2,1,0:T(8,128)(2,1)S(1)}, u32[]{:S(2)}, u32[]{:S(2)}) collective-permute-start(bf16[4,128,256]{2,1,0:T(8,128)(2,1)S(1)} %collective-permute-done.43.refs_1_), channel_id=1, source_target_pairs={{0,1},{1,0},{2,3},{3,2},{4,5},{5,4},{6,7},{7,6},{8,9},{9,8},{10,11... | collective-permute-start | bytes 786440 | tf_op jit(solution)/shard_map/ppermute | solution.py:184
  149.4 9.2 %collective-permute-start.51 = (bf16[2,128,256]{2,1,0:T(8,128)(2,1)S(1)}, bf16[2,128,256]{2,1,0:T(8,128)(2,1)S(1)}, u32[]{:S(2)}, u32[]{:S(2)}) collective-permute-start(bf16[2,128,256]{2,1,0:T(8,128)(2,1)S(1)} %pad_maximum_fusion.5), channel_id=1, source_target_pairs={{0,32},{1,37},{2,34},{3,39},{4,36},{5,33},{6,38},{7,35},{8,40},{9,... | collective-permute-start | bytes 393224 | tf_op jit(solution)/shard_map/ppermute | solution.py:184
  149.5 11.5 %collective-permute-start.52 = (bf16[2,128,256]{2,1,0:T(8,128)(2,1)S(1)}, bf16[2,128,256]{2,1,0:T(8,128)(2,1)S(1)}, u32[]{:S(2)}, u32[]{:S(2)}) collective-permute-start(bf16[2,128,256]{2,1,0:T(8,128)(2,1)S(1)} %pad_maximum_fusion.5), channel_id=1, source_target_pairs={{0,48},{1,53},{2,50},{3,55},{4,52},{5,49},{6,54},{7,51},{8,56},{9,... | collective-permute-start | bytes 393224 | tf_op jit(solution)/shard_map/ppermute | solution.py:184
  161.0 9.0 %collective-permute-start.55 = (bf16[4,128,256]{2,1,0:T(8,128)(2,1)S(1)}, bf16[4,128,256]{2,1,0:T(8,128)(2,1)S(1)}, u32[]{:S(2)}, u32[]{:S(2)}) collective-permute-start(bf16[4,128,256]{2,1,0:T(8,128)(2,1)S(1)} %constant_dynamic-update-slice_fusion.10.refs_0_), channel_id=1, source_target_pairs={{0,14},{1,31},{2,8},{3,25},{4,10},{5,27},{6,12},{7,29},{8,22},{9,7... | collective-permute-start | bytes 786440 | tf_op jit(solution)/shard_map/ppermute | solution.py:184
  163.4 9.4 %collective-permute-start.54 = (bf16[4,128,256]{2,1,0:T(8,128)(2,1)S(1)}, bf16[4,128,256]{2,1,0:T(8,128)(2,1)S(1)}, u32[]{:S(2)}, u32[]{:S(2)}) collective-permute-start(bf16[4,128,256]{2,1,0:T(8,128)(2,1)S(1)} %constant_dynamic-update-slice_fusion.10.refs_0_), channel_id=1, source_target_pairs={{0,2},{1,3},{2,4},{3,5},{4,6},{5,7},{6,0},{7,1},{8,10},{9,11},{10,... | collective-permute-start | bytes 786440 | tf_op jit(solution)/shard_map/ppermute | solution.py:184
  163.4 9.8 %collective-permute-start.53 = (bf16[4,128,256]{2,1,0:T(8,128)(2,1)S(1)}, bf16[4,128,256]{2,1,0:T(8,128)(2,1)S(1)}, u32[]{:S(2)}, u32[]{:S(2)}) collective-permute-start(bf16[4,128,256]{2,1,0:T(8,128)(2,1)S(1)} %constant_dynamic-update-slice_fusion.10.refs_0_), channel_id=1, source_target_pairs={{0,8},{1,25},{2,10},{3,27},{4,12},{5,29},{6,14},{7,31},{8,16},{9,1... | collective-permute-start | bytes 786440 | tf_op jit(solution)/shard_map/ppermute | solution.py:184
  164.5 8.9 %collective-permute-start.56 = (bf16[4,128,256]{2,1,0:T(8,128)(2,1)S(1)}, bf16[4,128,256]{2,1,0:T(8,128)(2,1)S(1)}, u32[]{:S(2)}, u32[]{:S(2)}) collective-permute-start(bf16[4,128,256]{2,1,0:T(8,128)(2,1)S(1)} %constant_dynamic-update-slice_fusion.10.refs_0_), channel_id=1, source_target_pairs={{0,1},{1,0},{2,3},{3,2},{4,5},{5,4},{6,7},{7,6},{8,9},{9,8},{10,11... | collective-permute-start | bytes 786440 | tf_op jit(solution)/shard_map/ppermute | solution.py:184
  170.0 3.4 %collective-permute-start.59 = (bf16[4,128,256]{2,1,0:T(8,128)(2,1)S(1)}, bf16[4,128,256]{2,1,0:T(8,128)(2,1)S(1)}, u32[]{:S(2)}, u32[]{:S(2)}) collective-permute-start(bf16[4,128,256]{2,1,0:T(8,128)(2,1)S(1)} %collective-permute-done.55.refs_3_), channel_id=1, source_target_pairs={{0,1},{1,0},{2,3},{3,2},{4,5},{5,4},{6,7},{7,6},{8,9},{9,8},{10,11... | collective-permute-start | bytes 786440 | tf_op jit(solution)/shard_map/ppermute | solution.py:184
  172.8 1.6 collective-permute-start.58
  (13 other events, 27.3 us)

commit v5 on v4

--- a/solution.py
+++ b/solution.py
@@ -93,22 +93,26 @@
     position = jnp.clip(tick - segment, 0, batches - 1)
     bits = as_column(bit_ref[pl.ds(position, 1), :].astype(jnp.float32), rows)
     product = jnp.where(bits > 0.5, totals[1], totals[0]) * (1.0 / divisor)
-    lanes = largest_lanes(rows)
-    local = as_row(jnp.max(jnp.abs(product), axis=1, keepdims=True) + epsilon, lanes)
+    local = jnp.max(jnp.abs(product), axis=1, keepdims=True) + epsilon
     if following is None:
         largest_refs, (product_ref, maxima_ref) = refs[:-2], refs[-2:]
         product_ref[...] = product
-        everything = [ref[0:1, :] for ref in largest_refs] + [local[0:1]]
+        lanes = maxima_ref.shape[2]
+        newest = as_row(local, lanes)[0:1]
         for segment_here in range(RING):
             @pl.when(segment == segment_here)
             def _():
-                taken = jnp.concatenate(everything[segment_here:segment_here + batches], axis=0)
+                taken = [
+                    as_row(ref[:, 0:1], lanes)[0:1]
+                    for ref in largest_refs[segment_here:segment_here + batches]
+                ]
+                taken = jnp.concatenate((taken + [newest])[:batches], axis=0)
                 for i in range(maxima_ref.shape[0]):
                     maxima_ref[i] = taken
         return
     left_ref, product_ref, largest_ref, block_ref = refs
     product_ref[...] = product
-    largest_ref[...] = local
+    largest_ref[...] = jnp.broadcast_to(local, largest_ref.shape)
     block_ref[...] = jnp.where(
         segment == RING - 1, left_ref[pl.ds(following * rows, rows), :], product.astype(jnp.bfloat16)
     )
@@ -126,7 +130,7 @@
     else:
         out_shape = (
             product,
-            jax.ShapeDtypeStruct((8, largest_lanes(rows)), jnp.float32),
+            jax.ShapeDtypeStruct((rows, 128), jnp.float32),
             jax.ShapeDtypeStruct((rows, width), jnp.bfloat16),
         )
     return pl.pallas_call(
@@ -193,6 +197,8 @@
     first = jnp.concatenate([
         moved(both, lambda s, z, y, c, d=d: (s + 1, z + 2 * d, y + 2 * c, c)) for d in range(2)
     ])
+    early = swapped(first)
+    first, early = lax.optimization_barrier((first, early))
     return [
         first,
         moved(first, lambda s, z, y, c: (s, z + 1 - 2 * c, y, c)),
@@ -218,7 +224,7 @@
         held = gathered(block, swapped(block) if tick > 0 else other)
         if tensor is None:
             tensor = hold(site_tensors[0], held[0])
-            held, tensor, bits, place = lax.optimization_barrier((held, tensor, bits, place))
+            held[2], tensor, bits, place = lax.optimization_barrier((held[2], tensor, bits, place))
         held += [swapped(piece) for piece in held]
         if tick + 1 < ticks:
             following = min(tick + 1, BATCHES - 1)

time: 190 us -> 188 us (0.989)
  starting transfers between devices: 59.7 us -> 52.7 us
  waiting for transfers between devices: 98.6 us -> 103 us
    ppermute x60, starting transfers between devices: 59.7 us -> 52.7 us  [moved(): return lax.ppermute(value, ('segment', 'col'), pairs)]
    ppermute x60, waiting for transfers between devices: 98.6 us -> 103 us  [moved(): return lax.ppermute(value, ('segment', 'col'), pairs)]
  transfers between devices with their start and end apart: 60 -> 60, of which waited for: 43 -> 39; matrix products, arithmetic and copies ran while one was open for 1% -> 1% of each run, Pallas kernels for 2% -> 2%
where the time goes in v5:
time: 188 us
  waiting for transfers between devices  103 us (55%)
  starting transfers between devices  52.7 us (28%)
  Pallas kernels  17.3 us (9%)
  blocking collectives  11.9 us (6%)
    ppermute x60, waiting for transfers between devices, moved(): return lax.ppermute(value, ('segment', 'col'), pairs)  103 us
    ppermute x60, starting transfers between devices, moved(): return lax.ppermute(value, ('segment', 'col'), pairs)  52.7 us
    pallas_call x6, Pallas kernels, site(): pl.pallas_call(functools.partial(site_kernel, tick, following, batches),...  12 us
    all_to_all x1, blocking collectives, local(): maxima = lax.all_to_all(maxima, 'col', 0, 0, tiled=True)  11.9 us
  transfers between devices with their start and end apart: 60, of which 39 were waited for; matrix products, arithmetic and copies ran while one was open for 1% of the time, Pallas kernels for 2%

profile of v5, /device:TPU:1, one launch (start us, length us, event | category | flops | bytes accessed | tf_op | source)
XLA Modules:
  0.0 188.0 jit_solution(14731828649068593311)
XLA Ops:
  0.6 1.5 collective-permute-start
  3.4 7.3 %collective-permute-start.2 = (bf16[2,128,256]{2,1,0:T(8,128)(2,1)S(1)}, bf16[2,128,256]{2,1,0:T(8,128)(2,1)S(1)}, u32[]{:S(2)}, u32[]{:S(2)}) collective-permute-start(bf16[2,128,256]{2,1,0:T(8,128)(2,1)S(1)} %pad_maximum_fusion.6), channel_id=1, source_target_pairs={{0,48},{1,53},{2,50},{3,55},{4,52},{5,49},{6,54},{7,51},{8,56},{9,... | collective-permute-start | bytes 393224 | tf_op jit(solution)/shard_map/ppermute | solution.py:188
  11.7 3.6 %collective-permute-done.2 = bf16[2,128,256]{2,1,0:T(8,128)(2,1)S(1)} collective-permute-done((bf16[2,128,256]{2,1,0:T(8,128)(2,1)S(1)}, bf16[2,128,256]{2,1,0:T(8,128)(2,1)S(1)}, u32[]{:S(2)}, u32[]{:S(2)}) %collective-permute-start.2) | collective-permute-done | bytes 131104 | tf_op jit(solution)/shard_map/ppermute | solution.py:188
  15.3 3.3 %collective-permute-done.1 = bf16[2,128,256]{2,1,0:T(8,128)(2,1)S(1)} collective-permute-done((bf16[2,128,256]{2,1,0:T(8,128)(2,1)S(1)}, bf16[2,128,256]{2,1,0:T(8,128)(2,1)S(1)}, u32[]{:S(2)}, u32[]{:S(2)}) %collective-permute-start.1) | collective-permute-done | bytes 131104 | tf_op jit(solution)/shard_map/ppermute | solution.py:188
  18.6 1.4 collective-permute-start.3
  19.9 1.6 collective-permute-start.5
  22.5 3.5 %hold.1.refs_9_ = bf16[2,8192,256]{2,1,0:T(8,128)(2,1)S(1)} custom-call(bf16[2,8192,256]{2,1,0:T(8,128)(2,1)} %bitcast.31, bf16[4,128,256]{2,1,0:T(8,128)(2,1)S(1)} %pad_maximum_fusion.after_ref.refs_0_), custom_call_target="tpu_custom_call" | custom-call | tf_op jit(solution)/shard_map/hold/pallas_call | solution.py:59
  26.0 1.2 collective-permute-done.3.refs_2_
  28.2 1.3 collective-permute-done.4.refs_1_
  29.5 1.1 collective-permute-start.7
  30.6 1.1 collective-permute-done.7.refs_5_
  32.1 2.1 %site.6 = (f32[128,256]{1,0:T(8,128)S(1)}, f32[128,128]{1,0:T(8,128)S(1)}, bf16[128,256]{1,0:T(8,128)(2,1)S(1)}) custom-call(s32[4]{0:T(128)S(1)} %pad_add_fusion.place_ref, bf16[4,128,256]{2,1,0:T(8,128)(2,1)S(1)} %pad_maximum_fusion.after_ref.refs_0_, bf16[4,128,256]{2,1,0:T(8,128)(2,1)S(1)} %collective-permute-done.4.refs_1_, ...), custom_call_target="tpu_custom_call" | custom-call | tf_op jit(solution)/shard_map/site/pallas_call | solution.py:136
  36.3 2.3 %collective-permute-start.11 = (bf16[2,128,256]{2,1,0:T(8,128)(2,1)S(1)}, bf16[2,128,256]{2,1,0:T(8,128)(2,1)S(1)}, u32[]{:S(2)}, u32[]{:S(2)}) collective-permute-start(bf16[2,128,256]{2,1,0:T(8,128)(2,1)S(1)} %pad_maximum_fusion.7), channel_id=1, source_target_pairs={{0,32},{1,37},{2,34},{3,39},{4,36},{5,33},{6,38},{7,35},{8,40},{9,... | collective-permute-start | bytes 393224 | tf_op jit(solution)/shard_map/ppermute | solution.py:188
  38.7 8.1 %collective-permute-done.12 = bf16[2,128,256]{2,1,0:T(8,128)(2,1)S(1)} collective-permute-done((bf16[2,128,256]{2,1,0:T(8,128)(2,1)S(1)}, bf16[2,128,256]{2,1,0:T(8,128)(2,1)S(1)}, u32[]{:S(2)}, u32[]{:S(2)}) %collective-permute-start.12) | collective-permute-done | bytes 131104 | tf_op jit(solution)/shard_map/ppermute | solution.py:188
  46.8 2.6 %collective-permute-start.15 = (bf16[4,128,256]{2,1,0:T(8,128)(2,1)S(1)}, bf16[4,128,256]{2,1,0:T(8,128)(2,1)S(1)}, u32[]{:S(2)}, u32[]{:S(2)}) collective-permute-start(bf16[4,128,256]{2,1,0:T(8,128)(2,1)S(1)} %pad_maximum_fusion.1.refs_0_), channel_id=1, source_target_pairs={{0,14},{1,31},{2,8},{3,25},{4,10},{5,27},{6,12},{7,29},{8,22},{9,7... | collective-permute-start | bytes 786440 | tf_op jit(solution)/shard_map/ppermute | solution.py:188
  51.1 4.5 %collective-permute-done.15.refs_3_ = bf16[4,128,256]{2,1,0:T(8,128)(2,1)S(1)} collective-permute-done((bf16[4,128,256]{2,1,0:T(8,128)(2,1)S(1)}, bf16[4,128,256]{2,1,0:T(8,128)(2,1)S(1)}, u32[]{:S(2)}, u32[]{:S(2)}) %collective-permute-start.15) | collective-permute-done | bytes 262176 | tf_op jit(solution)/shard_map/ppermute | solution.py:188
  56.1 2.3 %collective-permute-done.14.refs_2_ = bf16[4,128,256]{2,1,0:T(8,128)(2,1)S(1)} collective-permute-done((bf16[4,128,256]{2,1,0:T(8,128)(2,1)S(1)}, bf16[4,128,256]{2,1,0:T(8,128)(2,1)S(1)}, u32[]{:S(2)}, u32[]{:S(2)}) %collective-permute-start.14) | collective-permute-done | bytes 262176 | tf_op jit(solution)/shard_map/ppermute | solution.py:188
  58.9 1.0 collective-permute-done.18.refs_6_
  60.3 1.9 %site.7 = (f32[128,256]{1,0:T(8,128)S(1)}, f32[128,128]{1,0:T(8,128)S(1)}, bf16[128,256]{1,0:T(8,128)(2,1)S(1)}) custom-call(s32[4]{0:T(128)S(1)} %pad_add_fusion.place_ref, bf16[4,128,256]{2,1,0:T(8,128)(2,1)S(1)} %pad_maximum_fusion.1.refs_0_, bf16[4,128,256]{2,1,0:T(8,128)(2,1)S(1)} %collective-permute-done.13.refs_1_, ...), custom_call_target="tpu_custom_call" | custom-call | tf_op jit(solution)/shard_map/site/pallas_call | solution.py:136
  63.9 3.3 %collective-permute-start.21 = (bf16[2,128,256]{2,1,0:T(8,128)(2,1)S(1)}, bf16[2,128,256]{2,1,0:T(8,128)(2,1)S(1)}, u32[]{:S(2)}, u32[]{:S(2)}) collective-permute-start(bf16[2,128,256]{2,1,0:T(8,128)(2,1)S(1)} %pad_maximum_fusion.8), channel_id=1, source_target_pairs={{0,32},{1,37},{2,34},{3,39},{4,36},{5,33},{6,38},{7,35},{8,40},{9,... | collective-permute-start | bytes 393224 | tf_op jit(solution)/shard_map/ppermute | solution.py:188
  67.3 7.3 %collective-permute-done.22 = bf16[2,128,256]{2,1,0:T(8,128)(2,1)S(1)} collective-permute-done((bf16[2,128,256]{2,1,0:T(8,128)(2,1)S(1)}, bf16[2,128,256]{2,1,0:T(8,128)(2,1)S(1)}, u32[]{:S(2)}, u32[]{:S(2)}) %collective-permute-start.22) | collective-permute-done | bytes 131104 | tf_op jit(solution)/shard_map/ppermute | solution.py:188
  75.4 2.2 %collective-permute-start.25 = (bf16[4,128,256]{2,1,0:T(8,128)(2,1)S(1)}, bf16[4,128,256]{2,1,0:T(8,128)(2,1)S(1)}, u32[]{:S(2)}, u32[]{:S(2)}) collective-permute-start(bf16[4,128,256]{2,1,0:T(8,128)(2,1)S(1)} %pad_maximum_fusion.2.refs_0_), channel_id=1, source_target_pairs={{0,14},{1,31},{2,8},{3,25},{4,10},{5,27},{6,12},{7,29},{8,22},{9,7... | collective-permute-start | bytes 786440 | tf_op jit(solution)/shard_map/ppermute | solution.py:188
  78.0 6.2 %collective-permute-done.25.refs_3_ = bf16[4,128,256]{2,1,0:T(8,128)(2,1)S(1)} collective-permute-done((bf16[4,128,256]{2,1,0:T(8,128)(2,1)S(1)}, bf16[4,128,256]{2,1,0:T(8,128)(2,1)S(1)}, u32[]{:S(2)}, u32[]{:S(2)}) %collective-permute-start.25) | collective-permute-done | bytes 262176 | tf_op jit(solution)/shard_map/ppermute | solution.py:188
  84.9 1.5 collective-permute-done.24.refs_2_
  88.6 1.9 %site.8 = (f32[128,256]{1,0:T(8,128)S(1)}, f32[128,128]{1,0:T(8,128)S(1)}, bf16[128,256]{1,0:T(8,128)(2,1)S(1)}) custom-call(s32[4]{0:T(128)S(1)} %pad_add_fusion.place_ref, bf16[4,128,256]{2,1,0:T(8,128)(2,1)S(1)} %pad_maximum_fusion.2.refs_0_, bf16[4,128,256]{2,1,0:T(8,128)(2,1)S(1)} %collective-permute-done.23.refs_1_, ...), custom_call_target="tpu_custom_call" | custom-call | tf_op jit(solution)/shard_map/site/pallas_call | solution.py:136
  92.0 2.0 %collective-permute-start.31 = (bf16[2,128,256]{2,1,0:T(8,128)(2,1)S(1)}, bf16[2,128,256]{2,1,0:T(8,128)(2,1)S(1)}, u32[]{:S(2)}, u32[]{:S(2)}) collective-permute-start(bf16[2,128,256]{2,1,0:T(8,128)(2,1)S(1)} %pad_maximum_fusion.9), channel_id=1, source_target_pairs={{0,32},{1,37},{2,34},{3,39},{4,36},{5,33},{6,38},{7,35},{8,40},{9,... | collective-permute-start | bytes 393224 | tf_op jit(solution)/shard_map/ppermute | solution.py:188
  94.0 8.9 %collective-permute-done.32 = bf16[2,128,256]{2,1,0:T(8,128)(2,1)S(1)} collective-permute-done((bf16[2,128,256]{2,1,0:T(8,128)(2,1)S(1)}, bf16[2,128,256]{2,1,0:T(8,128)(2,1)S(1)}, u32[]{:S(2)}, u32[]{:S(2)}) %collective-permute-start.32) | collective-permute-done | bytes 131104 | tf_op jit(solution)/shard_map/ppermute | solution.py:188
  102.9 2.5 %collective-permute-start.35 = (bf16[4,128,256]{2,1,0:T(8,128)(2,1)S(1)}, bf16[4,128,256]{2,1,0:T(8,128)(2,1)S(1)}, u32[]{:S(2)}, u32[]{:S(2)}) collective-permute-start(bf16[4,128,256]{2,1,0:T(8,128)(2,1)S(1)} %pad_maximum_fusion.3.refs_0_), channel_id=1, source_target_pairs={{0,14},{1,31},{2,8},{3,25},{4,10},{5,27},{6,12},{7,29},{8,22},{9,7... | collective-permute-start | bytes 786440 | tf_op jit(solution)/shard_map/ppermute | solution.py:188
  106.4 5.6 %collective-permute-done.35.refs_3_ = bf16[4,128,256]{2,1,0:T(8,128)(2,1)S(1)} collective-permute-done((bf16[4,128,256]{2,1,0:T(8,128)(2,1)S(1)}, bf16[4,128,256]{2,1,0:T(8,128)(2,1)S(1)}, u32[]{:S(2)}, u32[]{:S(2)}) %collective-permute-start.35) | collective-permute-done | bytes 262176 | tf_op jit(solution)/shard_map/ppermute | solution.py:188
  111.9 1.2 collective-permute-start.39
  116.1 1.9 %site.9 = (f32[128,256]{1,0:T(8,128)S(1)}, f32[128,128]{1,0:T(8,128)S(1)}, bf16[128,256]{1,0:T(8,128)(2,1)S(1)}) custom-call(s32[4]{0:T(128)S(1)} %pad_add_fusion.place_ref, bf16[4,128,256]{2,1,0:T(8,128)(2,1)S(1)} %pad_maximum_fusion.3.refs_0_, bf16[4,128,256]{2,1,0:T(8,128)(2,1)S(1)} %collective-permute-done.33.refs_1_, ...), custom_call_target="tpu_custom_call" | custom-call | tf_op jit(solution)/shard_map/site/pallas_call | solution.py:136
  120.0 10.3 %collective-permute-done.42 = bf16[2,128,256]{2,1,0:T(8,128)(2,1)S(1)} collective-permute-done((bf16[2,128,256]{2,1,0:T(8,128)(2,1)S(1)}, bf16[2,128,256]{2,1,0:T(8,128)(2,1)S(1)}, u32[]{:S(2)}, u32[]{:S(2)}) %collective-permute-start.42) | collective-permute-done | bytes 131104 | tf_op jit(solution)/shard_map/ppermute | solution.py:188
  130.4 3.2 %collective-permute-start.45 = (bf16[4,128,256]{2,1,0:T(8,128)(2,1)S(1)}, bf16[4,128,256]{2,1,0:T(8,128)(2,1)S(1)}, u32[]{:S(2)}, u32[]{:S(2)}) collective-permute-start(bf16[4,128,256]{2,1,0:T(8,128)(2,1)S(1)} %pad_maximum_fusion.4.refs_0_), channel_id=1, source_target_pairs={{0,14},{1,31},{2,8},{3,25},{4,10},{5,27},{6,12},{7,29},{8,22},{9,7... | collective-permute-start | bytes 786440 | tf_op jit(solution)/shard_map/ppermute | solution.py:188
  133.8 5.6 %collective-permute-done.45.refs_3_ = bf16[4,128,256]{2,1,0:T(8,128)(2,1)S(1)} collective-permute-done((bf16[4,128,256]{2,1,0:T(8,128)(2,1)S(1)}, bf16[4,128,256]{2,1,0:T(8,128)(2,1)S(1)}, u32[]{:S(2)}, u32[]{:S(2)}) %collective-permute-start.45) | collective-permute-done | bytes 262176 | tf_op jit(solution)/shard_map/ppermute | solution.py:188
  139.5 1.2 collective-permute-start.49
  140.7 1.6 collective-permute-done.44.refs_2_
  142.8 1.0 collective-permute-done.48.refs_6_
  144.2 1.9 %site.10 = (f32[128,256]{1,0:T(8,128)S(1)}, f32[128,128]{1,0:T(8,128)S(1)}, bf16[128,256]{1,0:T(8,128)(2,1)S(1)}) custom-call(s32[4]{0:T(128)S(1)} %pad_add_fusion.place_ref, bf16[4,128,256]{2,1,0:T(8,128)(2,1)S(1)} %pad_maximum_fusion.4.refs_0_, bf16[4,128,256]{2,1,0:T(8,128)(2,1)S(1)} %collective-permute-done.43.refs_1_, ...), custom_call_target="tpu_custom_call" | custom-call | tf_op jit(solution)/shard_map/site/pallas_call | solution.py:136
  146.4 1.1 collective-permute-done.50
  148.6 10.2 %collective-permute-done.52 = bf16[2,128,256]{2,1,0:T(8,128)(2,1)S(1)} collective-permute-done((bf16[2,128,256]{2,1,0:T(8,128)(2,1)S(1)}, bf16[2,128,256]{2,1,0:T(8,128)(2,1)S(1)}, u32[]{:S(2)}, u32[]{:S(2)}) %collective-permute-start.52) | collective-permute-done | bytes 131104 | tf_op jit(solution)/shard_map/ppermute | solution.py:188
  158.8 2.6 %collective-permute-start.55 = (bf16[4,128,256]{2,1,0:T(8,128)(2,1)S(1)}, bf16[4,128,256]{2,1,0:T(8,128)(2,1)S(1)}, u32[]{:S(2)}, u32[]{:S(2)}) collective-permute-start(bf16[4,128,256]{2,1,0:T(8,128)(2,1)S(1)} %pad_maximum_fusion.5.refs_0_), channel_id=1, source_target_pairs={{0,14},{1,31},{2,8},{3,25},{4,10},{5,27},{6,12},{7,29},{8,22},{9,7... | collective-permute-start | bytes 786440 | tf_op jit(solution)/shard_map/ppermute | solution.py:188
  162.1 5.7 %collective-permute-done.55.refs_3_ = bf16[4,128,256]{2,1,0:T(8,128)(2,1)S(1)} collective-permute-done((bf16[4,128,256]{2,1,0:T(8,128)(2,1)S(1)}, bf16[4,128,256]{2,1,0:T(8,128)(2,1)S(1)}, u32[]{:S(2)}, u32[]{:S(2)}) %collective-permute-start.55) | collective-permute-done | bytes 262176 | tf_op jit(solution)/shard_map/ppermute | solution.py:188
  167.8 1.2 collective-permute-start.59
  169.1 1.2 collective-permute-done.54.refs_2_
  170.7 1.0 collective-permute-done.58.refs_6_
  172.1 2.2 %site.11 = (f32[128,256]{1,0:T(8,128)S(1)}, f32[32,3,128]{2,1,0:T(4,128)S(1)}) custom-call(s32[4]{0:T(128)S(1)} %pad_add_fusion.place_ref, bf16[4,128,256]{2,1,0:T(8,128)(2,1)S(1)} %pad_maximum_fusion.5.refs_0_, bf16[4,128,256]{2,1,0:T(8,128)(2,1)S(1)} %collective-permute-done.53.refs_1_, bf16[4,128,256]{2,1,0:T(8,128)(2,1)S(1)} %collective-permute-done.54.refs_2_, ...), custom_call_target="tpu_custom_call" | custom-call | tf_op jit(solution)/shard_map/site/pallas_call | solution.py:136
  174.3 11.9 %all_to_all.5.maxima_ref = f32[32,3,128]{2,1,0:T(4,128)S(1)} all-to-all(f32[32,3,128]{2,1,0:T(4,128)S(1)} %get-tuple-element.37), channel_id=1, replica_groups=mesh['segment'=4,'col'=32] {'col'}, dimensions={0} | all-to-all | bytes 98304 | tf_op jit(solution)/shard_map/all_to_all | solution.py:237
  186.2 1.8 finish.1
  (99 shorter events, 27.2 us)
Async XLA Ops:
  0.6 2.8 %collective-permute-start = (bf16[384,256]{1,0:T(8,128)(2,1)}, bf16[384,256]{1,0:T(8,128)(2,1)S(1)}, u32[]{:S(2)}, u32[]{:S(2)}) collective-permute-start(bf16[384,256]{1,0:T(8,128)(2,1)} %refs_10_.9), channel_id=1, source_target_pairs={{0,1},{1,0},{2,3},{3,2},{4,5},{5,4},{6,7},{7,6},{8,9},{9,8},{10,11... | collective-permute-start | bytes 589832 | tf_op jit(solution)/shard_map/ppermute | solution.py:188
  3.4 11.8 %collective-permute-start.2 = (bf16[2,128,256]{2,1,0:T(8,128)(2,1)S(1)}, bf16[2,128,256]{2,1,0:T(8,128)(2,1)S(1)}, u32[]{:S(2)}, u32[]{:S(2)}) collective-permute-start(bf16[2,128,256]{2,1,0:T(8,128)(2,1)S(1)} %pad_maximum_fusion.6), channel_id=1, source_target_pairs={{0,48},{1,53},{2,50},{3,55},{4,52},{5,49},{6,54},{7,51},{8,56},{9,... | collective-permute-start | bytes 393224 | tf_op jit(solution)/shard_map/ppermute | solution.py:188
  10.7 7.8 %collective-permute-start.1 = (bf16[2,128,256]{2,1,0:T(8,128)(2,1)S(1)}, bf16[2,128,256]{2,1,0:T(8,128)(2,1)S(1)}, u32[]{:S(2)}, u32[]{:S(2)}) collective-permute-start(bf16[2,128,256]{2,1,0:T(8,128)(2,1)S(1)} %pad_maximum_fusion.6), channel_id=1, source_target_pairs={{0,32},{1,37},{2,34},{3,39},{4,36},{5,33},{6,38},{7,35},{8,40},{9,... | collective-permute-start | bytes 393224 | tf_op jit(solution)/shard_map/ppermute | solution.py:188
  18.6 8.6 %collective-permute-start.3 = (bf16[4,128,256]{2,1,0:T(8,128)(2,1)S(1)}, bf16[4,128,256]{2,1,0:T(8,128)(2,1)S(1)}, u32[]{:S(2)}, u32[]{:S(2)}) collective-permute-start(bf16[4,128,256]{2,1,0:T(8,128)(2,1)S(1)} %pad_maximum_fusion.after_ref.refs_0_), channel_id=1, source_target_pairs={{0,2},{1,3},{2,4},{3,5},{4,6},{5,7},{6,0},{7,1},{8,10},{9,11},{10,... | collective-permute-start | bytes 786440 | tf_op jit(solution)/shard_map/ppermute | solution.py:188
  19.9 7.3 %collective-permute-start.5 = (bf16[4,128,256]{2,1,0:T(8,128)(2,1)S(1)}, bf16[4,128,256]{2,1,0:T(8,128)(2,1)S(1)}, u32[]{:S(2)}, u32[]{:S(2)}) collective-permute-start(bf16[4,128,256]{2,1,0:T(8,128)(2,1)S(1)} %pad_maximum_fusion.after_ref.refs_0_), channel_id=1, source_target_pairs={{0,14},{1,31},{2,8},{3,25},{4,10},{5,27},{6,12},{7,29},{8,22},{9,7... | collective-permute-start | bytes 786440 | tf_op jit(solution)/shard_map/ppermute | solution.py:188
  21.5 8.0 %collective-permute-start.4 = (bf16[4,128,256]{2,1,0:T(8,128)(2,1)S(1)}, bf16[4,128,256]{2,1,0:T(8,128)(2,1)S(1)}, u32[]{:S(2)}, u32[]{:S(2)}) collective-permute-start(bf16[4,128,256]{2,1,0:T(8,128)(2,1)S(1)} %pad_maximum_fusion.after_ref.refs_0_), channel_id=1, source_target_pairs={{0,8},{1,25},{2,10},{3,27},{4,12},{5,29},{6,14},{7,31},{8,16},{9,1... | collective-permute-start | bytes 786440 | tf_op jit(solution)/shard_map/ppermute | solution.py:188
  22.4 8.1 %collective-permute-start.6 = (bf16[4,128,256]{2,1,0:T(8,128)(2,1)S(1)}, bf16[4,128,256]{2,1,0:T(8,128)(2,1)S(1)}, u32[]{:S(2)}, u32[]{:S(2)}) collective-permute-start(bf16[4,128,256]{2,1,0:T(8,128)(2,1)S(1)} %pad_maximum_fusion.after_ref.refs_0_), channel_id=1, source_target_pairs={{0,1},{1,0},{2,3},{3,2},{4,5},{5,4},{6,7},{7,6},{8,9},{9,8},{10,11... | collective-permute-start | bytes 786440 | tf_op jit(solution)/shard_map/ppermute | solution.py:188
  27.3 3.3 %collective-permute-start.9 = (bf16[4,128,256]{2,1,0:T(8,128)(2,1)S(1)}, bf16[4,128,256]{2,1,0:T(8,128)(2,1)S(1)}, u32[]{:S(2)}, u32[]{:S(2)}) collective-permute-start(bf16[4,128,256]{2,1,0:T(8,128)(2,1)S(1)} %collective-permute-done.5.refs_3_), channel_id=1, source_target_pairs={{0,1},{1,0},{2,3},{3,2},{4,5},{5,4},{6,7},{7,6},{8,9},{9,8},{10,11... | collective-permute-start | bytes 786440 | tf_op jit(solution)/shard_map/ppermute | solution.py:188
  29.5 2.3 %collective-permute-start.7 = (bf16[4,128,256]{2,1,0:T(8,128)(2,1)S(1)}, bf16[4,128,256]{2,1,0:T(8,128)(2,1)S(1)}, u32[]{:S(2)}, u32[]{:S(2)}) collective-permute-start(bf16[4,128,256]{2,1,0:T(8,128)(2,1)S(1)} %collective-permute-done.4.refs_1_), channel_id=1, source_target_pairs={{0,1},{1,0},{2,3},{3,2},{4,5},{5,4},{6,7},{7,6},{8,9},{9,8},{10,11... | collective-permute-start | bytes 786440 | tf_op jit(solution)/shard_map/ppermute | solution.py:188
  35.6 11.2 %collective-permute-start.12 = (bf16[2,128,256]{2,1,0:T(8,128)(2,1)S(1)}, bf16[2,128,256]{2,1,0:T(8,128)(2,1)S(1)}, u32[]{:S(2)}, u32[]{:S(2)}) collective-permute-start(bf16[2,128,256]{2,1,0:T(8,128)(2,1)S(1)} %pad_maximum_fusion.7), channel_id=1, source_target_pairs={{0,48},{1,53},{2,50},{3,55},{4,52},{5,49},{6,54},{7,51},{8,56},{9,... | collective-permute-start | bytes 393224 | tf_op jit(solution)/shard_map/ppermute | solution.py:188
  36.3 10.5 %collective-permute-start.11 = (bf16[2,128,256]{2,1,0:T(8,128)(2,1)S(1)}, bf16[2,128,256]{2,1,0:T(8,128)(2,1)S(1)}, u32[]{:S(2)}, u32[]{:S(2)}) collective-permute-start(bf16[2,128,256]{2,1,0:T(8,128)(2,1)S(1)} %pad_maximum_fusion.7), channel_id=1, source_target_pairs={{0,32},{1,37},{2,34},{3,39},{4,36},{5,33},{6,38},{7,35},{8,40},{9,... | collective-permute-start | bytes 393224 | tf_op jit(solution)/shard_map/ppermute | solution.py:188
  46.8 8.7 %collective-permute-start.15 = (bf16[4,128,256]{2,1,0:T(8,128)(2,1)S(1)}, bf16[4,128,256]{2,1,0:T(8,128)(2,1)S(1)}, u32[]{:S(2)}, u32[]{:S(2)}) collective-permute-start(bf16[4,128,256]{2,1,0:T(8,128)(2,1)S(1)} %pad_maximum_fusion.1.refs_0_), channel_id=1, source_target_pairs={{0,14},{1,31},{2,8},{3,25},{4,10},{5,27},{6,12},{7,29},{8,22},{9,7... | collective-permute-start | bytes 786440 | tf_op jit(solution)/shard_map/ppermute | solution.py:188
  49.5 8.9 %collective-permute-start.14 = (bf16[4,128,256]{2,1,0:T(8,128)(2,1)S(1)}, bf16[4,128,256]{2,1,0:T(8,128)(2,1)S(1)}, u32[]{:S(2)}, u32[]{:S(2)}) collective-permute-start(bf16[4,128,256]{2,1,0:T(8,128)(2,1)S(1)} %pad_maximum_fusion.1.refs_0_), channel_id=1, source_target_pairs={{0,2},{1,3},{2,4},{3,5},{4,6},{5,7},{6,0},{7,1},{8,10},{9,11},{10,... | collective-permute-start | bytes 786440 | tf_op jit(solution)/shard_map/ppermute | solution.py:188
  50.3 8.5 %collective-permute-start.13 = (bf16[4,128,256]{2,1,0:T(8,128)(2,1)S(1)}, bf16[4,128,256]{2,1,0:T(8,128)(2,1)S(1)}, u32[]{:S(2)}, u32[]{:S(2)}) collective-permute-start(bf16[4,128,256]{2,1,0:T(8,128)(2,1)S(1)} %pad_maximum_fusion.1.refs_0_), channel_id=1, source_target_pairs={{0,8},{1,25},{2,10},{3,27},{4,12},{5,29},{6,14},{7,31},{8,16},{9,1... | collective-permute-start | bytes 786440 | tf_op jit(solution)/shard_map/ppermute | solution.py:188
  51.1 7.8 %collective-permute-start.16 = (bf16[4,128,256]{2,1,0:T(8,128)(2,1)S(1)}, bf16[4,128,256]{2,1,0:T(8,128)(2,1)S(1)}, u32[]{:S(2)}, u32[]{:S(2)}) collective-permute-start(bf16[4,128,256]{2,1,0:T(8,128)(2,1)S(1)} %pad_maximum_fusion.1.refs_0_), channel_id=1, source_target_pairs={{0,1},{1,0},{2,3},{3,2},{4,5},{5,4},{6,7},{7,6},{8,9},{9,8},{10,11... | collective-permute-start | bytes 786440 | tf_op jit(solution)/shard_map/ppermute | solution.py:188
  55.6 3.4 %collective-permute-start.19 = (bf16[4,128,256]{2,1,0:T(8,128)(2,1)S(1)}, bf16[4,128,256]{2,1,0:T(8,128)(2,1)S(1)}, u32[]{:S(2)}, u32[]{:S(2)}) collective-permute-start(bf16[4,128,256]{2,1,0:T(8,128)(2,1)S(1)} %collective-permute-done.15.refs_3_), channel_id=1, source_target_pairs={{0,1},{1,0},{2,3},{3,2},{4,5},{5,4},{6,7},{7,6},{8,9},{9,8},{10,11... | collective-permute-start | bytes 786440 | tf_op jit(solution)/shard_map/ppermute | solution.py:188
  58.7 1.5 collective-permute-start.17
  63.6 11.0 %collective-permute-start.22 = (bf16[2,128,256]{2,1,0:T(8,128)(2,1)S(1)}, bf16[2,128,256]{2,1,0:T(8,128)(2,1)S(1)}, u32[]{:S(2)}, u32[]{:S(2)}) collective-permute-start(bf16[2,128,256]{2,1,0:T(8,128)(2,1)S(1)} %pad_maximum_fusion.8), channel_id=1, source_target_pairs={{0,48},{1,53},{2,50},{3,55},{4,52},{5,49},{6,54},{7,51},{8,56},{9,... | collective-permute-start | bytes 393224 | tf_op jit(solution)/shard_map/ppermute | solution.py:188
  63.9 11.4 %collective-permute-start.21 = (bf16[2,128,256]{2,1,0:T(8,128)(2,1)S(1)}, bf16[2,128,256]{2,1,0:T(8,128)(2,1)S(1)}, u32[]{:S(2)}, u32[]{:S(2)}) collective-permute-start(bf16[2,128,256]{2,1,0:T(8,128)(2,1)S(1)} %pad_maximum_fusion.8), channel_id=1, source_target_pairs={{0,32},{1,37},{2,34},{3,39},{4,36},{5,33},{6,38},{7,35},{8,40},{9,... | collective-permute-start | bytes 393224 | tf_op jit(solution)/shard_map/ppermute | solution.py:188
  75.4 8.8 %collective-permute-start.25 = (bf16[4,128,256]{2,1,0:T(8,128)(2,1)S(1)}, bf16[4,128,256]{2,1,0:T(8,128)(2,1)S(1)}, u32[]{:S(2)}, u32[]{:S(2)}) collective-permute-start(bf16[4,128,256]{2,1,0:T(8,128)(2,1)S(1)} %pad_maximum_fusion.2.refs_0_), channel_id=1, source_target_pairs={{0,14},{1,31},{2,8},{3,25},{4,10},{5,27},{6,12},{7,29},{8,22},{9,7... | collective-permute-start | bytes 786440 | tf_op jit(solution)/shard_map/ppermute | solution.py:188
  77.6 8.9 %collective-permute-start.24 = (bf16[4,128,256]{2,1,0:T(8,128)(2,1)S(1)}, bf16[4,128,256]{2,1,0:T(8,128)(2,1)S(1)}, u32[]{:S(2)}, u32[]{:S(2)}) collective-permute-start(bf16[4,128,256]{2,1,0:T(8,128)(2,1)S(1)} %pad_maximum_fusion.2.refs_0_), channel_id=1, source_target_pairs={{0,2},{1,3},{2,4},{3,5},{4,6},{5,7},{6,0},{7,1},{8,10},{9,11},{10,... | collective-permute-start | bytes 786440 | tf_op jit(solution)/shard_map/ppermute | solution.py:188
  77.8 8.7 %collective-permute-start.23 = (bf16[4,128,256]{2,1,0:T(8,128)(2,1)S(1)}, bf16[4,128,256]{2,1,0:T(8,128)(2,1)S(1)}, u32[]{:S(2)}, u32[]{:S(2)}) collective-permute-start(bf16[4,128,256]{2,1,0:T(8,128)(2,1)S(1)} %pad_maximum_fusion.2.refs_0_), channel_id=1, source_target_pairs={{0,8},{1,25},{2,10},{3,27},{4,12},{5,29},{6,14},{7,31},{8,16},{9,1... | collective-permute-start | bytes 786440 | tf_op jit(solution)/shard_map/ppermute | solution.py:188
  77.9 9.6 %collective-permute-start.26 = (bf16[4,128,256]{2,1,0:T(8,128)(2,1)S(1)}, bf16[4,128,256]{2,1,0:T(8,128)(2,1)S(1)}, u32[]{:S(2)}, u32[]{:S(2)}) collective-permute-start(bf16[4,128,256]{2,1,0:T(8,128)(2,1)S(1)} %pad_maximum_fusion.2.refs_0_), channel_id=1, source_target_pairs={{0,1},{1,0},{2,3},{3,2},{4,5},{5,4},{6,7},{7,6},{8,9},{9,8},{10,11... | collective-permute-start | bytes 786440 | tf_op jit(solution)/shard_map/ppermute | solution.py:188
  84.2 3.3 %collective-permute-start.29 = (bf16[4,128,256]{2,1,0:T(8,128)(2,1)S(1)}, bf16[4,128,256]{2,1,0:T(8,128)(2,1)S(1)}, u32[]{:S(2)}, u32[]{:S(2)}) collective-permute-start(bf16[4,128,256]{2,1,0:T(8,128)(2,1)S(1)} %collective-permute-done.25.refs_3_), channel_id=1, source_target_pairs={{0,1},{1,0},{2,3},{3,2},{4,5},{5,4},{6,7},{7,6},{8,9},{9,8},{10,11... | collective-permute-start | bytes 786440 | tf_op jit(solution)/shard_map/ppermute | solution.py:188
  86.5 2.1 %collective-permute-start.27 = (bf16[4,128,256]{2,1,0:T(8,128)(2,1)S(1)}, bf16[4,128,256]{2,1,0:T(8,128)(2,1)S(1)}, u32[]{:S(2)}, u32[]{:S(2)}) collective-permute-start(bf16[4,128,256]{2,1,0:T(8,128)(2,1)S(1)} %collective-permute-done.23.refs_1_), channel_id=1, source_target_pairs={{0,1},{1,0},{2,3},{3,2},{4,5},{5,4},{6,7},{7,6},{8,9},{9,8},{10,11... | collective-permute-start | bytes 786440 | tf_op jit(solution)/shard_map/ppermute | solution.py:188
  91.9 10.9 %collective-permute-start.32 = (bf16[2,128,256]{2,1,0:T(8,128)(2,1)S(1)}, bf16[2,128,256]{2,1,0:T(8,128)(2,1)S(1)}, u32[]{:S(2)}, u32[]{:S(2)}) collective-permute-start(bf16[2,128,256]{2,1,0:T(8,128)(2,1)S(1)} %pad_maximum_fusion.9), channel_id=1, source_target_pairs={{0,48},{1,53},{2,50},{3,55},{4,52},{5,49},{6,54},{7,51},{8,56},{9,... | collective-permute-start | bytes 393224 | tf_op jit(solution)/shard_map/ppermute | solution.py:188
  92.0 10.8 %collective-permute-start.31 = (bf16[2,128,256]{2,1,0:T(8,128)(2,1)S(1)}, bf16[2,128,256]{2,1,0:T(8,128)(2,1)S(1)}, u32[]{:S(2)}, u32[]{:S(2)}) collective-permute-start(bf16[2,128,256]{2,1,0:T(8,128)(2,1)S(1)} %pad_maximum_fusion.9), channel_id=1, source_target_pairs={{0,32},{1,37},{2,34},{3,39},{4,36},{5,33},{6,38},{7,35},{8,40},{9,... | collective-permute-start | bytes 393224 | tf_op jit(solution)/shard_map/ppermute | solution.py:188
  102.9 9.1 %collective-permute-start.35 = (bf16[4,128,256]{2,1,0:T(8,128)(2,1)S(1)}, bf16[4,128,256]{2,1,0:T(8,128)(2,1)S(1)}, u32[]{:S(2)}, u32[]{:S(2)}) collective-permute-start(bf16[4,128,256]{2,1,0:T(8,128)(2,1)S(1)} %pad_maximum_fusion.3.refs_0_), channel_id=1, source_target_pairs={{0,14},{1,31},{2,8},{3,25},{4,10},{5,27},{6,12},{7,29},{8,22},{9,7... | collective-permute-start | bytes 786440 | tf_op jit(solution)/shard_map/ppermute | solution.py:188
  105.4 8.8 %collective-permute-start.34 = (bf16[4,128,256]{2,1,0:T(8,128)(2,1)S(1)}, bf16[4,128,256]{2,1,0:T(8,128)(2,1)S(1)}, u32[]{:S(2)}, u32[]{:S(2)}) collective-permute-start(bf16[4,128,256]{2,1,0:T(8,128)(2,1)S(1)} %pad_maximum_fusion.3.refs_0_), channel_id=1, source_target_pairs={{0,2},{1,3},{2,4},{3,5},{4,6},{5,7},{6,0},{7,1},{8,10},{9,11},{10,... | collective-permute-start | bytes 786440 | tf_op jit(solution)/shard_map/ppermute | solution.py:188
  105.4 9.1 %collective-permute-start.33 = (bf16[4,128,256]{2,1,0:T(8,128)(2,1)S(1)}, bf16[4,128,256]{2,1,0:T(8,128)(2,1)S(1)}, u32[]{:S(2)}, u32[]{:S(2)}) collective-permute-start(bf16[4,128,256]{2,1,0:T(8,128)(2,1)S(1)} %pad_maximum_fusion.3.refs_0_), channel_id=1, source_target_pairs={{0,8},{1,25},{2,10},{3,27},{4,12},{5,29},{6,14},{7,31},{8,16},{9,1... | collective-permute-start | bytes 786440 | tf_op jit(solution)/shard_map/ppermute | solution.py:188
  106.4 8.3 %collective-permute-start.36 = (bf16[4,128,256]{2,1,0:T(8,128)(2,1)S(1)}, bf16[4,128,256]{2,1,0:T(8,128)(2,1)S(1)}, u32[]{:S(2)}, u32[]{:S(2)}) collective-permute-start(bf16[4,128,256]{2,1,0:T(8,128)(2,1)S(1)} %pad_maximum_fusion.3.refs_0_), channel_id=1, source_target_pairs={{0,1},{1,0},{2,3},{3,2},{4,5},{5,4},{6,7},{7,6},{8,9},{9,8},{10,11... | collective-permute-start | bytes 786440 | tf_op jit(solution)/shard_map/ppermute | solution.py:188
  111.9 2.8 %collective-permute-start.39 = (bf16[4,128,256]{2,1,0:T(8,128)(2,1)S(1)}, bf16[4,128,256]{2,1,0:T(8,128)(2,1)S(1)}, u32[]{:S(2)}, u32[]{:S(2)}) collective-permute-start(bf16[4,128,256]{2,1,0:T(8,128)(2,1)S(1)} %collective-permute-done.35.refs_3_), channel_id=1, source_target_pairs={{0,1},{1,0},{2,3},{3,2},{4,5},{5,4},{6,7},{7,6},{8,9},{9,8},{10,11... | collective-permute-start | bytes 786440 | tf_op jit(solution)/shard_map/ppermute | solution.py:188
  114.5 1.6 collective-permute-start.37
  119.4 11.0 %collective-permute-start.42 = (bf16[2,128,256]{2,1,0:T(8,128)(2,1)S(1)}, bf16[2,128,256]{2,1,0:T(8,128)(2,1)S(1)}, u32[]{:S(2)}, u32[]{:S(2)}) collective-permute-start(bf16[2,128,256]{2,1,0:T(8,128)(2,1)S(1)} %pad_maximum_fusion.10), channel_id=1, source_target_pairs={{0,48},{1,53},{2,50},{3,55},{4,52},{5,49},{6,54},{7,51},{8,56},{9,... | collective-permute-start | bytes 393224 | tf_op jit(solution)/shard_map/ppermute | solution.py:188
  119.5 10.9 %collective-permute-start.41 = (bf16[2,128,256]{2,1,0:T(8,128)(2,1)S(1)}, bf16[2,128,256]{2,1,0:T(8,128)(2,1)S(1)}, u32[]{:S(2)}, u32[]{:S(2)}) collective-permute-start(bf16[2,128,256]{2,1,0:T(8,128)(2,1)S(1)} %pad_maximum_fusion.10), channel_id=1, source_target_pairs={{0,32},{1,37},{2,34},{3,39},{4,36},{5,33},{6,38},{7,35},{8,40},{9,... | collective-permute-start | bytes 393224 | tf_op jit(solution)/shard_map/ppermute | solution.py:188
  130.4 9.1 %collective-permute-start.45 = (bf16[4,128,256]{2,1,0:T(8,128)(2,1)S(1)}, bf16[4,128,256]{2,1,0:T(8,128)(2,1)S(1)}, u32[]{:S(2)}, u32[]{:S(2)}) collective-permute-start(bf16[4,128,256]{2,1,0:T(8,128)(2,1)S(1)} %pad_maximum_fusion.4.refs_0_), channel_id=1, source_target_pairs={{0,14},{1,31},{2,8},{3,25},{4,10},{5,27},{6,12},{7,29},{8,22},{9,7... | collective-permute-start | bytes 786440 | tf_op jit(solution)/shard_map/ppermute | solution.py:188
  133.6 8.7 %collective-permute-start.44 = (bf16[4,128,256]{2,1,0:T(8,128)(2,1)S(1)}, bf16[4,128,256]{2,1,0:T(8,128)(2,1)S(1)}, u32[]{:S(2)}, u32[]{:S(2)}) collective-permute-start(bf16[4,128,256]{2,1,0:T(8,128)(2,1)S(1)} %pad_maximum_fusion.4.refs_0_), channel_id=1, source_target_pairs={{0,2},{1,3},{2,4},{3,5},{4,6},{5,7},{6,0},{7,1},{8,10},{9,11},{10,... | collective-permute-start | bytes 786440 | tf_op jit(solution)/shard_map/ppermute | solution.py:188
  133.6 8.9 %collective-permute-start.43 = (bf16[4,128,256]{2,1,0:T(8,128)(2,1)S(1)}, bf16[4,128,256]{2,1,0:T(8,128)(2,1)S(1)}, u32[]{:S(2)}, u32[]{:S(2)}) collective-permute-start(bf16[4,128,256]{2,1,0:T(8,128)(2,1)S(1)} %pad_maximum_fusion.4.refs_0_), channel_id=1, source_target_pairs={{0,8},{1,25},{2,10},{3,27},{4,12},{5,29},{6,14},{7,31},{8,16},{9,1... | collective-permute-start | bytes 786440 | tf_op jit(solution)/shard_map/ppermute | solution.py:188
  133.6 9.2 %collective-permute-start.46 = (bf16[4,128,256]{2,1,0:T(8,128)(2,1)S(1)}, bf16[4,128,256]{2,1,0:T(8,128)(2,1)S(1)}, u32[]{:S(2)}, u32[]{:S(2)}) collective-permute-start(bf16[4,128,256]{2,1,0:T(8,128)(2,1)S(1)} %pad_maximum_fusion.4.refs_0_), channel_id=1, source_target_pairs={{0,1},{1,0},{2,3},{3,2},{4,5},{5,4},{6,7},{7,6},{8,9},{9,8},{10,11... | collective-permute-start | bytes 786440 | tf_op jit(solution)/shard_map/ppermute | solution.py:188
  139.5 3.3 %collective-permute-start.49 = (bf16[4,128,256]{2,1,0:T(8,128)(2,1)S(1)}, bf16[4,128,256]{2,1,0:T(8,128)(2,1)S(1)}, u32[]{:S(2)}, u32[]{:S(2)}) collective-permute-start(bf16[4,128,256]{2,1,0:T(8,128)(2,1)S(1)} %collective-permute-done.45.refs_3_), channel_id=1, source_target_pairs={{0,1},{1,0},{2,3},{3,2},{4,5},{5,4},{6,7},{7,6},{8,9},{9,8},{10,11... | collective-permute-start | bytes 786440 | tf_op jit(solution)/shard_map/ppermute | solution.py:188
  142.5 1.7 collective-permute-start.47
  147.5 11.2 %collective-permute-start.52 = (bf16[2,128,256]{2,1,0:T(8,128)(2,1)S(1)}, bf16[2,128,256]{2,1,0:T(8,128)(2,1)S(1)}, u32[]{:S(2)}, u32[]{:S(2)}) collective-permute-start(bf16[2,128,256]{2,1,0:T(8,128)(2,1)S(1)} %pad_maximum_fusion.11), channel_id=1, source_target_pairs={{0,48},{1,53},{2,50},{3,55},{4,52},{5,49},{6,54},{7,51},{8,56},{9,... | collective-permute-start | bytes 393224 | tf_op jit(solution)/shard_map/ppermute | solution.py:188
  147.6 11.1 %collective-permute-start.51 = (bf16[2,128,256]{2,1,0:T(8,128)(2,1)S(1)}, bf16[2,128,256]{2,1,0:T(8,128)(2,1)S(1)}, u32[]{:S(2)}, u32[]{:S(2)}) collective-permute-start(bf16[2,128,256]{2,1,0:T(8,128)(2,1)S(1)} %pad_maximum_fusion.11), channel_id=1, source_target_pairs={{0,32},{1,37},{2,34},{3,39},{4,36},{5,33},{6,38},{7,35},{8,40},{9,... | collective-permute-start | bytes 393224 | tf_op jit(solution)/shard_map/ppermute | solution.py:188
  158.8 9.1 %collective-permute-start.55 = (bf16[4,128,256]{2,1,0:T(8,128)(2,1)S(1)}, bf16[4,128,256]{2,1,0:T(8,128)(2,1)S(1)}, u32[]{:S(2)}, u32[]{:S(2)}) collective-permute-start(bf16[4,128,256]{2,1,0:T(8,128)(2,1)S(1)} %pad_maximum_fusion.5.refs_0_), channel_id=1, source_target_pairs={{0,14},{1,31},{2,8},{3,25},{4,10},{5,27},{6,12},{7,29},{8,22},{9,7... | collective-permute-start | bytes 786440 | tf_op jit(solution)/shard_map/ppermute | solution.py:188
  161.4 8.8 %collective-permute-start.54 = (bf16[4,128,256]{2,1,0:T(8,128)(2,1)S(1)}, bf16[4,128,256]{2,1,0:T(8,128)(2,1)S(1)}, u32[]{:S(2)}, u32[]{:S(2)}) collective-permute-start(bf16[4,128,256]{2,1,0:T(8,128)(2,1)S(1)} %pad_maximum_fusion.5.refs_0_), channel_id=1, source_target_pairs={{0,2},{1,3},{2,4},{3,5},{4,6},{5,7},{6,0},{7,1},{8,10},{9,11},{10,... | collective-permute-start | bytes 786440 | tf_op jit(solution)/shard_map/ppermute | solution.py:188
  161.4 9.2 %collective-permute-start.53 = (bf16[4,128,256]{2,1,0:T(8,128)(2,1)S(1)}, bf16[4,128,256]{2,1,0:T(8,128)(2,1)S(1)}, u32[]{:S(2)}, u32[]{:S(2)}) collective-permute-start(bf16[4,128,256]{2,1,0:T(8,128)(2,1)S(1)} %pad_maximum_fusion.5.refs_0_), channel_id=1, source_target_pairs={{0,8},{1,25},{2,10},{3,27},{4,12},{5,29},{6,14},{7,31},{8,16},{9,1... | collective-permute-start | bytes 786440 | tf_op jit(solution)/shard_map/ppermute | solution.py:188
  162.0 8.8 %collective-permute-start.56 = (bf16[4,128,256]{2,1,0:T(8,128)(2,1)S(1)}, bf16[4,128,256]{2,1,0:T(8,128)(2,1)S(1)}, u32[]{:S(2)}, u32[]{:S(2)}) collective-permute-start(bf16[4,128,256]{2,1,0:T(8,128)(2,1)S(1)} %pad_maximum_fusion.5.refs_0_), channel_id=1, source_target_pairs={{0,1},{1,0},{2,3},{3,2},{4,5},{5,4},{6,7},{7,6},{8,9},{9,8},{10,11... | collective-permute-start | bytes 786440 | tf_op jit(solution)/shard_map/ppermute | solution.py:188
  167.8 2.9 %collective-permute-start.59 = (bf16[4,128,256]{2,1,0:T(8,128)(2,1)S(1)}, bf16[4,128,256]{2,1,0:T(8,128)(2,1)S(1)}, u32[]{:S(2)}, u32[]{:S(2)}) collective-permute-start(bf16[4,128,256]{2,1,0:T(8,128)(2,1)S(1)} %collective-permute-done.55.refs_3_), channel_id=1, source_target_pairs={{0,1},{1,0},{2,3},{3,2},{4,5},{5,4},{6,7},{7,6},{8,9},{9,8},{10,11... | collective-permute-start | bytes 786440 | tf_op jit(solution)/shard_map/ppermute | solution.py:188
  (13 other events, 27.1 us)
